TPU v7x, 256 devices: a whole 4x4x8 slice. The times are simulated.
256 devices in a mesh: vel: 4 (over x_lo, core), space: 64 (over x_hi, y, z).
Axes of the slice: x: 4 (x_hi: 2, x_lo: 2; x = x_hi * 2 + x_lo), y: 4, z: 8, core: 2. Of those that a mesh axis runs over, the one named last changes fastest.
Arguments:
- distribution: float32 [256, 8, 64, 512], P('space', None, None, 'vel'), may hold values from -8 to 8
- forcing: float32 [3, 256, 8, 64], P(None, 'space'), may hold values from -6 to 6
Outputs:
- updated: float32 [256, 8, 64, 512], P('space', None, None, 'vel')
- macro_fields: float32 [5, 256, 8, 64], P(None, 'space')
All inputs are finite; a program needn't handle non-finite values.
Results may differ from a plain program's by a relative error of at most 0.0001.
Values sent between devices are 32-bit elements; how exact they have to be, the bound alone decides.
No kernel may reach another device: no remote copies, remote signals or barrier semaphores. Data moves between devices by JAX's collectives and lax.ppermute only.
A program may use at most 128 MiB of HBM per device.

v0:
```python
import math

import jax
import jax.numpy as jnp
import numpy as np
from jax import lax
from jax.experimental import pallas as pl
from jax.experimental.pallas import tpu as pltpu
from jax.sharding import PartitionSpec as P

INTERPRET = False
DT = 0.02
RF = 0.4472135954999579
POINTS = [-1.0, -RF, RF, 1.0]
WEIGHTS = [1.0 / 6.0, 5.0 / 6.0, 5.0 / 6.0, 1.0 / 6.0]
EPS = 1e-6
HI = lax.Precision.HIGHEST


def lagrange_table(points):
    n = len(points)
    bary = []
    for i in range(n):
        product = 1.0
        for j in range(n):
            if j != i:
                product *= points[i] - points[j]
        bary.append(1.0 / product)
    rows = [[0.0] * n for _ in range(n)]
    for i in range(n):
        for j in range(n):
            if j != i:
                rows[i][j] = bary[j] / bary[i] / (points[i] - points[j])
        rows[i][i] = -sum(rows[i])
    return rows


D4 = lagrange_table(POINTS)
for _i in (1, 2):
    D4[_i][_i] = 0.0
PR = [[(1.0 - x) / 2.0, (1.0 + x) / 2.0] for x in POINTS]
RT = [[WEIGHTS[i] * PR[i][a] for i in range(4)] for a in range(2)]


def constant_tables():
    k = np.arange(512)
    b, j = k // 128, k % 128
    s = j // 64
    m = ((b * 64 + j % 64) * 5179 + 7) % 16384
    xi = np.stack([16 * s + m // 1024, (m // 32) % 32, m % 32]).astype(np.float64)
    xi = -4.0 + 0.25 * (xi + 0.5)
    sq = (xi * xi).sum(0)
    e = math.pi ** (-1.5) * np.exp(-sq)
    x, y, z = xi
    phi = np.stack(
        [np.ones(512), x, y, z, 2 * sq / 3 - 1, 2 * (x * x - sq / 3), 2 * (y * y - sq / 3),
         2 * x * y, 2 * x * z, 2 * y * z, x * (sq - 2.5), y * (sq - 2.5), z * (sq - 2.5)]
    )
    p = phi[0] + phi[4]
    zero = np.zeros(512)

    def eight(rows):
        return np.stack(list(rows) + [zero] * (8 - len(rows)))

    low = eight(phi[:5])
    along_x = eight([phi[1], p + phi[5], phi[7], phi[8], phi[1] + phi[10]])
    along_y = eight([phi[2], phi[7], p + phi[6], phi[9], phi[2] + phi[11]])
    along_z = eight([phi[3], phi[8], phi[9], p - phi[5] - phi[6], phi[3] + phi[12]])
    rows32 = np.concatenate([low, along_x, along_y, along_z])
    ec = eight([e, 2 * x * e, 2 * y * e, 2 * z * e, e * (sq - 1.5)])
    pos, neg = np.maximum(xi, 0.0), np.minimum(xi, 0.0)

    def per_rank(rows):
        return np.stack([rows[:, r * 128:(r + 1) * 128] for r in range(4)]).astype(np.float32)

    ispos = (x > 0).astype(np.float64)
    ax = np.abs(x)
    d4 = np.array(D4)
    vec = [-DT * 0.5 * x, -DT * 0.5 * y, -DT * 0.5 * z,
           -3 * DT * pos[1], -3 * DT * neg[1], -3 * DT * pos[2], -3 * DT * neg[2],
           -3 * DT * pos[0], 3 * DT * neg[0], 3 * DT * ax]
    for i in range(4):
        kap = -DT * 0.5 * x * np.where(ispos > 0, d4[i][0], d4[i][3])
        if i == 0:
            kap = kap + ispos * (0.8 - 3 * DT * ax)
        if i == 3:
            kap = kap + (1 - ispos) * (0.8 - 3 * DT * ax)
        vec.append(kap)
    vec.append(ispos)
    for jj in range(4):
        vec.append(-DT * 0.5 * x * np.where(ispos > 0, d4[3][jj], d4[0][jj]))
    while len(vec) < 24:
        vec.append(zero)
    vec = per_rank(np.stack(vec))

    def moment_columns(start, rows):
        out = np.zeros((4, 128, 128))
        for r in range(4):
            out[r, :, start:start + len(rows)] = rows[:, r * 128:(r + 1) * 128].T
        return out.astype(np.float32)

    tab2 = moment_columns(0, rows32)
    tab1 = moment_columns(40, low)
    tab0 = moment_columns(32, low)
    tabr = moment_columns(0, low)
    g = rows32 @ ec.T
    g5 = g[:8]
    mix = np.zeros((40, 64))
    mix[:32, 0:8] = 0.16 * g + 0.04 * g @ g5
    mix[:32, 8:16] = 0.2 * g
    mix[32:, 0:8] = 0.2 * g5
    mix[32:, 8:16] = np.eye(8)
    final = [ec]
    for d in range(3):
        for i, part in enumerate((pos[d], neg[d])):
            c0 = 16 + 16 * d + 8 * i
            mix[:32, c0:c0 + 8] = -0.2 * DT * (rows32 * part) @ ec.T
            final.append(-0.2 * DT * ec * part)
    final = per_rank(np.concatenate(final))
    lane = np.arange(128)
    yi, ze = (lane // 16) % 4, lane % 16
    rows = []
    shifts = (-3, -2, -1, 1, 2, 3)

    def entry(table, sft):
        return np.array([table(i, i + sft) if 0 <= i + sft < 4 else 0.0 for i in yi])

    for sft in shifts:
        c = entry(lambda i, q: 0.5 * D4[i][q], sft)
        if sft == -1:
            c = c - 1.5 * (yi == 0)
        if sft == 1:
            c = c + 1.5 * (yi == 3)
        rows.append(c)
    for a in range(2):
        for sft in range(-3, 4):
            rows.append(entry(lambda i, q: RT[a][q], sft))
    rows += [np.array([PR[i][0] for i in yi]), np.array([PR[i][1] for i in yi])]
    rows += [np.array([WEIGHTS[i] for i in yi]), (yi == 0) * 1.0, (ze == 0) * 1.0, (ze == 15) * 1.0]
    for sft in shifts:
        rows.append(entry(lambda i, q: 0.5 * D4[i][q], sft))
    rows += [entry(lambda i, q: 0.5 * D4[i][q], 0), 3.0 * (yi == 0), 3.0 * (yi == 3)]
    while len(rows) < 40:
        rows.append(np.zeros(128))
    lanes = np.stack(rows).astype(np.float32)
    return dict(vec=vec, tab2=tab2, tab1=tab1, tab0=tab0, tabr=tabr, mix=mix.astype(np.float32),
                final=final, lanes=lanes, ec=per_rank(ec))


def call(kernel, name, idx, full, ranked, outs, scratch=()):
    in_specs = [pl.BlockSpec(a.shape, lambda i, s, n=a.ndim: (0,) * n) for a in full]
    in_specs += [pl.BlockSpec((1,) + a.shape[1:], lambda i, s, n=a.ndim: (s[0],) + (0,) * (n - 1))
                 for a in ranked]
    res = pl.pallas_call(
        kernel,
        name=name,
        out_shape=[jax.ShapeDtypeStruct(s, jnp.float32) for s in outs],
        grid_spec=pltpu.PrefetchScalarGridSpec(
            num_scalar_prefetch=1, grid=(1,), in_specs=in_specs,
            out_specs=[pl.BlockSpec(s, lambda i, t, n=len(s): (0,) * n) for s in outs],
            scratch_shapes=[pltpu.VMEM(s, jnp.float32) for s in scratch]),
        compiler_params=pltpu.CompilerParams(vmem_limit_bytes=56 << 20),
        interpret=INTERPRET,
    )(idx, *full, *ranked)
    return res


def combine(row, values):
    total = None
    for c, v in zip(row, values):
        if c != 0.0:
            total = c * v if total is None else total + c * v
    return total


def layer_yz(src, dst, vec):
    def over_y(y, _):
        q = [src[zi, y] for zi in range(4)]
        for zi in range(4):
            v = vec[0, 2:3] * combine(D4[zi], q)
            if zi == 0:
                v = v + vec[0, 5:6] * (q[0] - pltpu.roll(q[3], 1, 0))
            if zi == 3:
                v = v + vec[0, 6:7] * (pltpu.roll(q[0], 15, 0) - q[3])
            dst[zi, y] = v
        return 0
    lax.fori_loop(0, 8, over_y, 0)

    def over_z(zi, _):
        q = [src[zi, y] for y in range(8)]
        for y in range(8):
            e, yi = 4 * (y // 4), y % 4
            v = vec[0, 1:2] * combine(D4[yi], q[e:e + 4])
            if yi == 0:
                v = v + vec[0, 3:4] * (q[y] - q[(y + 7) % 8])
            if yi == 3:
                v = v + vec[0, 4:5] * (q[(y + 1) % 8] - q[y])
            dst[zi, y] = dst[zi, y] + v
        return 0
    lax.fori_loop(0, 4, over_z, 0)


def every_fourth(h, xi, y, zi):
    if INTERPRET:
        return h[xi, y][zi::4]
    return h[xi, y, pl.ds(zi, 16, stride=4), :]


def rim_kernel(idx, h, vec, tabr, up, down, q, t, r0, r3):
    pos = vec[0, 14:15] > 0.5
    for zi in range(4):
        def over_y(y, _):
            x = [every_fourth(h, xi, y, zi) for xi in range(4)]
            ql = jnp.where(pos, x[3], x[0])
            q[zi, y] = ql
            r0[zi, y] = x[0]
            r3[zi, y] = x[3]
            v = 0.8 * ql
            for j in range(4):
                v = v + vec[0, 15 + j:16 + j] * x[j]
            up[pl.ds(pl.multiple_of((zi * 8 + y) * 16, 16), 16)] = v
            return 0
        lax.fori_loop(0, 8, over_y, 0)
    layer_yz(q, t, vec)
    right = lax.broadcasted_iota(jnp.int32, (16, 128), 1) >= 64

    def pack(n, _):
        zi, y = n // 8, n % 8
        at = pl.ds(pl.multiple_of(n * 16, 16), 16)
        tl = pltpu.roll(t[zi, y] + up[at], 64, 1)
        ql = q[zi, y]
        up[at] = jnp.where(right, ql, tl)
        down[at] = jnp.where(right, tl, ql)
        return 0
    lax.fori_loop(0, 32, pack, 0)
    for zi in range(4):
        for out, layer in ((up, r3), (down, r0)):
            m = jnp.dot(layer[zi].reshape(128, 128), tabr[0], precision=HI,
                        preferred_element_type=jnp.float32)
            out[512 + 8 * zi:520 + 8 * zi] = m.T[0:8]


def local_update(src, dst, vec):
    def over_y(y, _):
        q = [src[c, y] for c in range(16)]
        for xi in range(4):
            for zi in range(4):
                own = q[xi * 4 + zi]
                v = 0.8 * own + vec[0, 0:1] * combine(D4[xi], [q[j * 4 + zi] for j in range(4)])
                v = v + vec[0, 2:3] * combine(D4[zi], q[xi * 4:xi * 4 + 4])
                if zi == 0:
                    v = v + vec[0, 5:6] * (own - pltpu.roll(q[xi * 4 + 3], 1, 0))
                if zi == 3:
                    v = v + vec[0, 6:7] * (pltpu.roll(q[xi * 4], 15, 0) - own)
                if xi == 0:
                    v = v + vec[0, 7:8] * own
                if xi == 3:
                    v = v + vec[0, 8:9] * own
                dst[xi * 4 + zi, y] = v
        return 0
    lax.fori_loop(0, 8, over_y, 0)

    def over_c(c, _):
        q = [src[c, y] for y in range(8)]
        for y in range(8):
            e, yi = 4 * (y // 4), y % 4
            v = vec[0, 1:2] * combine(D4[yi], q[e:e + 4])
            if yi == 0:
                v = v + vec[0, 3:4] * (q[y] - q[(y + 7) % 8])
            if yi == 3:
                v = v + vec[0, 4:5] * (q[(y + 1) % 8] - q[y])
            dst[c, y] = dst[c, y] + v
        return 0
    lax.fori_loop(0, 16, over_c, 0)


def local_kernel(idx, h, vec, tab0, tab1, twice, mom, first, once):
    for c in range(16):
        xi, zi = c // 4, c % 4

        def over_y(y, _):
            first[c, y] = every_fourth(h, xi, y, zi)
            return 0
        lax.fori_loop(0, 8, over_y, 0)
    local_update(first, once, vec)
    local_update(once, twice, vec)

    def moments(c, _):
        m = jnp.dot(first[c].reshape(128, 128), tab0[0], precision=HI,
                    preferred_element_type=jnp.float32)
        m = m + jnp.dot(once[c].reshape(128, 128), tab1[0], precision=HI,
                        preferred_element_type=jnp.float32)
        mom[c] = m.T[32:48]
        return 0
    lax.fori_loop(0, 16, moments, 0)


def z_before(q, lt):
    return jnp.where(lt[24:25] > 0.5, pltpu.roll(q, 113, 1), pltpu.roll(q, 1, 1))


def z_after(q, lt):
    return jnp.where(lt[25:26] > 0.5, pltpu.roll(q, 15, 1), pltpu.roll(q, 127, 1))


SHIFTS = (-3, -2, -1, 1, 2, 3)


def central_y(q, lt):
    total = None
    for n, s in enumerate(SHIFTS):
        term = lt[n:n + 1] * pltpu.roll(q, (-16 * s) % 128, 1)
        total = term if total is None else total + term
    return total


def one_sided(load, low, high, c, lt):
    xi, zi = c // 4, c % 4
    q = load(c)
    cx = combine([0.5 * v for v in D4[xi]], [load(j * 4 + zi) for j in range(4)])
    px = cx + 3.0 * (q - low(zi)) if xi == 0 else cx
    mx = cx + 3.0 * (high(zi) - q) if xi == 3 else cx
    cy = lt[32:33] * q
    for n, s in enumerate(SHIFTS):
        r = pltpu.roll(q, (-16 * s) % 128, 1)
        cy = cy + lt[26 + n:27 + n] * r
        if s == -1:
            py = lt[33:34] * (q - r)
        if s == 1:
            my = lt[34:35] * (r - q)
    cz = combine([0.5 * v for v in D4[zi]], [load(xi * 4 + j) for j in range(4)])
    pz = cz + 3.0 * (q - z_before(load(xi * 4 + 3), lt)) if zi == 0 else cz
    mz = cz + 3.0 * (z_after(load(xi * 4), lt) - q) if zi == 3 else cz
    return [px, mx, cy + py, cy + my, pz, mz]


CENTRAL = [[0.0 if i == j else 0.5 * D4[i][j] for j in range(4)] for i in range(4)]


def moment_kernel(idx, up, down, twice, moma, mix, lt, vec, tab2, tab1, pay, t2,
                  delta, yz, extra, mom, full):
    right = lax.broadcasted_iota(jnp.int32, (16, 128), 1) >= 64
    pos = vec[0, 14:15]

    def unpack(n, _):
        at = pl.ds(pl.multiple_of(n * 16, 16), 16)
        u, d = up[at], down[at]
        zi, y = n // 8, n % 8
        delta[zi, y] = vec[0, 9:10] * jnp.where(right, u, d)
        extra[zi, y] = vec[0, 9:10] * pltpu.roll(jnp.where(right, d, u), 64, 1)
        return 0
    lax.fori_loop(0, 32, unpack, 0)
    layer_yz(delta, yz, vec)
    for xi in range(4):
        def over_n(n, _):
            zi, y = n // 8, n % 8
            v = twice[xi * 4 + zi, y] + vec[0, 10 + xi:11 + xi] * delta[zi, y]
            if xi in (0, 3):
                w = pos if xi == 0 else 1.0 - pos
                v = v + w * (yz[zi, y] + extra[zi, y])
            t2[xi * 4 + zi, y] = v
            return 0
        lax.fori_loop(0, 32, over_n, 0)

        def over_z(zi, _):
            c = xi * 4 + zi
            m = jnp.dot(t2[c].reshape(128, 128), tab2[0], precision=HI,
                        preferred_element_type=jnp.float32)
            if xi in (0, 3):
                w = pos if xi == 0 else 1.0 - pos
                m = m + jnp.dot(delta[zi].reshape(128, 128) * w, tab1[0], precision=HI,
                                preferred_element_type=jnp.float32)
            m = m.T
            mom[c, 0:32] = m[0:32]
            mom[c, 32:48] = m[32:48] + moma[c]
            return 0
        lax.fori_loop(0, 4, over_z, 0)

    def load0(c):
        return mom[c, 32:40]

    for c in range(16):
        six = one_sided(load0, lambda zi: up[512 + 8 * zi:520 + 8 * zi],
                        lambda zi: down[512 + 8 * zi:520 + 8 * zi], c, lt)
        stack = jnp.concatenate([mom[c, 32:40], mom[c, 40:48]] + six, axis=0)
        add = jnp.dot(mix[...], stack, precision=HI, preferred_element_type=jnp.float32)
        full[c, 0:32] = mom[c, 0:32] + add[0:32]
        full[c, 32:40] = add[32:40]
    for c in range(16):
        xi, zi = c // 4, c % 4
        r = combine(CENTRAL[xi], [full[j * 4 + zi, 8:16] for j in range(4)])
        r = r + central_y(full[c, 16:24], lt)
        r = r + combine(CENTRAL[zi], [full[xi * 4 + j, 24:32] for j in range(4)])
        if zi == 0:
            r = r - 1.5 * z_before(full[xi * 4 + 3, 24:32], lt)
        if zi == 3:
            r = r + 1.5 * z_after(full[xi * 4, 24:32], lt)
        pay[5 * c:5 * c + 5] = -r[0:5]
        pay[120 + 5 * c:125 + 5 * c] = full[c, 0:5]
        pay[200 + 5 * c:205 + 5 * c] = mom[c, 32:37]
        pay[280 + 5 * c:285 + 5 * c] = full[c, 32:37]
    for zi in range(4):
        pay[80 + 5 * zi:85 + 5 * zi] = full[zi, 8:13]
        pay[100 + 5 * zi:105 + 5 * zi] = full[12 + zi, 8:13]
        pay[360 + 5 * zi:365 + 5 * zi] = up[512 + 8 * zi:517 + 8 * zi]
        pay[380 + 5 * zi:385 + 5 * zi] = down[512 + 8 * zi:517 + 8 * zi]


def residual_kernel(idx, got, force, out, peers):
    t = got[0, 0:120] + got[1, 0:120] + got[2, 0:120] + got[3, 0:120]
    v = t[0:80] + force[...]
    for n in range(peers):
        out[n, 0:80] = v
        out[n, 80:120] = t[80:120]


def feq_kernel(idx, got, t2, lt, final, h2, low, s0, lo, hi):
    def total(a, n):
        return got[0, a:a + n] + got[1, a:a + n] + got[2, a:a + n] + got[3, a:a + n]

    s0[...] = jnp.zeros_like(s0)
    lo[...] = jnp.zeros_like(lo)
    hi[...] = jnp.zeros_like(hi)
    for c in range(16):
        s0[c, 0:5] = total(200 + 5 * c, 5)
    for zi in range(4):
        lo[zi, 0:5] = total(360 + 5 * zi, 5)
        hi[zi, 0:5] = total(380 + 5 * zi, 5)
    low[...] = total(120, 80)
    pad = jnp.zeros((3, 128), jnp.float32)
    for c in range(16):
        z = jnp.concatenate([0.2 * total(280 + 5 * c, 5), pad], axis=0) + 0.16 * s0[c]
        six = one_sided(lambda k: s0[k], lambda zi: lo[zi], lambda zi: hi[zi], c, lt)
        stack = jnp.concatenate([z] + six, axis=0)
        add = lax.dot_general(stack, final[0], (((0,), (0,)), ((), ())), precision=HI,
                              preferred_element_type=jnp.float32)
        h2[c] = t2[c] + add.reshape(8, 16, 128)


def apply_operator(src, dst, lt):
    def along_x(zi, _):
        u = [src[16 + j * 4 + zi] for j in range(4)]
        p = [src[j * 4 + zi] + src[64 + j * 4 + zi] for j in range(4)]
        for xi in range(4):
            du = combine(CENTRAL[xi], u)
            dp = combine(CENTRAL[xi], p)
            if xi == 0:
                du = du - 1.5 * pltpu.roll(u[3], 1, 0)
                dp = dp - 1.5 * pltpu.roll(p[3], 1, 0)
            if xi == 3:
                du = du + 1.5 * pltpu.roll(u[0], 23, 0)
                dp = dp + 1.5 * pltpu.roll(p[0], 23, 0)
            dst[xi * 4 + zi] = du
            dst[16 + xi * 4 + zi] = 2.0 * u[xi] + dp
        return 0
    lax.fori_loop(0, 4, along_x, 0)

    def along_z(xi, _):
        u = [src[48 + xi * 4 + j] for j in range(4)]
        p = [src[xi * 4 + j] + src[64 + xi * 4 + j] for j in range(4)]
        for zi in range(4):
            du = combine(CENTRAL[zi], u)
            dp = combine(CENTRAL[zi], p)
            if zi == 0:
                du = du - 1.5 * z_before(u[3], lt)
                dp = dp - 1.5 * z_before(p[3], lt)
            if zi == 3:
                du = du + 1.5 * z_after(u[0], lt)
                dp = dp + 1.5 * z_after(p[0], lt)
            dst[xi * 4 + zi] = dst[xi * 4 + zi] + du
            dst[48 + xi * 4 + zi] = 2.0 * u[zi] + dp
        return 0
    lax.fori_loop(0, 4, along_z, 0)

    def along_y(c, _):
        rho, u, t = src[c], src[32 + c], src[64 + c]
        div = dst[c] + central_y(u, lt)
        dst[32 + c] = 2.0 * u + central_y(rho + t, lt)
        dst[c] = 2.0 * rho + div
        dst[64 + c] = 2.0 * t + div
        return 0
    lax.fori_loop(0, 16, along_y, 0)


def two_level(r, pe, co, lt):
    def over_f(f, _):
        tz = [[None, None] for _ in range(4)]
        for xi in range(4):
            q = [r[f * 16 + xi * 4 + zi] for zi in range(4)]
            for za in range(2):
                tz[xi][za] = combine(RT[za], q)
        for za in range(2):
            py = []
            for xa in range(2):
                t = combine(RT[xa], [tz[xi][za] for xi in range(4)])
                e0, e1 = lt[9:10] * t, lt[16:17] * t
                for s in SHIFTS:
                    rolled = pltpu.roll(t, (-16 * s) % 128, 1)
                    e0 = e0 + lt[9 + s:10 + s] * rolled
                    e1 = e1 + lt[16 + s:17 + s] * rolled
                co[f * 8 + xa * 4 + za * 2] = e0
                co[f * 8 + xa * 4 + za * 2 + 1] = e1
                py.append(lt[20:21] * e0 + lt[21:22] * e1)
            for xi in range(4):
                v = combine(PR[xi], py)
                for zi in range(4):
                    if PR[zi][za] == 0.0:
                        continue
                    at = f * 16 + xi * 4 + zi
                    if za == 0 or PR[zi][0] == 0.0:
                        pe[at] = PR[zi][za] * v
                    else:
                        pe[at] = pe[at] + PR[zi][za] * v
        return 0
    lax.fori_loop(0, 5, over_f, 0)


def coarse_products(co, lt):
    def at(f, xa, za, ya):
        return co[f * 8 + xa * 4 + za * 2 + ya]

    def own(q):
        return q[8:16]

    def dx(q, xa, za, ya):
        if xa == 0:
            v = q(1, za, ya)
            return 0.25 * (own(v) - own(pltpu.roll(v, 1, 0)))
        v = q(0, za, ya)
        return 0.25 * (own(pltpu.roll(v, 23, 0)) - own(v))

    def dz(q, xa, za, ya):
        v = own(q(xa, 1 - za, ya))
        if za == 0:
            return 0.25 * (v - z_before(v, lt))
        return 0.25 * (z_after(v, lt) - v)

    def dy(q, xa, za, ya):
        v = own(q(xa, za, 1 - ya))
        w = pltpu.roll(v, 64, 1)
        return 0.25 * (v - w) if ya == 0 else 0.25 * (w - v)

    up = jnp.zeros((8, 128), jnp.float32)
    low = jnp.zeros((8, 128), jnp.float32)
    for xa in range(2):
        for za in range(2):
            for ya in range(2):
                def field(f):
                    return lambda a, b, c: at(f, a, b, c)

                def pressure(a, b, c):
                    return at(0, a, b, c) + at(4, a, b, c)
                e = [own(at(f, xa, za, ya)) for f in range(5)]
                div = (dx(field(1), xa, za, ya) + dy(field(2), xa, za, ya)
                       + dz(field(3), xa, za, ya))
                g = [2.0 * e[0] + div, 2.0 * e[1] + dx(pressure, xa, za, ya),
                     2.0 * e[2] + dy(pressure, xa, za, ya),
                     2.0 * e[3] + dz(pressure, xa, za, ya), 2.0 * e[4] + div]
                for f in range(5):
                    up = up + e[f] * g[f]
                    low = low + g[f] * g[f]
    return up * lt[23:24], low * lt[23:24]


def fine_products(r, m, ar, am, lt):
    total = [jnp.zeros((8, 128), jnp.float32) for _ in range(6)]
    for xi in range(4):
        for zi in range(4):
            def over_f(f, acc):
                k = f * 16 + xi * 4 + zi
                a, b, c, d = r[k, 8:16], m[k, 8:16], ar[k, 8:16], am[k, 8:16]
                return (acc[0] + a * c, acc[1] + a * d + b * c, acc[2] + b * d,
                        acc[3] + c * c, acc[4] + c * d, acc[5] + d * d)
            zero = jnp.zeros((8, 128), jnp.float32)
            acc = lax.fori_loop(0, 5, over_f, (zero,) * 6, unroll=True)
            w = WEIGHTS[xi] * WEIGHTS[zi]
            total = [t + w * a for t, a in zip(total, acc)]
    return [t * lt[22:23] for t in total]


def pass_words(r, m, ar, am, pe, co, gram, lt, peers):
    two_level(r, pe, co, lt)
    apply_operator(pe, m, lt)
    apply_operator(r, ar, lt)
    apply_operator(m, am, lt)
    products = list(coarse_products(co, lt)) + fine_products(r, m, ar, am, lt)
    rows = jnp.concatenate([jnp.sum(p, axis=0, keepdims=True) for p in products], axis=0)
    for n in range(peers):
        gram[n] = rows


def first_pass_kernel(idx, lower, mine, upper, lt, r, m, ar, am, pe, gram, co, lox, hix):
    for f in range(5):
        for zi in range(4):
            for n, src in enumerate((lower, mine, upper)):
                lox[f * 4 + zi, 8 * n:8 * n + 8] = src[pl.ds(80 + 5 * zi + f, 8, stride=120), :]
                hix[f * 4 + zi, 8 * n:8 * n + 8] = src[pl.ds(100 + 5 * zi + f, 8, stride=120), :]
        for c in range(16):
            xi, zi = c // 4, c % 4
            for n, src in enumerate((lower, mine, upper)):
                r[f * 16 + c, 8 * n:8 * n + 8] = src[pl.ds(5 * c + f, 8, stride=120), :]
            if xi == 0:
                r[f * 16 + c] = r[f * 16 + c] + 1.5 * pltpu.roll(hix[f * 4 + zi], 1, 0)
            if xi == 3:
                r[f * 16 + c] = r[f * 16 + c] - 1.5 * pltpu.roll(lox[f * 4 + zi], 23, 0)
    pass_words(r, m, ar, am, pe, co, gram, lt, gram.shape[0])


def step_sizes(sums, peers):
    s = sums[0]
    for n in range(1, peers):
        s = s + sums[n]
    s = jnp.broadcast_to(jnp.sum(s, axis=1, keepdims=True), (8, 128))
    a1 = s[0:1] / (s[1:2] + EPS)
    up = s[2:3] - a1 * s[3:4] + a1 * a1 * s[4:5]
    low = s[5:6] - 2.0 * a1 * s[6:7] + a1 * a1 * s[7:8]
    return a1, up / (low + EPS)


def next_pass_kernel(first, idx, sums, r, m, ar, am, pe, *rest):
    if first:
        lt, r2, m2, ar2, am2, pe2, acc2, gram, co = rest
    else:
        acc, lt, r2, m2, ar2, am2, pe2, acc2, gram, co = rest
    a1, a2 = step_sizes(sums, gram.shape[0])

    def over_k(k, _):
        q = r[k] - a1 * m[k]
        v = a1 * pe[k, 8:16] + a2 * q[8:16]
        acc2[k] = v if first else acc[k] + v
        r2[k] = q - a2 * (ar[k] - a1 * am[k])
        return 0
    lax.fori_loop(0, 80, over_k, 0, unroll=4)
    pass_words(r2, m2, ar2, am2, pe2, co, gram, lt, gram.shape[0])


def last_kernel(idx, sums, r, m, pe, acc, low, h2, ec, out, fields, change):
    a1, a2 = step_sizes(sums, sums.shape[0])

    def over_k(k, _):
        q = r[k, 8:16] - a1 * m[k, 8:16]
        change[pl.ds(pl.multiple_of(k * 8, 8), 8)] = acc[k] + a1 * pe[k, 8:16] + a2 * q
        return 0
    lax.fori_loop(0, 80, over_k, 0, unroll=4)
    z = idx[1]
    zero = jnp.zeros((3, 128), jnp.float32)
    for c in range(16):
        xi, zi = c // 4, c % 4
        d = jnp.concatenate([change[pl.ds((f * 16 + c) * 8 + z, 1)] for f in range(5)] + [zero], axis=0)
        new = low[5 * c:5 * c + 5] + d[0:5]
        for f in range(5):
            fields[16 * f + c:16 * f + c + 1] = new[f:f + 1]
        add = lax.dot_general(d, ec[0], (((0,), (0,)), ((), ())), precision=HI,
                              preferred_element_type=jnp.float32)
        v = h2[c] + add.reshape(8, 16, 128)
        for y in range(8):
            out[xi, y, pl.ds(zi, 16, stride=4), :] = v[y]


def on_device(distribution, forcing):
    import functools
    tables = {k: jnp.asarray(v) for k, v in constant_tables().items()}
    spaces = lax.axis_size("space")
    blocks = spaces // 8
    idx = jnp.stack([lax.axis_index("vel"), lax.axis_index("space") % 8]).astype(jnp.int32)
    vec, lt = tables["vec"], tables["lanes"]
    wide = (16, 8, 16, 128)
    layer = (4, 8, 16, 128)

    def shifted(x, by):
        return lax.ppermute(x, "space", [(i, (i + by) % spaces) for i in range(spaces)])

    up, down = call(rim_kernel, "rims", idx, [distribution], [vec, tables["tabr"]],
                    [(544, 128)] * 2, [layer] * 4)
    up, down = shifted(up, 1), shifted(down, -1)
    twice, moma = call(local_kernel, "local", idx, [distribution],
                       [vec, tables["tab0"], tables["tab1"]],
                       [wide, (16, 16, 128)], [wide, wide])
    force = jnp.pad(forcing, ((1, 1), (0, 0), (0, 0), (0, 0)))
    force = force.reshape(5, 4, 8, 16, 4).transpose(1, 4, 0, 2, 3).reshape(80, 128)
    pay, t2 = call(moment_kernel, "moments", idx, [up, down, twice, moma, tables["mix"], lt],
                   [vec, tables["tab2"], tables["tab1"]], [(400, 128), wide],
                   [layer, layer, layer, (16, 48, 128), (16, 40, 128)])
    got = lax.all_gather(pay, "vel")
    (res,) = call(lambda i, g, fo, o: residual_kernel(i, g, fo, o, 8), "residual", idx,
                  [got, force], [], [(8, 120, 128)])
    near = [[a * 8 + b for b in range(8)] for a in range(blocks)]
    far = [[a * 8 + b for a in range(blocks)] for b in range(8)]
    mine = lax.all_to_all(res, "space", 0, 0, axis_index_groups=near, tiled=True).reshape(960, 128)
    lower, upper = shifted(mine, 8), shifted(mine, -8)
    h2, low = call(feq_kernel, "feq", idx, [got, t2, lt], [tables["final"]],
                   [wide, (80, 128)], [(16, 8, 128), (4, 8, 128), (4, 8, 128)])

    def summed(gram):
        return lax.all_to_all(gram, "space", 0, 0, axis_index_groups=far, tiled=True)

    win, own, part = (80, 24, 128), (80, 8, 128), (blocks, 8, 128)
    co = (40, 24, 128)
    r, m, ar, am, pe, gram = call(first_pass_kernel, "pass1", idx, [lower, mine, upper, lt], [],
                                  [win] * 5 + [part], [co, (20, 24, 128), (20, 24, 128)])
    r, m, ar, am, pe, acc, gram = call(functools.partial(next_pass_kernel, True), "pass2", idx,
                                       [summed(gram), r, m, ar, am, pe, lt], [],
                                       [win] * 5 + [own, part], [co])
    r, m, ar, am, pe, acc, gram = call(functools.partial(next_pass_kernel, False), "pass3", idx,
                                       [summed(gram), r, m, ar, am, pe, acc, lt], [],
                                       [win] * 5 + [own, part], [co])
    out, fields = call(last_kernel, "last", idx, [summed(gram), r, m, pe, acc, low, h2],
                       [tables["ec"]], [(4, 8, 64, 128), (80, 128)], [(640, 128)])
    fields = fields.reshape(5, 4, 4, 8, 16).transpose(0, 1, 3, 4, 2).reshape(5, 4, 8, 64)
    return out, fields


def solution(mesh):
    return jax.shard_map(
        on_device,
        mesh=mesh,
        in_specs=(P("space", None, None, "vel"), P(None, "space", None, None)),
        out_specs=(P("space", None, None, "vel"), P(None, "space", None, None)),
        check_vma=False,
    )
```

profile of v0, /device:TPU:2, one launch (start us, length us, event | category | flops | bytes accessed | tf_op | source)
XLA Modules:
  0.0 177.2 jit_solution(14429748622238897841)
XLA Ops:
  0.6 0.6 pad_add_fusion.idx.i
  1.2 0.0 copy-start.6
  1.2 6.3 %rims.1 = (f32[544,128]{1,0:T(8,128)}, f32[544,128]{1,0:T(8,128)}) custom-call(s32[2]{0:T(128)} %pad_add_fusion.idx.i, f32[4,8,64,128]{3,2,1,0:T(8,128)} %h.3, f32[4,24,128]{2,1,0:T(8,128)} %constant.43.clone.vec, f32[4,128,128]{2,1,0:T(8,128)} %constant.47.clone.tabr), custom_call_target="tpu_custom_call" | custom-call | tf_op jit(solution)/shard_map/rims/pallas_call | solution.py:154
  7.6 1.9 %collective-permute-start = (f32[544,128]{1,0:T(8,128)}, f32[544,128]{1,0:T(8,128)S(1)}, u32[]{:S(2)}, u32[]{:S(2)}) collective-permute-start(f32[544,128]{1,0:T(8,128)} %get-tuple-element.30), channel_id=1, source_target_pairs={{0,1},{1,2},{2,3},{3,4},{4,5},{5,6},{6,7},{7,8},{8,9},{9,10},{10,1... | collective-permute-start | bytes 835592 | tf_op jit(solution)/shard_map/ppermute | solution.py:671
  9.5 8.0 %collective-permute-start.1 = (f32[544,128]{1,0:T(8,128)}, f32[544,128]{1,0:T(8,128)S(1)}, u32[]{:S(2)}, u32[]{:S(2)}) collective-permute-start(f32[544,128]{1,0:T(8,128)} %get-tuple-element.31), channel_id=1, source_target_pairs={{0,63},{1,0},{2,1},{3,2},{4,3},{5,4},{6,5},{7,6},{8,7},{9,8},{10,9... | collective-permute-start | bytes 835592 | tf_op jit(solution)/shard_map/ppermute | solution.py:671
  17.5 0.0 copy-done.6
  17.5 0.2 copy.19
  17.6 0.1 pad.4.clone
  17.7 0.2 copy.16
  17.9 0.8 reshape.20.fo
  18.7 11.1 %local.1 = (f32[16,8,16,128]{3,2,1,0:T(8,128)}, f32[16,16,128]{2,1,0:T(8,128)}) custom-call(s32[2]{0:T(128)} %pad_add_fusion.idx.i, f32[4,8,64,128]{3,2,1,0:T(8,128)} %h.3, f32[4,24,128]{2,1,0:T(8,128)} %constant.43.clone.vec, f32[4,128,128]{2,1,0:T(8,128)} %constant.46.clone.tab0, f32[4,128,128]{2,1,0:T(8,128)} %constant.45.clone.tab1), custom_call_target="tpu_custom_call" | custom-call | tf_op jit(solution)/shard_map/local/pallas_call | solution.py:154
  29.8 0.0 collective-permute-done.up
  29.8 0.0 copy-start.3
  29.8 0.0 collective-permute-done.1.down
  29.8 0.0 copy-start.4
  29.8 0.7 copy-done.3
  30.5 0.1 copy-done.4
  30.6 12.7 %moments.1 = (f32[400,128]{1,0:T(8,128)}, f32[16,8,16,128]{3,2,1,0:T(8,128)}) custom-call(s32[2]{0:T(128)} %pad_add_fusion.idx.i, f32[544,128]{1,0:T(8,128)} %copy-done.3, f32[544,128]{1,0:T(8,128)} %copy-done.4, f32[16,8,16,128]{3,2,1,0:T(8,128)} %get-tuple-element.32.twice, f32[16,16,128]{2,1,0:T(8,128)} %get-tuple-element.33.moma, ...), custom_call_target="tpu_custom_call" | custom-call | tf_op jit(solution)/shard_map/moments/pallas_call | solution.py:154
  43.3 10.1 %all-gather = f32[1600,128]{1,0:T(8,128)} all-gather(f32[400,128]{1,0:T(8,128)} %get-tuple-element.34), channel_id=2, replica_groups=mesh['vel'=4,'space'=64] {'vel'}, dimensions={0}, use_global_device_ids=true | all-gather | bytes 1024000 | tf_op jit(solution)/shard_map/all_gather | solution.py:684
  53.4 2.6 %residual.1 = f32[8,120,128]{2,1,0:T(8,128)} custom-call(s32[2]{0:T(128)} %pad_add_fusion.idx.i, f32[4,400,128]{2,1,0:T(8,128)} %bitcast.12, f32[80,128]{1,0:T(8,128)} %reshape.20.fo), custom_call_target="tpu_custom_call" | custom-call | tf_op jit(solution)/shard_map/residual/pallas_call | solution.py:154
  56.0 21.0 %all_to_all.20 = f32[8,120,128]{2,1,0:T(8,128)S(1)} all-to-all(f32[8,120,128]{2,1,0:T(8,128)} %residual.1), channel_id=1, replica_groups={{0,1,2,3,4,5,6,7},{8,9,10,11,12,13,14,15},{16,17,18,19,20,21,22,23},{24..., dimensions={0} | all-to-all | bytes 983040 | tf_op jit(solution)/shard_map/all_to_all | solution.py:689
  77.0 0.0 copy-start
  77.0 1.8 %collective-permute-start.3 = (f32[960,128]{1,0:T(8,128)S(1)}, f32[960,128]{1,0:T(8,128)S(1)}, u32[]{:S(2)}, u32[]{:S(2)}) collective-permute-start(f32[960,128]{1,0:T(8,128)S(1)} %bitcast.16), channel_id=1, source_target_pairs={{0,56},{1,57},{2,58},{3,59},{4,60},{5,61},{6,62},{7,63},{8,0},{9,1... | collective-permute-start | bytes 1474568 | tf_op jit(solution)/shard_map/ppermute | solution.py:671
  78.8 0.2 collective-permute-start.2
  79.0 11.2 %collective-permute-done.3.upper = f32[960,128]{1,0:T(8,128)S(1)} collective-permute-done((f32[960,128]{1,0:T(8,128)S(1)}, f32[960,128]{1,0:T(8,128)S(1)}, u32[]{:S(2)}, u32[]{:S(2)}) %collective-permute-start.3) | collective-permute-done | bytes 491552 | tf_op jit(solution)/shard_map/ppermute | solution.py:671
  90.2 0.0 copy-start.1
  90.2 5.1 %collective-permute-done.2.lower = f32[960,128]{1,0:T(8,128)S(1)} collective-permute-done((f32[960,128]{1,0:T(8,128)S(1)}, f32[960,128]{1,0:T(8,128)S(1)}, u32[]{:S(2)}, u32[]{:S(2)}) %collective-permute-start.2) | collective-permute-done | bytes 491552 | tf_op jit(solution)/shard_map/ppermute | solution.py:671
  95.2 0.0 copy-done
  95.2 0.0 copy-done.1
  95.2 0.0 copy-start.2
  95.2 0.8 copy-done.2
  96.0 12.0 %pass1.1 = (f32[80,24,128]{2,1,0:T(8,128)}, f32[80,24,128]{2,1,0:T(8,128)}, f32[80,24,128]{2,1,0:T(8,128)}, f32[80,24,128]{2,1,0:T(8,128)}, f32[80,24,128]{2,1,0:T(8,128)}, /*index=5*/f32[8,8,128]{2,1,0:T(8,128)}) custom-call(s32[2]{0:T(128)} %pad_add_fusion.idx.i, f32[960,128]{1,0:T(8,128)} %copy-done.2, f32[960,128]{1,0:T(8,128)} %bitcast.18, ...), custom_call_target="tpu_custom_call" | custom-call | tf_op jit(solution)/shard_map/pass1/pallas_call | solution.py:154
  108.0 11.7 %all_to_all.21.sums = f32[8,8,128]{2,1,0:T(8,128)} all-to-all(f32[8,8,128]{2,1,0:T(8,128)} %get-tuple-element.35), channel_id=1, replica_groups={{0,8,16,24,32,40,48,56},{1,9,17,25,33,41,49,57},{2,10,18,26,34,42,50,58..., dimensions={0} | all-to-all | bytes 65536 | tf_op jit(solution)/shard_map/all_to_all | solution.py:695
  119.7 13.4 %pass2.1 = (f32[80,24,128]{2,1,0:T(8,128)}, f32[80,24,128]{2,1,0:T(8,128)}, f32[80,24,128]{2,1,0:T(8,128)}, f32[80,24,128]{2,1,0:T(8,128)}, f32[80,24,128]{2,1,0...) custom-call(s32[2]{0:T(128)} %pad_add_fusion.idx.i, f32[8,8,128]{2,1,0:T(8,128)} %all_to_all.21.sums, ...), custom_call_target="tpu_custom_call" | custom-call | tf_op jit(solution)/shard_map/pass2/pallas_call | solution.py:154
  133.1 11.7 %all_to_all.22.sums = f32[8,8,128]{2,1,0:T(8,128)} all-to-all(f32[8,8,128]{2,1,0:T(8,128)} %get-tuple-element.41), channel_id=1, replica_groups={{0,8,16,24,32,40,48,56},{1,9,17,25,33,41,49,57},{2,10,18,26,34,42,50,58..., dimensions={0} | all-to-all | bytes 65536 | tf_op jit(solution)/shard_map/all_to_all | solution.py:695
  144.8 13.4 %pass3.1 = (f32[80,24,128]{2,1,0:T(8,128)}, f32[80,24,128]{2,1,0:T(8,128)}, f32[80,24,128]{2,1,0:T(8,128)}, f32[80,24,128]{2,1,0:T(8,128)}, f32[80,24,128]{2,1,0...) custom-call(s32[2]{0:T(128)} %pad_add_fusion.idx.i, f32[8,8,128]{2,1,0:T(8,128)} %all_to_all.22.sums, ...), custom_call_target="tpu_custom_call" | custom-call | tf_op jit(solution)/shard_map/pass3/pallas_call | solution.py:154
  158.2 3.3 %all-to-all-start.3 = ((f32[8,8,128]{2,1,0:T(8,128)}), f32[8,8,128]{2,1,0:T(8,128)S(1)}, u32[]{:S(2)}, u32[]{:S(2)}) async-start(f32[8,8,128]{2,1,0:T(8,128)} %get-tuple-element.48), calls=%async_computation.3 | async-start | bytes 65536 | tf_op jit(solution)/shard_map/all_to_all | solution.py:695
  161.6 4.4 %feq.1 = (f32[16,8,16,128]{3,2,1,0:T(8,128)}, f32[80,128]{1,0:T(8,128)}) custom-call(s32[2]{0:T(128)} %pad_add_fusion.idx.i, f32[4,400,128]{2,1,0:T(8,128)} %bitcast.13, f32[16,8,16,128]{3,2,1,0:T(8,128)} %get-tuple-element.53.t2, f32[40,128]{1,0:T(8,128)} %constant.50.clone.lt.rest_0_.rest_1_, f32[4,56,128]{2,1,0:T(8,128)} %constant.49.clone.final), custom_call_target="tpu_custom_call" | custom-call | tf_op jit(solution)/shard_map/feq/pallas_call | solution.py:154
  166.0 3.2 %all-to-all-done.3.sums = f32[8,8,128]{2,1,0:T(8,128)S(1)} async-done(((f32[8,8,128]{2,1,0:T(8,128)}), f32[8,8,128]{2,1,0:T(8,128)S(1)}, u32[]{:S(2)}, u32[]{:S(2)}) %all-to-all-start.3) | async-done | bytes 32800 | tf_op jit(solution)/shard_map/all_to_all | solution.py:695
  169.2 0.0 copy-start.5
  169.3 0.6 copy-done.5
  169.9 5.2 %last.1 = (f32[4,8,64,128]{3,2,1,0:T(8,128)}, f32[80,128]{1,0:T(8,128)}) custom-call(s32[2]{0:T(128)} %pad_add_fusion.idx.i, f32[8,8,128]{2,1,0:T(8,128)} %copy-done.5, f32[80,24,128]{2,1,0:T(8,128)} %get-tuple-element.49.r, f32[80,24,128]{2,1,0:T(8,128)} %get-tuple-element.50.m, f32[80,24,128]{2,1,0:T(8,128)} %get-tuple-element.51.pe, ...), custom_call_target="tpu_custom_call" | custom-call | tf_op jit(solution)/shard_map/last/pallas_call | solution.py:154
  175.1 0.9 reshape.22
  176.0 0.3 copy.17
  176.3 0.9 copy.18
Async XLA Ops:
  1.2 16.2 %copy-start.6 = (f32[3,4,8,64]{3,2,1,0:T(8,128)S(1)}, f32[3,4,8,64]{3,2,1,0:T(8,128)}, u32[]{:S(2)}) copy-start(f32[3,4,8,64]{3,2,1,0:T(8,128)} %param.12) | copy-start | bytes 73732
  7.6 22.2 %collective-permute-start = (f32[544,128]{1,0:T(8,128)}, f32[544,128]{1,0:T(8,128)S(1)}, u32[]{:S(2)}, u32[]{:S(2)}) collective-permute-start(f32[544,128]{1,0:T(8,128)} %get-tuple-element.30), channel_id=1, source_target_pairs={{0,1},{1,2},{2,3},{3,4},{4,5},{5,6},{6,7},{7,8},{8,9},{9,10},{10,1... | collective-permute-start | bytes 835592 | tf_op jit(solution)/shard_map/ppermute | solution.py:671
  9.5 20.3 %collective-permute-start.1 = (f32[544,128]{1,0:T(8,128)}, f32[544,128]{1,0:T(8,128)S(1)}, u32[]{:S(2)}, u32[]{:S(2)}) collective-permute-start(f32[544,128]{1,0:T(8,128)} %get-tuple-element.31), channel_id=1, source_target_pairs={{0,63},{1,0},{2,1},{3,2},{4,3},{5,4},{6,5},{7,6},{8,7},{9,8},{10,9... | collective-permute-start | bytes 835592 | tf_op jit(solution)/shard_map/ppermute | solution.py:671
  29.8 0.7 copy-start.3
  29.8 0.8 copy-start.4
  77.0 18.2 %copy-start = (f32[8,120,128]{2,1,0:T(8,128)}, f32[8,120,128]{2,1,0:T(8,128)S(1)}, u32[]{:S(2)}) copy-start(f32[8,120,128]{2,1,0:T(8,128)S(1)} %all_to_all.20) | copy-start | bytes 1474564
  77.0 13.2 %collective-permute-start.3 = (f32[960,128]{1,0:T(8,128)S(1)}, f32[960,128]{1,0:T(8,128)S(1)}, u32[]{:S(2)}, u32[]{:S(2)}) collective-permute-start(f32[960,128]{1,0:T(8,128)S(1)} %bitcast.16), channel_id=1, source_target_pairs={{0,56},{1,57},{2,58},{3,59},{4,60},{5,61},{6,62},{7,63},{8,0},{9,1... | collective-permute-start | bytes 1474568 | tf_op jit(solution)/shard_map/ppermute | solution.py:671
  78.8 16.4 %collective-permute-start.2 = (f32[960,128]{1,0:T(8,128)S(1)}, f32[960,128]{1,0:T(8,128)S(1)}, u32[]{:S(2)}, u32[]{:S(2)}) collective-permute-start(f32[960,128]{1,0:T(8,128)S(1)} %bitcast.17), channel_id=1, source_target_pairs={{0,8},{1,9},{2,10},{3,11},{4,12},{5,13},{6,14},{7,15},{8,16},{9,17... | collective-permute-start | bytes 1474568 | tf_op jit(solution)/shard_map/ppermute | solution.py:671
  90.2 5.1 %copy-start.1 = (f32[960,128]{1,0:T(8,128)}, f32[960,128]{1,0:T(8,128)S(1)}, u32[]{:S(2)}) copy-start(f32[960,128]{1,0:T(8,128)S(1)} %collective-permute-done.3.upper) | copy-start | bytes 1474564
  95.2 0.8 copy-start.2
  158.2 11.0 %all-to-all-start.3 = ((f32[8,8,128]{2,1,0:T(8,128)}), f32[8,8,128]{2,1,0:T(8,128)S(1)}, u32[]{:S(2)}, u32[]{:S(2)}) async-start(f32[8,8,128]{2,1,0:T(8,128)} %get-tuple-element.48), calls=%async_computation.3 | async-start | bytes 65536 | tf_op jit(solution)/shard_map/all_to_all | solution.py:695
  169.2 0.6 copy-start.5
where the time goes:
time: 178 us; the launch traced here: 177 us
  Pallas kernels  81.2 us (46%)
  blocking collectives  54.4 us (31%)
  waiting for transfers between devices  19.5 us (11%)
  starting transfers between devices  15.2 us (9%)
  local copies, waits for them, and re-layouts  5.52 us (3%)
    pallas_call x9, Pallas kernels, call(): pl.pallas_call(kernel, name=name, out_shape=[jax.ShapeDtypeStruct(s, jnp....  81.2 us
    all_to_all x2, blocking collectives, summed(): lax.all_to_all(gram, 'space', 0, 0, axis_index_groups=far, tiled=True)  23.4 us
    all_to_all x1, blocking collectives, on_device(): lax.all_to_all(res, 'space', 0, 0, axis_index_groups=near, tiled=True)  21 us
    ppermute x4, waiting for transfers between devices, shifted(): lax.ppermute(x, 'space', [(i, (i + by) % spaces) for i in range(spaces)])  16.2 us
    ppermute x4, starting transfers between devices, shifted(): lax.ppermute(x, 'space', [(i, (i + by) % spaces) for i in range(spaces)])  11.9 us
    all_gather x1, blocking collectives, on_device(): got = lax.all_gather(pay, 'vel')  10.1 us
  transfers between devices with their start and end apart: 5, of which 3 were waited for; matrix products, arithmetic and copies ran while one was open for 1% of the time, Pallas kernels for 9%

commit v1 on v0

--- a/solution.py
+++ b/solution.py
@@ -147,22 +147,28 @@
                 final=final, lanes=lanes, ec=per_rank(ec))
 
 
-def call(kernel, name, idx, full, ranked, outs, scratch=()):
-    in_specs = [pl.BlockSpec(a.shape, lambda i, s, n=a.ndim: (0,) * n) for a in full]
-    in_specs += [pl.BlockSpec((1,) + a.shape[1:], lambda i, s, n=a.ndim: (s[0],) + (0,) * (n - 1))
-                 for a in ranked]
-    res = pl.pallas_call(
-        kernel,
+def call(kernel, name, idx, full, ranked, outs, scratch=(), limit=24):
+    n = len(full)
+
+    def body(idx, *refs):
+        rank = [r.at[pl.ds(idx[0], 1)] for r in refs[n:n + len(ranked)]]
+        kernel(idx, *refs[:n], *rank, *refs[n + len(ranked):])
+
+    vmem = pl.BlockSpec(memory_space=pltpu.VMEM)
+    return pl.pallas_call(
+        body,
         name=name,
         out_shape=[jax.ShapeDtypeStruct(s, jnp.float32) for s in outs],
-        grid_spec=pltpu.PrefetchScalarGridSpec(
-            num_scalar_prefetch=1, grid=(1,), in_specs=in_specs,
-            out_specs=[pl.BlockSpec(s, lambda i, t, n=len(s): (0,) * n) for s in outs],
-            scratch_shapes=[pltpu.VMEM(s, jnp.float32) for s in scratch]),
-        compiler_params=pltpu.CompilerParams(vmem_limit_bytes=56 << 20),
+        in_specs=[pl.BlockSpec(memory_space=pltpu.SMEM)] + [vmem] * (n + len(ranked)),
+        out_specs=[vmem] * len(outs),
+        scratch_shapes=[pltpu.VMEM(s, jnp.float32) for s in scratch],
+        compiler_params=pltpu.CompilerParams(vmem_limit_bytes=limit << 20),
         interpret=INTERPRET,
     )(idx, *full, *ranked)
-    return res
+
+
+def exact_dot(a, b):
+    return jnp.dot(a, b, precision=HI, preferred_element_type=jnp.float32)
 
 
 def combine(row, values):
@@ -206,15 +212,15 @@
     return h[xi, y, pl.ds(zi, 16, stride=4), :]
 
 
-def rim_kernel(idx, h, vec, tabr, up, down, q, t, r0, r3):
+def rim_kernel(idx, h, vec, tabr, up, down, q, t, ends, m):
     pos = vec[0, 14:15] > 0.5
     for zi in range(4):
         def over_y(y, _):
             x = [every_fourth(h, xi, y, zi) for xi in range(4)]
             ql = jnp.where(pos, x[3], x[0])
             q[zi, y] = ql
-            r0[zi, y] = x[0]
-            r3[zi, y] = x[3]
+            ends[zi, y] = x[0]
+            ends[4 + zi, y] = x[3]
             v = 0.8 * ql
             for j in range(4):
                 v = v + vec[0, 15 + j:16 + j] * x[j]
@@ -233,11 +239,10 @@
         down[at] = jnp.where(right, tl, ql)
         return 0
     lax.fori_loop(0, 32, pack, 0)
-    for zi in range(4):
-        for out, layer in ((up, r3), (down, r0)):
-            m = jnp.dot(layer[zi].reshape(128, 128), tabr[0], precision=HI,
-                        preferred_element_type=jnp.float32)
-            out[512 + 8 * zi:520 + 8 * zi] = m.T[0:8]
+    m[...] = exact_dot(ends[...].reshape(1024, 128), tabr[0])
+    for n in range(8):
+        zi, out = n % 4, (down, up)[n // 4]
+        out[512 + 8 * zi:520 + 8 * zi] = m[128 * n:128 * n + 128].T[0:8]
 
 
 def local_update(src, dst, vec):
@@ -274,7 +279,7 @@
     lax.fori_loop(0, 16, over_c, 0)
 
 
-def local_kernel(idx, h, vec, tab0, tab1, twice, mom, first, once):
+def local_kernel(idx, h, vec, tab0, tab1, twice, mom, first, once, m):
     for c in range(16):
         xi, zi = c // 4, c % 4
 
@@ -285,14 +290,10 @@
     local_update(first, once, vec)
     local_update(once, twice, vec)
 
-    def moments(c, _):
-        m = jnp.dot(first[c].reshape(128, 128), tab0[0], precision=HI,
-                    preferred_element_type=jnp.float32)
-        m = m + jnp.dot(once[c].reshape(128, 128), tab1[0], precision=HI,
-                        preferred_element_type=jnp.float32)
-        mom[c] = m.T[32:48]
-        return 0
-    lax.fori_loop(0, 16, moments, 0)
+    m[...] = exact_dot(first[...].reshape(2048, 128), tab0[0])
+    m[...] = m[...] + exact_dot(once[...].reshape(2048, 128), tab1[0])
+    for c in range(16):
+        mom[c] = m[128 * c:128 * c + 128].T[32:48]
 
 
 def z_before(q, lt):
@@ -338,7 +339,7 @@
 
 
 def moment_kernel(idx, up, down, twice, moma, mix, lt, vec, tab2, tab1, pay, t2,
-                  delta, yz, extra, mom, full):
+                  delta, yz, extra, mom, full, m, stack):
     right = lax.broadcasted_iota(jnp.int32, (16, 128), 1) >= 64
     pos = vec[0, 14:15]
 
@@ -362,19 +363,14 @@
             return 0
         lax.fori_loop(0, 32, over_n, 0)
 
-        def over_z(zi, _):
-            c = xi * 4 + zi
-            m = jnp.dot(t2[c].reshape(128, 128), tab2[0], precision=HI,
-                        preferred_element_type=jnp.float32)
-            if xi in (0, 3):
-                w = pos if xi == 0 else 1.0 - pos
-                m = m + jnp.dot(delta[zi].reshape(128, 128) * w, tab1[0], precision=HI,
-                                preferred_element_type=jnp.float32)
-            m = m.T
-            mom[c, 0:32] = m[0:32]
-            mom[c, 32:48] = m[32:48] + moma[c]
-            return 0
-        lax.fori_loop(0, 4, over_z, 0)
+    m[...] = exact_dot(t2[...].reshape(2048, 128), tab2[0])
+    d = delta[...].reshape(512, 128)
+    m[0:512] = m[0:512] + exact_dot(d * pos, tab1[0])
+    m[1536:2048] = m[1536:2048] + exact_dot(d * (1.0 - pos), tab1[0])
+    for c in range(16):
+        t = m[128 * c:128 * c + 128].T
+        mom[c, 0:32] = t[0:32]
+        mom[c, 32:48] = t[32:48] + moma[c]
 
     def load0(c):
         return mom[c, 32:40]
@@ -382,10 +378,15 @@
     for c in range(16):
         six = one_sided(load0, lambda zi: up[512 + 8 * zi:520 + 8 * zi],
                         lambda zi: down[512 + 8 * zi:520 + 8 * zi], c, lt)
-        stack = jnp.concatenate([mom[c, 32:40], mom[c, 40:48]] + six, axis=0)
-        add = jnp.dot(mix[...], stack, precision=HI, preferred_element_type=jnp.float32)
-        full[c, 0:32] = mom[c, 0:32] + add[0:32]
-        full[c, 32:40] = add[32:40]
+        at = slice(128 * c, 128 * c + 128)
+        stack[0:16, at] = mom[c, 32:48]
+        for n in range(6):
+            stack[16 + 8 * n:24 + 8 * n, at] = six[n]
+    add = exact_dot(mix[...], stack[...])
+    for c in range(16):
+        at = slice(128 * c, 128 * c + 128)
+        full[c, 0:32] = mom[c, 0:32] + add[0:32, at]
+        full[c, 32:40] = add[32:40, at]
     for c in range(16):
         xi, zi = c // 4, c % 4
         r = combine(CENTRAL[xi], [full[j * 4 + zi, 8:16] for j in range(4)])
@@ -414,7 +415,7 @@
         out[n, 80:120] = t[80:120]
 
 
-def feq_kernel(idx, got, t2, lt, final, h2, low, s0, lo, hi):
+def feq_kernel(idx, got, t2, lt, final, h2, low, s0, lo, hi, stack):
     def total(a, n):
         return got[0, a:a + n] + got[1, a:a + n] + got[2, a:a + n] + got[3, a:a + n]
 
@@ -431,10 +432,11 @@
     for c in range(16):
         z = jnp.concatenate([0.2 * total(280 + 5 * c, 5), pad], axis=0) + 0.16 * s0[c]
         six = one_sided(lambda k: s0[k], lambda zi: lo[zi], lambda zi: hi[zi], c, lt)
-        stack = jnp.concatenate([z] + six, axis=0)
-        add = lax.dot_general(stack, final[0], (((0,), (0,)), ((), ())), precision=HI,
-                              preferred_element_type=jnp.float32)
-        h2[c] = t2[c] + add.reshape(8, 16, 128)
+        for n, v in enumerate([z] + six):
+            stack[8 * n:8 * n + 8, 128 * c:128 * c + 128] = v
+    add = lax.dot_general(stack[...], final[0], (((0,), (0,)), ((), ())), precision=HI,
+                          preferred_element_type=jnp.float32)
+    h2[...] = t2[...] + add.reshape(16, 8, 16, 128)
 
 
 def apply_operator(src, dst, lt):
@@ -453,7 +455,7 @@
             dst[xi * 4 + zi] = du
             dst[16 + xi * 4 + zi] = 2.0 * u[xi] + dp
         return 0
-    lax.fori_loop(0, 4, along_x, 0)
+    lax.fori_loop(0, 4, along_x, 0, unroll=True)
 
     def along_z(xi, _):
         u = [src[48 + xi * 4 + j] for j in range(4)]
@@ -470,7 +472,7 @@
             dst[xi * 4 + zi] = dst[xi * 4 + zi] + du
             dst[48 + xi * 4 + zi] = 2.0 * u[zi] + dp
         return 0
-    lax.fori_loop(0, 4, along_z, 0)
+    lax.fori_loop(0, 4, along_z, 0, unroll=True)
 
     def along_y(c, _):
         rho, u, t = src[c], src[32 + c], src[64 + c]
@@ -479,7 +481,7 @@
         dst[c] = 2.0 * rho + div
         dst[64 + c] = 2.0 * t + div
         return 0
-    lax.fori_loop(0, 16, along_y, 0)
+    lax.fori_loop(0, 16, along_y, 0, unroll=4)
 
 
 def two_level(r, pe, co, lt):
@@ -589,20 +591,43 @@
         gram[n] = rows
 
 
-def first_pass_kernel(idx, lower, mine, upper, lt, r, m, ar, am, pe, gram, co, lox, hix):
+def pack_kernel(idx, mine, own, to_upper, to_lower):
+    first = lax.broadcasted_iota(jnp.int32, (8, 128), 0) == 0
+    last = lax.broadcasted_iota(jnp.int32, (8, 128), 0) == 7
     for f in range(5):
         for zi in range(4):
-            for n, src in enumerate((lower, mine, upper)):
-                lox[f * 4 + zi, 8 * n:8 * n + 8] = src[pl.ds(80 + 5 * zi + f, 8, stride=120), :]
-                hix[f * 4 + zi, 8 * n:8 * n + 8] = src[pl.ds(100 + 5 * zi + f, 8, stride=120), :]
+            high = mine[pl.ds(100 + 5 * zi + f, 8, stride=120), :]
+            low = mine[pl.ds(80 + 5 * zi + f, 8, stride=120), :]
+            for xi in range(4):
+                c = xi * 4 + zi
+                k = f * 16 + c
+                v = mine[pl.ds(5 * c + f, 8, stride=120), :]
+                if xi == 0:
+                    v = v + 1.5 * jnp.where(first, 0.0, pltpu.roll(high, 1, 0))
+                if xi == 3:
+                    v = v - 1.5 * jnp.where(last, 0.0, pltpu.roll(low, 7, 0))
+                own[k] = v
+                to_upper[pl.ds(k, 6, stride=80), :] = v[2:8]
+                to_lower[pl.ds(k, 6, stride=80), :] = v[0:6]
+            to_upper[480 + f * 4 + zi:481 + f * 4 + zi] = high[7:8]
+            to_lower[480 + f * 4 + zi:481 + f * 4 + zi] = low[0:1]
+
+
+def first_pass_kernel(idx, lower, own, upper, edge_low, edge_high, lt, r, m, ar, am, pe, gram, co):
+    zero = jnp.zeros((2, 128), jnp.float32)
+    for f in range(5):
         for c in range(16):
             xi, zi = c // 4, c % 4
-            for n, src in enumerate((lower, mine, upper)):
-                r[f * 16 + c, 8 * n:8 * n + 8] = src[pl.ds(5 * c + f, 8, stride=120), :]
+            k, e = f * 16 + c, f * 4 + zi
+            r[k, 0:8] = jnp.concatenate([zero, lower[pl.ds(k, 6, stride=80), :]], axis=0)
+            r[k, 8:16] = own[k]
+            r[k, 16:24] = jnp.concatenate([upper[pl.ds(k, 6, stride=80), :], zero], axis=0)
             if xi == 0:
-                r[f * 16 + c] = r[f * 16 + c] + 1.5 * pltpu.roll(hix[f * 4 + zi], 1, 0)
+                r[k, 8:9] = r[k, 8:9] + 1.5 * lower[480 + e:481 + e]
+                r[k, 16:17] = r[k, 16:17] + 1.5 * edge_high[480 + e:481 + e]
             if xi == 3:
-                r[f * 16 + c] = r[f * 16 + c] - 1.5 * pltpu.roll(lox[f * 4 + zi], 23, 0)
+                r[k, 15:16] = r[k, 15:16] - 1.5 * upper[480 + e:481 + e]
+                r[k, 7:8] = r[k, 7:8] - 1.5 * edge_low[480 + e:481 + e]
     pass_words(r, m, ar, am, pe, co, gram, lt, gram.shape[0])
 
 
@@ -634,25 +659,35 @@
     pass_words(r2, m2, ar2, am2, pe2, co, gram, lt, gram.shape[0])
 
 
-def last_kernel(idx, sums, r, m, pe, acc, low, h2, ec, out, fields, change):
+def third_pass_kernel(idx, sums, r, m, ar, am, pe, acc, lt, ro, mo, po, acc2, gram,
+                      r2, m2, ar2, am2, pe2, co):
+    next_pass_kernel(False, idx, sums, r, m, ar, am, pe, acc, lt, r2, m2, ar2, am2, pe2, acc2, gram, co)
+    ro[...] = r2[:, 8:16]
+    mo[...] = m2[:, 8:16]
+    po[...] = pe2[:, 8:16]
+
+
+def last_kernel(idx, sums, r, m, pe, acc, low, h2, ec, out, fields, change, stack):
     a1, a2 = step_sizes(sums, sums.shape[0])
 
     def over_k(k, _):
-        q = r[k, 8:16] - a1 * m[k, 8:16]
-        change[pl.ds(pl.multiple_of(k * 8, 8), 8)] = acc[k] + a1 * pe[k, 8:16] + a2 * q
+        q = r[k] - a1 * m[k]
+        change[pl.ds(pl.multiple_of(k * 8, 8), 8)] = acc[k] + a1 * pe[k] + a2 * q
         return 0
     lax.fori_loop(0, 80, over_k, 0, unroll=4)
     z = idx[1]
-    zero = jnp.zeros((3, 128), jnp.float32)
+    stack[...] = jnp.zeros_like(stack)
+    for c in range(16):
+        for f in range(5):
+            k = f * 16 + c
+            d = change[pl.ds(k * 8 + z, 1)]
+            stack[f:f + 1, 128 * c:128 * c + 128] = d
+            fields[k:k + 1] = low[5 * c + f:5 * c + f + 1] + d
+    add = lax.dot_general(stack[...], ec[0], (((0,), (0,)), ((), ())), precision=HI,
+                          preferred_element_type=jnp.float32).reshape(16, 8, 16, 128)
     for c in range(16):
         xi, zi = c // 4, c % 4
-        d = jnp.concatenate([change[pl.ds((f * 16 + c) * 8 + z, 1)] for f in range(5)] + [zero], axis=0)
-        new = low[5 * c:5 * c + 5] + d[0:5]
-        for f in range(5):
-            fields[16 * f + c:16 * f + c + 1] = new[f:f + 1]
-        add = lax.dot_general(d, ec[0], (((0,), (0,)), ((), ())), precision=HI,
-                              preferred_element_type=jnp.float32)
-        v = h2[c] + add.reshape(8, 16, 128)
+        v = h2[c] + add[c]
         for y in range(8):
             out[xi, y, pl.ds(zi, 16, stride=4), :] = v[y]
 
@@ -671,41 +706,44 @@
         return lax.ppermute(x, "space", [(i, (i + by) % spaces) for i in range(spaces)])
 
     up, down = call(rim_kernel, "rims", idx, [distribution], [vec, tables["tabr"]],
-                    [(544, 128)] * 2, [layer] * 4)
+                    [(544, 128)] * 2, [layer, layer, (8, 8, 16, 128), (1024, 128)])
     up, down = shifted(up, 1), shifted(down, -1)
     twice, moma = call(local_kernel, "local", idx, [distribution],
                        [vec, tables["tab0"], tables["tab1"]],
-                       [wide, (16, 16, 128)], [wide, wide])
+                       [wide, (16, 16, 128)], [wide, wide, (2048, 128)])
     force = jnp.pad(forcing, ((1, 1), (0, 0), (0, 0), (0, 0)))
     force = force.reshape(5, 4, 8, 16, 4).transpose(1, 4, 0, 2, 3).reshape(80, 128)
     pay, t2 = call(moment_kernel, "moments", idx, [up, down, twice, moma, tables["mix"], lt],
                    [vec, tables["tab2"], tables["tab1"]], [(400, 128), wide],
-                   [layer, layer, layer, (16, 48, 128), (16, 40, 128)])
+                   [layer, layer, layer, (16, 48, 128), (16, 40, 128), (2048, 128), (64, 2048)])
     got = lax.all_gather(pay, "vel")
     (res,) = call(lambda i, g, fo, o: residual_kernel(i, g, fo, o, 8), "residual", idx,
                   [got, force], [], [(8, 120, 128)])
     near = [[a * 8 + b for b in range(8)] for a in range(blocks)]
     far = [[a * 8 + b for a in range(blocks)] for b in range(8)]
     mine = lax.all_to_all(res, "space", 0, 0, axis_index_groups=near, tiled=True).reshape(960, 128)
-    lower, upper = shifted(mine, 8), shifted(mine, -8)
+    own_r, to_upper, to_lower = call(pack_kernel, "pack", idx, [mine], [],
+                                     [(80, 8, 128), (500, 128), (500, 128)])
+    lower, upper = shifted(to_upper, 8), shifted(to_lower, -8)
     h2, low = call(feq_kernel, "feq", idx, [got, t2, lt], [tables["final"]],
-                   [wide, (80, 128)], [(16, 8, 128), (4, 8, 128), (4, 8, 128)])
+                   [wide, (80, 128)], [(16, 8, 128), (4, 8, 128), (4, 8, 128), (56, 2048)])
 
     def summed(gram):
         return lax.all_to_all(gram, "space", 0, 0, axis_index_groups=far, tiled=True)
 
     win, own, part = (80, 24, 128), (80, 8, 128), (blocks, 8, 128)
     co = (40, 24, 128)
-    r, m, ar, am, pe, gram = call(first_pass_kernel, "pass1", idx, [lower, mine, upper, lt], [],
-                                  [win] * 5 + [part], [co, (20, 24, 128), (20, 24, 128)])
+    r, m, ar, am, pe, gram = call(first_pass_kernel, "pass1", idx,
+                                  [lower, own_r, upper, to_lower, to_upper, lt], [],
+                                  [win] * 5 + [part], [co])
     r, m, ar, am, pe, acc, gram = call(functools.partial(next_pass_kernel, True), "pass2", idx,
                                        [summed(gram), r, m, ar, am, pe, lt], [],
                                        [win] * 5 + [own, part], [co])
-    r, m, ar, am, pe, acc, gram = call(functools.partial(next_pass_kernel, False), "pass3", idx,
-                                       [summed(gram), r, m, ar, am, pe, acc, lt], [],
-                                       [win] * 5 + [own, part], [co])
+    r, m, pe, acc, gram = call(third_pass_kernel, "pass3", idx,
+                               [summed(gram), r, m, ar, am, pe, acc, lt], [],
+                               [own] * 4 + [part], [win] * 5 + [co])
     out, fields = call(last_kernel, "last", idx, [summed(gram), r, m, pe, acc, low, h2],
-                       [tables["ec"]], [(4, 8, 64, 128), (80, 128)], [(640, 128)])
+                       [tables["ec"]], [(4, 8, 64, 128), (80, 128)], [(640, 128), (8, 2048)])
     fields = fields.reshape(5, 4, 4, 8, 16).transpose(0, 1, 3, 4, 2).reshape(5, 4, 8, 64)
     return out, fields
 

time: 178 us -> 138 us (0.78)
  Pallas kernels: 81.2 us -> 39.7 us
  waiting for transfers between devices: 19.5 us -> 12.1 us
  local copies, waits for them, and re-layouts: 5.52 us -> 12.6 us
  starting transfers between devices: 15.2 us -> 19.1 us
    pallas_call x9 -> x10, Pallas kernels: 81.2 us -> 39.7 us  [call(): pl.pallas_call(body, name=name, out_shape=[jax.ShapeDtypeStruct(s, jnp.fl...]
    ppermute x4, waiting for transfers between devices: 16.2 us -> 6.17 us  [shifted(): lax.ppermute(x, 'space', [(i, (i + by) % spaces) for i in range(spaces)])]
    unnamed x16 -> x38, local copies, waits for them, and re-layouts: 3.25 us -> 9.8 us
    ppermute x4, starting transfers between devices: 11.9 us -> 15.7 us  [shifted(): lax.ppermute(x, 'space', [(i, (i + by) % spaces) for i in range(spaces)])]
    all_to_all x1, waiting for transfers between devices: 3.25 us -> 5.9 us  [summed(): lax.all_to_all(gram, 'space', 0, 0, axis_index_groups=far, tiled=True)]
  transfers between devices with their start and end apart: 5 -> 5, of which waited for: 3 -> 2; matrix products, arithmetic and copies ran while one was open for 1% -> 2% of each run, Pallas kernels for 9% -> 5%
where the time goes in v1:
time: 138 us; the launch traced here: 137 us
  blocking collectives  53 us (38%)
  Pallas kernels  39.7 us (29%)
  starting transfers between devices  19.1 us (14%)
  local copies, waits for them, and re-layouts  12.6 us (9%)
  waiting for transfers between devices  12.1 us (9%)
    pallas_call x10, Pallas kernels, call(): pl.pallas_call(body, name=name, out_shape=[jax.ShapeDtypeStruct(s, jnp.fl...  39.7 us
    all_to_all x2, blocking collectives, summed(): lax.all_to_all(gram, 'space', 0, 0, axis_index_groups=far, tiled=True)  24.3 us
    all_to_all x1, blocking collectives, on_device(): lax.all_to_all(res, 'space', 0, 0, axis_index_groups=near, tiled=True)  20 us
    ppermute x4, starting transfers between devices, shifted(): lax.ppermute(x, 'space', [(i, (i + by) % spaces) for i in range(spaces)])  15.7 us
    unnamed x38, local copies, waits for them, and re-layouts  9.8 us
    all_gather x1, blocking collectives, on_device(): got = lax.all_gather(pay, 'vel')  8.72 us
    ppermute x4, waiting for transfers between devices, shifted(): lax.ppermute(x, 'space', [(i, (i + by) % spaces) for i in range(spaces)])  6.17 us
    all_to_all x1, waiting for transfers between devices, summed(): lax.all_to_all(gram, 'space', 0, 0, axis_index_groups=far, tiled=True)  5.9 us
  transfers between devices with their start and end apart: 5, of which 2 were waited for; matrix products, arithmetic and copies ran while one was open for 2% of the time, Pallas kernels for 5%

profile of v1, /device:TPU:2, one launch (start us, length us, event | category | flops | bytes accessed | tf_op | source)
XLA Modules:
  0.0 137.4 jit_solution(3153787218184534086)
XLA Ops:
  0.6 0.0 copy-start.4
  0.7 0.1 pad_add_fusion.idx
  0.7 0.7 copy-done.4
  1.4 1.2 copy-done
  2.7 0.9 copy-done.12
  3.6 4.0 %rims.1 = (f32[544,128]{1,0:T(8,128)S(1)}, f32[544,128]{1,0:T(8,128)S(1)}) custom-call(s32[2]{0:T(128)S(1)} %pad_add_fusion.idx, f32[4,8,64,128]{3,2,1,0:T(8,128)S(1)} %copy-done, f32[4,24,128]{2,1,0:T(8,128)S(1)} %copy-done.4, f32[4,128,128]{2,1,0:T(8,128)S(1)} %copy-done.12), custom_call_target="tpu_custom_call" | custom-call | tf_op jit(solution)/shard_map/rims/pallas_call | solution.py:158
  7.6 2.0 %collective-permute-start = (f32[544,128]{1,0:T(8,128)S(1)}, f32[544,128]{1,0:T(8,128)S(1)}, u32[]{:S(2)}, u32[]{:S(2)}) collective-permute-start(f32[544,128]{1,0:T(8,128)S(1)} %get-tuple-element.33), channel_id=1, source_target_pairs={{0,1},{1,2},{2,3},{3,4},{4,5},{5,6},{6,7},{7,8},{8,9},{9,10},{10,1... | collective-permute-start | bytes 835592 | tf_op jit(solution)/shard_map/ppermute | solution.py:706
  9.6 8.0 %collective-permute-start.1 = (f32[544,128]{1,0:T(8,128)S(1)}, f32[544,128]{1,0:T(8,128)S(1)}, u32[]{:S(2)}, u32[]{:S(2)}) collective-permute-start(f32[544,128]{1,0:T(8,128)S(1)} %get-tuple-element.34), channel_id=1, source_target_pairs={{0,63},{1,0},{2,1},{3,2},{4,3},{5,4},{6,5},{7,6},{8,7},{9,8},{10,9... | collective-permute-start | bytes 835592 | tf_op jit(solution)/shard_map/ppermute | solution.py:706
  17.6 0.0 copy-done.17
  17.6 0.2 copy.19
  17.8 0.0 copy-start.1
  17.8 0.9 pad.4.clone
  18.7 1.4 copy.16
  20.1 0.0 copy-start.2
  20.1 0.1 reshape.20.refs_1_
  20.2 0.0 copy-done.1
  20.3 0.8 copy-done.2
  21.0 5.6 %local.1 = (f32[16,8,16,128]{3,2,1,0:T(8,128)S(1)}, f32[16,16,128]{2,1,0:T(8,128)S(1)}) custom-call(s32[2]{0:T(128)S(1)} %pad_add_fusion.idx, f32[4,8,64,128]{3,2,1,0:T(8,128)S(1)} %copy-done.1, f32[4,24,128]{2,1,0:T(8,128)S(1)} %copy-done.4, f32[4,128,128]{2,1,0:T(8,128)S(1)} %copy-done.13, f32[4,128,128]{2,1,0:T(8,128)S(1)} %copy-done.2), custom_call_target="tpu_custom_call" | custom-call | tf_op jit(solution)/shard_map/local/pallas_call | solution.py:158
  26.7 0.0 collective-permute-done.refs_0_
  26.7 0.0 collective-permute-done.1.refs_1_
  26.7 7.2 %moments.1 = (f32[400,128]{1,0:T(8,128)S(1)}, f32[16,8,16,128]{3,2,1,0:T(8,128)S(1)}) custom-call(s32[2]{0:T(128)S(1)} %pad_add_fusion.idx, f32[544,128]{1,0:T(8,128)S(1)} %collective-permute-done.refs_0_, f32[544,128]{1,0:T(8,128)S(1)} %collective-permute-done.1.refs_1_, f32[16,8,16,128]{3,2,1,0:T(8,128)S(1)} %get-tuple-element.35.refs_2_, ...), custom_call_target="tpu_custom_call" | custom-call | tf_op jit(solution)/shard_map/moments/pallas_call | solution.py:158
  33.9 8.7 %all-gather = f32[1600,128]{1,0:T(8,128)S(1)} all-gather(f32[400,128]{1,0:T(8,128)S(1)} %get-tuple-element.37), channel_id=2, replica_groups=mesh['vel'=4,'space'=64] {'vel'}, dimensions={0}, use_global_device_ids=true | all-gather | bytes 1024000 | tf_op jit(solution)/shard_map/all_gather | solution.py:719
  42.6 0.6 residual.1
  43.2 20.0 %all_to_all.20 = f32[8,120,128]{2,1,0:T(8,128)S(1)} all-to-all(f32[8,120,128]{2,1,0:T(8,128)S(1)} %residual.1), channel_id=1, replica_groups={{0,1,2,3,4,5,6,7},{8,9,10,11,12,13,14,15},{16,17,18,19,20,21,22,23},{24..., dimensions={0} | all-to-all | bytes 983040 | tf_op jit(solution)/shard_map/all_to_all | solution.py:724
  63.2 0.8 pack.1
  64.0 0.1 collective-permute-start.2
  64.0 5.6 %collective-permute-start.3 = (f32[500,128]{1,0:T(8,128)S(1)}, f32[500,128]{1,0:T(8,128)S(1)}, u32[]{:S(2)}, u32[]{:S(2)}) collective-permute-start(f32[500,128]{1,0:T(8,128)S(1)} %get-tuple-element.40.refs_3_), channel_id=1, source_target_pairs={{0,56},{1,57},{2,58},{3,59},{4,60},{5,61},{6,62},{7,63},{8,0},{9,1... | collective-permute-start | bytes 768008 | tf_op jit(solution)/shard_map/ppermute | solution.py:706
  69.7 6.2 %collective-permute-done.2.refs_0_ = f32[500,128]{1,0:T(8,128)S(1)} collective-permute-done((f32[500,128]{1,0:T(8,128)S(1)}, f32[500,128]{1,0:T(8,128)S(1)}, u32[]{:S(2)}, u32[]{:S(2)}) %collective-permute-start.2) | collective-permute-done | bytes 256032 | tf_op jit(solution)/shard_map/ppermute | solution.py:706
  75.8 0.0 collective-permute-done.3.refs_2_
  75.8 5.3 %pass1.1 = (f32[80,24,128]{2,1,0:T(8,128)S(1)}, f32[80,24,128]{2,1,0:T(8,128)S(1)}, f32[80,24,128]{2,1,0:T(8,128)S(1)}, f32[80,24,128]{2,1,0:T(8,128)S(1)}, f32[...) custom-call(s32[2]{0:T(128)S(1)} %pad_add_fusion.idx, f32[500,128]{1,0:T(8,128)S(1)} %collective-permute-done.2.refs_0_, ...), custom_call_target="tpu_custom_call" | custom-call | tf_op jit(solution)/shard_map/pass1/pallas_call | solution.py:158
  81.1 14.2 %all_to_all.21.refs_0_ = f32[8,8,128]{2,1,0:T(8,128)S(1)} all-to-all(f32[8,8,128]{2,1,0:T(8,128)S(1)} %get-tuple-element.41), channel_id=1, replica_groups={{0,8,16,24,32,40,48,56},{1,9,17,25,33,41,49,57},{2,10,18,26,34,42,50,58..., dimensions={0} | all-to-all | bytes 65536 | tf_op jit(solution)/shard_map/all_to_all | solution.py:732
  95.3 5.5 %pass2.1 = (f32[80,24,128]{2,1,0:T(8,128)S(1)}, f32[80,24,128]{2,1,0:T(8,128)S(1)}, f32[80,24,128]{2,1,0:T(8,128)S(1)}, f32[80,24,128]{2,1,0:T(8,128)S(1)}, f32[...) custom-call(s32[2]{0:T(128)S(1)} %pad_add_fusion.idx, ...), custom_call_target="tpu_custom_call" | custom-call | tf_op jit(solution)/shard_map/pass2/pallas_call | solution.py:158
  100.8 10.1 %all_to_all.22.refs_0_ = f32[8,8,128]{2,1,0:T(8,128)S(1)} all-to-all(f32[8,8,128]{2,1,0:T(8,128)S(1)} %get-tuple-element.47), channel_id=1, replica_groups={{0,8,16,24,32,40,48,56},{1,9,17,25,33,41,49,57},{2,10,18,26,34,42,50,58..., dimensions={0} | all-to-all | bytes 65536 | tf_op jit(solution)/shard_map/all_to_all | solution.py:732
  111.0 6.1 %pass3.1 = (f32[80,8,128]{2,1,0:T(8,128)S(1)}, f32[80,8,128]{2,1,0:T(8,128)S(1)}, f32[80,8,128]{2,1,0:T(8,128)S(1)}, f32[80,8,128]{2,1,0:T(8,128)S(1)}, f32[8,8,128]{2,1,0:T(8,128)}) custom-call(s32[2]{0:T(128)S(1)} %pad_add_fusion.idx, f32[8,8,128]{2,1,0:T(8,128)S(1)} %all_to_all.22.refs_0_, f32[80,24,128]{2,1,0:T(8,128)S(1)} %get-tuple-element.48.refs_1_, ...), custom_call_target="tpu_custom_call" | custom-call | tf_op jit(solution)/shard_map/pass3/pallas_call | solution.py:158
  117.1 0.7 copy-done.5
  117.8 0.7 copy-done.7
  118.5 0.7 copy-done.9
  119.3 3.3 %all-to-all-start.3 = ((f32[8,8,128]{2,1,0:T(8,128)}), f32[8,8,128]{2,1,0:T(8,128)S(1)}, u32[]{:S(2)}, u32[]{:S(2)}) async-start(f32[8,8,128]{2,1,0:T(8,128)} %get-tuple-element.54), calls=%async_computation.3 | async-start | bytes 65536 | tf_op jit(solution)/shard_map/all_to_all | solution.py:732
  122.6 0.0 copy-start.16
  122.6 1.8 %feq.1 = (f32[16,8,16,128]{3,2,1,0:T(8,128)S(1)}, f32[80,128]{1,0:T(8,128)S(1)}) custom-call(s32[2]{0:T(128)S(1)} %pad_add_fusion.idx, f32[4,400,128]{2,1,0:T(8,128)S(1)} %bitcast.13, f32[16,8,16,128]{3,2,1,0:T(8,128)S(1)} %get-tuple-element.59.refs_1_, f32[40,128]{1,0:T(8,128)S(1)} %copy-done.3, f32[4,56,128]{2,1,0:T(8,128)S(1)} %copy-done.14), custom_call_target="tpu_custom_call" | custom-call | tf_op jit(solution)/shard_map/feq/pallas_call | solution.py:158
  124.4 5.9 %all-to-all-done.3.refs_0_ = f32[8,8,128]{2,1,0:T(8,128)S(1)} async-done(((f32[8,8,128]{2,1,0:T(8,128)}), f32[8,8,128]{2,1,0:T(8,128)S(1)}, u32[]{:S(2)}, u32[]{:S(2)}) %all-to-all-start.3) | async-done | bytes 32800 | tf_op jit(solution)/shard_map/all_to_all | solution.py:732
  130.3 1.0 copy-done.6
  131.3 1.0 copy-done.8
  132.3 1.0 copy-done.10
  133.2 2.9 %last.1 = (f32[4,8,64,128]{3,2,1,0:T(8,128)}, f32[80,128]{1,0:T(8,128)S(1)}) custom-call(s32[2]{0:T(128)S(1)} %pad_add_fusion.idx, f32[8,8,128]{2,1,0:T(8,128)S(1)} %all-to-all-done.3.refs_0_, f32[80,8,128]{2,1,0:T(8,128)S(1)} %get-tuple-element.55.refs_1_, f32[80,8,128]{2,1,0:T(8,128)S(1)} %copy-done.6, f32[80,8,128]{2,1,0:T(8,128)S(1)} %copy-done.8, ...), custom_call_target="tpu_custom_call" | custom-call | tf_op jit(solution)/shard_map/last/pallas_call | solution.py:158
  136.1 0.1 reshape.22
  136.2 0.3 copy.17
  136.5 0.9 copy.18
  (20 shorter events, 0.0 us)
Async XLA Ops:
  0.6 0.8 copy-start.4
  1.4 1.2 copy-start
  2.7 0.9 copy-start.12
  3.6 14.0 %copy-start.17 = (f32[3,4,8,64]{3,2,1,0:T(8,128)S(1)}, f32[3,4,8,64]{3,2,1,0:T(8,128)}, u32[]{:S(2)}) copy-start(f32[3,4,8,64]{3,2,1,0:T(8,128)} %param.12) | copy-start | bytes 73732
  7.6 19.0 %collective-permute-start = (f32[544,128]{1,0:T(8,128)S(1)}, f32[544,128]{1,0:T(8,128)S(1)}, u32[]{:S(2)}, u32[]{:S(2)}) collective-permute-start(f32[544,128]{1,0:T(8,128)S(1)} %get-tuple-element.33), channel_id=1, source_target_pairs={{0,1},{1,2},{2,3},{3,4},{4,5},{5,6},{6,7},{7,8},{8,9},{9,10},{10,1... | collective-permute-start | bytes 835592 | tf_op jit(solution)/shard_map/ppermute | solution.py:706
  9.6 17.1 %collective-permute-start.1 = (f32[544,128]{1,0:T(8,128)S(1)}, f32[544,128]{1,0:T(8,128)S(1)}, u32[]{:S(2)}, u32[]{:S(2)}) collective-permute-start(f32[544,128]{1,0:T(8,128)S(1)} %get-tuple-element.34), channel_id=1, source_target_pairs={{0,63},{1,0},{2,1},{3,2},{4,3},{5,4},{6,5},{7,6},{8,7},{9,8},{10,9... | collective-permute-start | bytes 835592 | tf_op jit(solution)/shard_map/ppermute | solution.py:706
  17.8 2.4 %copy-start.1 = (f32[4,8,64,128]{3,2,1,0:T(8,128)S(1)}, f32[4,8,64,128]{3,2,1,0:T(8,128)}, u32[]{:S(2)}) copy-start(f32[4,8,64,128]{3,2,1,0:T(8,128)} %refs_0_.3) | copy-start | bytes 3145732
  18.7 1.5 %copy-start.13 = (f32[4,128,128]{2,1,0:T(8,128)S(1)}, f32[4,128,128]{2,1,0:T(8,128)}, u32[]{:S(2)}) copy-start(f32[4,128,128]{2,1,0:T(8,128)} %constant.46.clone.refs_2_) | copy-start | bytes 786436
  20.1 1.0 copy-start.2
  21.0 5.6 %copy-start.3 = (f32[40,128]{1,0:T(8,128)S(1)}, f32[40,128]{1,0:T(8,128)}, u32[]{:S(2)}) copy-start(f32[40,128]{1,0:T(8,128)} %constant.50.clone.refs_5_.refs_6_.refs_7_.refs_2_) | copy-start | bytes 61444
  21.0 5.7 %copy-start.11 = (f32[4,128,128]{2,1,0:T(8,128)S(1)}, f32[4,128,128]{2,1,0:T(8,128)}, u32[]{:S(2)}) copy-start(f32[4,128,128]{2,1,0:T(8,128)} %constant.44.clone.refs_7_) | copy-start | bytes 786436
  21.0 5.7 %copy-start.15 = (f32[40,64]{1,0:T(8,128)S(1)}, f32[40,64]{1,0:T(8,128)}, u32[]{:S(2)}) copy-start(f32[40,64]{1,0:T(8,128)} %constant.48.clone.refs_4_) | copy-start | bytes 30724
  64.0 11.9 %collective-permute-start.2 = (f32[500,128]{1,0:T(8,128)S(1)}, f32[500,128]{1,0:T(8,128)S(1)}, u32[]{:S(2)}, u32[]{:S(2)}) collective-permute-start(f32[500,128]{1,0:T(8,128)S(1)} %get-tuple-element.38.refs_4_), channel_id=1, source_target_pairs={{0,8},{1,9},{2,10},{3,11},{4,12},{5,13},{6,14},{7,15},{8,16},{9,17... | collective-permute-start | bytes 768008 | tf_op jit(solution)/shard_map/ppermute | solution.py:706
  64.0 11.8 %collective-permute-start.3 = (f32[500,128]{1,0:T(8,128)S(1)}, f32[500,128]{1,0:T(8,128)S(1)}, u32[]{:S(2)}, u32[]{:S(2)}) collective-permute-start(f32[500,128]{1,0:T(8,128)S(1)} %get-tuple-element.40.refs_3_), channel_id=1, source_target_pairs={{0,56},{1,57},{2,58},{3,59},{4,60},{5,61},{6,62},{7,63},{8,0},{9,1... | collective-permute-start | bytes 768008 | tf_op jit(solution)/shard_map/ppermute | solution.py:706
  111.0 11.6 %copy-start.14 = (f32[4,56,128]{2,1,0:T(8,128)S(1)}, f32[4,56,128]{2,1,0:T(8,128)}, u32[]{:S(2)}) copy-start(f32[4,56,128]{2,1,0:T(8,128)} %constant.49.clone.refs_3_) | copy-start | bytes 344068
  117.1 0.7 copy-start.5
  117.8 0.7 copy-start.7
  118.5 0.7 copy-start.9
  119.3 11.0 %all-to-all-start.3 = ((f32[8,8,128]{2,1,0:T(8,128)}), f32[8,8,128]{2,1,0:T(8,128)S(1)}, u32[]{:S(2)}, u32[]{:S(2)}) async-start(f32[8,8,128]{2,1,0:T(8,128)} %get-tuple-element.54), calls=%async_computation.3 | async-start | bytes 65536 | tf_op jit(solution)/shard_map/all_to_all | solution.py:732
  122.6 7.7 %copy-start.16 = (f32[4,8,128]{2,1,0:T(8,128)S(1)}, f32[4,8,128]{2,1,0:T(8,128)}, u32[]{:S(2)}) copy-start(f32[4,8,128]{2,1,0:T(8,128)} %constant.51.clone.refs_7_) | copy-start | bytes 49156
  130.3 1.0 copy-start.6
  131.3 1.0 copy-start.8
  132.3 1.0 copy-start.10

commit v2 on v1

--- a/solution.py
+++ b/solution.py
@@ -93,16 +93,19 @@
         vec.append(zero)
     vec = per_rank(np.stack(vec))
 
-    def moment_columns(start, rows):
-        out = np.zeros((4, 128, 128))
-        for r in range(4):
-            out[r, :, start:start + len(rows)] = rows[:, r * 128:(r + 1) * 128].T
-        return out.astype(np.float32)
-
-    tab2 = moment_columns(0, rows32)
-    tab1 = moment_columns(40, low)
-    tab0 = moment_columns(32, low)
-    tabr = moment_columns(0, low)
+    def moment_rows(start, rows, height):
+        out = np.zeros((height, 512))
+        out[start:start + len(rows)] = rows
+        return per_rank(out)
+
+    tab2 = moment_rows(0, rows32, 48)
+    tab1 = moment_rows(40, low, 48)
+    tab0 = moment_rows(32, low, 48)
+    tabr = moment_rows(0, low, 8)
+    select = np.zeros((64, 512))
+    for n in range(4):
+        for la in range(128):
+            select[4 * (la % 16) + n, 128 * n + la] = 1.0
     g = rows32 @ ec.T
     g5 = g[:8]
     mix = np.zeros((40, 64))
@@ -144,7 +147,7 @@
         rows.append(np.zeros(128))
     lanes = np.stack(rows).astype(np.float32)
     return dict(vec=vec, tab2=tab2, tab1=tab1, tab0=tab0, tabr=tabr, mix=mix.astype(np.float32),
-                final=final, lanes=lanes, ec=per_rank(ec))
+                final=final, lanes=lanes, ec=per_rank(ec), select=select.astype(np.float32))
 
 
 def call(kernel, name, idx, full, ranked, outs, scratch=(), limit=24):
@@ -169,6 +172,11 @@
 
 def exact_dot(a, b):
     return jnp.dot(a, b, precision=HI, preferred_element_type=jnp.float32)
+
+
+def project(x, rows):
+    return lax.dot_general(x, rows, (((1,), (1,)), ((), ())), precision=HI,
+                           preferred_element_type=jnp.float32)
 
 
 def combine(row, values):
@@ -239,10 +247,10 @@
         down[at] = jnp.where(right, tl, ql)
         return 0
     lax.fori_loop(0, 32, pack, 0)
-    m[...] = exact_dot(ends[...].reshape(1024, 128), tabr[0])
+    m[...] = project(ends[...].reshape(1024, 128), tabr[0])
     for n in range(8):
         zi, out = n % 4, (down, up)[n // 4]
-        out[512 + 8 * zi:520 + 8 * zi] = m[128 * n:128 * n + 128].T[0:8]
+        out[512 + 8 * zi:520 + 8 * zi] = m[128 * n:128 * n + 128].T
 
 
 def local_update(src, dst, vec):
@@ -279,7 +287,20 @@
     lax.fori_loop(0, 16, over_c, 0)
 
 
-def local_kernel(idx, h, vec, tab0, tab1, twice, mom, first, once, m):
+def row_of_y():
+    y = lax.broadcasted_iota(jnp.int32, (8, 128), 0)
+    return (lax.broadcasted_iota(jnp.int32, (8, 128), 1) // 16 == y).astype(jnp.float32)
+
+
+def local_kernel(idx, h, forcing, select, vec, tab0, tab1, twice, mom, force, first, once, m):
+    spread = exact_dot(forcing[...].reshape(96, 64), select[...])
+    here = row_of_y()
+    force[...] = jnp.zeros_like(force)
+    for f in range(3):
+        for c in range(16):
+            n = 8 * (f * 4 + c // 4)
+            v = spread[n:n + 8, 128 * (c % 4):128 * (c % 4) + 128] * here
+            force[5 * c + f + 1:5 * c + f + 2] = jnp.sum(v, axis=0, keepdims=True)
     for c in range(16):
         xi, zi = c // 4, c % 4
 
@@ -290,8 +311,8 @@
     local_update(first, once, vec)
     local_update(once, twice, vec)
 
-    m[...] = exact_dot(first[...].reshape(2048, 128), tab0[0])
-    m[...] = m[...] + exact_dot(once[...].reshape(2048, 128), tab1[0])
+    m[...] = project(first[...].reshape(2048, 128), tab0[0])
+    m[...] = m[...] + project(once[...].reshape(2048, 128), tab1[0])
     for c in range(16):
         mom[c] = m[128 * c:128 * c + 128].T[32:48]
 
@@ -363,10 +384,10 @@
             return 0
         lax.fori_loop(0, 32, over_n, 0)
 
-    m[...] = exact_dot(t2[...].reshape(2048, 128), tab2[0])
+    m[...] = project(t2[...].reshape(2048, 128), tab2[0])
     d = delta[...].reshape(512, 128)
-    m[0:512] = m[0:512] + exact_dot(d * pos, tab1[0])
-    m[1536:2048] = m[1536:2048] + exact_dot(d * (1.0 - pos), tab1[0])
+    m[0:512] = m[0:512] + project(d * pos, tab1[0])
+    m[1536:2048] = m[1536:2048] + project(d * (1.0 - pos), tab1[0])
     for c in range(16):
         t = m[128 * c:128 * c + 128].T
         mom[c, 0:32] = t[0:32]
@@ -613,7 +634,7 @@
             to_lower[480 + f * 4 + zi:481 + f * 4 + zi] = low[0:1]
 
 
-def first_pass_kernel(idx, lower, own, upper, edge_low, edge_high, lt, r, m, ar, am, pe, gram, co):
+def first_pass_kernel(idx, lower, own, upper, edge_low, edge_high, after, lt, r, m, ar, am, pe, gram, co):
     zero = jnp.zeros((2, 128), jnp.float32)
     for f in range(5):
         for c in range(16):
@@ -667,7 +688,7 @@
     po[...] = pe2[:, 8:16]
 
 
-def last_kernel(idx, sums, r, m, pe, acc, low, h2, ec, out, fields, change, stack):
+def last_kernel(idx, sums, r, m, pe, acc, low, h2, select, ec, out, fields, change, stack, rows):
     a1, a2 = step_sizes(sums, sums.shape[0])
 
     def over_k(k, _):
@@ -677,12 +698,15 @@
     lax.fori_loop(0, 80, over_k, 0, unroll=4)
     z = idx[1]
     stack[...] = jnp.zeros_like(stack)
+    here = row_of_y()
     for c in range(16):
         for f in range(5):
             k = f * 16 + c
             d = change[pl.ds(k * 8 + z, 1)]
             stack[f:f + 1, 128 * c:128 * c + 128] = d
-            fields[k:k + 1] = low[5 * c + f:5 * c + f + 1] + d
+            n = 8 * (k // 4)
+            rows[n:n + 8, 128 * (c % 4):128 * (c % 4) + 128] = (low[5 * c + f:5 * c + f + 1] + d) * here
+    fields[...] = project(rows[...], select[...]).reshape(5, 4, 8, 64)
     add = lax.dot_general(stack[...], ec[0], (((0,), (0,)), ((), ())), precision=HI,
                           preferred_element_type=jnp.float32).reshape(16, 8, 16, 128)
     for c in range(16):
@@ -706,16 +730,14 @@
         return lax.ppermute(x, "space", [(i, (i + by) % spaces) for i in range(spaces)])
 
     up, down = call(rim_kernel, "rims", idx, [distribution], [vec, tables["tabr"]],
-                    [(544, 128)] * 2, [layer, layer, (8, 8, 16, 128), (1024, 128)])
+                    [(544, 128)] * 2, [layer, layer, (8, 8, 16, 128), (1024, 8)])
     up, down = shifted(up, 1), shifted(down, -1)
-    twice, moma = call(local_kernel, "local", idx, [distribution],
-                       [vec, tables["tab0"], tables["tab1"]],
-                       [wide, (16, 16, 128)], [wide, wide, (2048, 128)])
-    force = jnp.pad(forcing, ((1, 1), (0, 0), (0, 0), (0, 0)))
-    force = force.reshape(5, 4, 8, 16, 4).transpose(1, 4, 0, 2, 3).reshape(80, 128)
+    twice, moma, force = call(local_kernel, "local", idx, [distribution, forcing, tables["select"]],
+                              [vec, tables["tab0"], tables["tab1"]],
+                              [wide, (16, 16, 128), (80, 128)], [wide, wide, (2048, 48)])
     pay, t2 = call(moment_kernel, "moments", idx, [up, down, twice, moma, tables["mix"], lt],
                    [vec, tables["tab2"], tables["tab1"]], [(400, 128), wide],
-                   [layer, layer, layer, (16, 48, 128), (16, 40, 128), (2048, 128), (64, 2048)])
+                   [layer, layer, layer, (16, 48, 128), (16, 40, 128), (2048, 48), (64, 2048)])
     got = lax.all_gather(pay, "vel")
     (res,) = call(lambda i, g, fo, o: residual_kernel(i, g, fo, o, 8), "residual", idx,
                   [got, force], [], [(8, 120, 128)])
@@ -734,7 +756,7 @@
     win, own, part = (80, 24, 128), (80, 8, 128), (blocks, 8, 128)
     co = (40, 24, 128)
     r, m, ar, am, pe, gram = call(first_pass_kernel, "pass1", idx,
-                                  [lower, own_r, upper, to_lower, to_upper, lt], [],
+                                  [lower, own_r, upper, to_lower, to_upper, low, lt], [],
                                   [win] * 5 + [part], [co])
     r, m, ar, am, pe, acc, gram = call(functools.partial(next_pass_kernel, True), "pass2", idx,
                                        [summed(gram), r, m, ar, am, pe, lt], [],
@@ -742,9 +764,9 @@
     r, m, pe, acc, gram = call(third_pass_kernel, "pass3", idx,
                                [summed(gram), r, m, ar, am, pe, acc, lt], [],
                                [own] * 4 + [part], [win] * 5 + [co])
-    out, fields = call(last_kernel, "last", idx, [summed(gram), r, m, pe, acc, low, h2],
-                       [tables["ec"]], [(4, 8, 64, 128), (80, 128)], [(640, 128), (8, 2048)])
-    fields = fields.reshape(5, 4, 4, 8, 16).transpose(0, 1, 3, 4, 2).reshape(5, 4, 8, 64)
+    out, fields = call(last_kernel, "last", idx,
+                       [summed(gram), r, m, pe, acc, low, h2, tables["select"]], [tables["ec"]],
+                       [(4, 8, 64, 128), (5, 4, 8, 64)], [(640, 128), (8, 2048), (160, 512)])
     return out, fields
 
 

time: 138 us -> 129 us (0.935)
  blocking collectives: 53 us -> 63.4 us
  local copies, waits for them, and re-layouts: 12.6 us -> 2.68 us
  waiting for transfers between devices: 12.1 us -> 4.77 us
  starting transfers between devices: 19.1 us -> 16.3 us
    all_to_all x2 -> x3, blocking collectives: 24.3 us -> 34.7 us  [summed(): lax.all_to_all(gram, 'space', 0, 0, axis_index_groups=far, tiled=True)]
    unnamed x38 -> x24, local copies, waits for them, and re-layouts: 9.8 us -> 2.68 us
    all_to_all x1 -> x0, waiting for transfers between devices: 5.9 us -> none  [summed(): lax.all_to_all(gram, 'space', 0, 0, axis_index_groups=far, tiled=True)]
    all_to_all x1 -> x0, starting transfers between devices: 3.34 us -> none  [summed(): lax.all_to_all(gram, 'space', 0, 0, axis_index_groups=far, tiled=True)]
    ppermute x4, waiting for transfers between devices: 6.17 us -> 4.77 us  [shifted(): lax.ppermute(x, 'space', [(i, (i + by) % spaces) for i in range(spaces)])]
  transfers between devices with their start and end apart: 5 -> 4, of which waited for: 2 -> 2; matrix products, arithmetic and copies ran while one was open for 2% -> 0% of each run, Pallas kernels for 5% -> 6%
where the time goes in v2:
time: 129 us; the launch traced here: 128 us
  blocking collectives  63.4 us (49%)
  Pallas kernels  40 us (31%)
  starting transfers between devices  16.3 us (13%)
  waiting for transfers between devices  4.77 us (4%)
  local copies, waits for them, and re-layouts  2.68 us (2%)
    pallas_call x10, Pallas kernels, call(): pl.pallas_call(body, name=name, out_shape=[jax.ShapeDtypeStruct(s, jnp.fl...  40 us
    all_to_all x3, blocking collectives, summed(): lax.all_to_all(gram, 'space', 0, 0, axis_index_groups=far, tiled=True)  34.7 us
    all_to_all x1, blocking collectives, on_device(): lax.all_to_all(res, 'space', 0, 0, axis_index_groups=near, tiled=True)  20 us
    ppermute x4, starting transfers between devices, shifted(): lax.ppermute(x, 'space', [(i, (i + by) % spaces) for i in range(spaces)])  16.3 us
    all_gather x1, blocking collectives, on_device(): got = lax.all_gather(pay, 'vel')  8.72 us
    ppermute x4, waiting for transfers between devices, shifted(): lax.ppermute(x, 'space', [(i, (i + by) % spaces) for i in range(spaces)])  4.77 us
    unnamed x24, local copies, waits for them, and re-layouts  2.68 us
  transfers between devices with their start and end apart: 4, of which 2 were waited for; matrix products, arithmetic and copies ran while one was open for 0% of the time, Pallas kernels for 6%

profile of v2, /device:TPU:2, one launch (start us, length us, event | category | flops | bytes accessed | tf_op | source)
XLA Modules:
  0.0 128.1 jit_solution(17859485849527952615)
XLA Ops:
  0.6 0.0 copy-start.3
  0.7 0.1 pad_add_fusion.idx
  0.7 0.7 copy-done.3
  1.4 0.0 copy-start
  1.4 1.2 copy-done
  2.7 0.0 copy-start.11
  2.7 0.7 copy-done.11
  3.4 0.0 copy-start.1
  3.4 0.0 copy-start.4
  3.4 0.0 copy-start.7
  3.4 0.0 copy-start.8
  3.4 4.1 %rims.1 = (f32[544,128]{1,0:T(8,128)S(1)}, f32[544,128]{1,0:T(8,128)S(1)}) custom-call(s32[2]{0:T(128)S(1)} %pad_add_fusion.idx, f32[4,8,64,128]{3,2,1,0:T(8,128)S(1)} %copy-done, f32[4,24,128]{2,1,0:T(8,128)S(1)} %copy-done.3, f32[4,8,128]{2,1,0:T(8,128)S(1)} %copy-done.11), custom_call_target="tpu_custom_call" | custom-call | tf_op jit(solution)/shard_map/rims/pallas_call | solution.py:161
  7.4 2.0 %collective-permute-start = (f32[544,128]{1,0:T(8,128)S(1)}, f32[544,128]{1,0:T(8,128)S(1)}, u32[]{:S(2)}, u32[]{:S(2)}) collective-permute-start(f32[544,128]{1,0:T(8,128)S(1)} %get-tuple-element.32), channel_id=1, source_target_pairs={{0,1},{1,2},{2,3},{3,4},{4,5},{5,6},{6,7},{7,8},{8,9},{9,10},{10,1... | collective-permute-start | bytes 835592 | tf_op jit(solution)/shard_map/ppermute | solution.py:730
  9.4 0.0 copy-start.2
  9.4 0.0 copy-start.6
  9.4 0.0 copy-start.9
  9.4 8.1 %collective-permute-start.1 = (f32[544,128]{1,0:T(8,128)S(1)}, f32[544,128]{1,0:T(8,128)S(1)}, u32[]{:S(2)}, u32[]{:S(2)}) collective-permute-start(f32[544,128]{1,0:T(8,128)S(1)} %get-tuple-element.33), channel_id=1, source_target_pairs={{0,63},{1,0},{2,1},{3,2},{4,3},{5,4},{6,5},{7,6},{8,7},{9,8},{10,9... | collective-permute-start | bytes 835592 | tf_op jit(solution)/shard_map/ppermute | solution.py:730
  17.5 0.0 copy-done.1
  17.5 0.0 copy-done.4
  17.5 0.0 copy-done.7
  17.5 0.0 copy-done.8
  17.5 6.0 %local.1 = (f32[16,8,16,128]{3,2,1,0:T(8,128)S(1)}, f32[16,16,128]{2,1,0:T(8,128)S(1)}, f32[80,128]{1,0:T(8,128)S(1)}) custom-call(s32[2]{0:T(128)S(1)} %pad_add_fusion.idx, f32[4,8,64,128]{3,2,1,0:T(8,128)S(1)} %copy-done, f32[3,4,8,64]{3,2,1,0:T(8,128)S(1)} %copy-done.8, f32[64,512]{1,0:T(8,128)S(1)} %copy-done.1, f32[4,24,128]{2,1,0:T(8,128)S(1)} %copy-done.3, ...), custom_call_target="tpu_custom_call" | custom-call | tf_op jit(solution)/shard_map/local/pallas_call | solution.py:161
  23.6 0.5 collective-permute-done.refs_0_
  24.0 0.0 collective-permute-done.1.refs_1_
  24.0 0.0 copy-done.2
  24.0 0.0 copy-done.6
  24.0 0.0 copy-done.9
  24.0 7.3 %moments.1 = (f32[400,128]{1,0:T(8,128)S(1)}, f32[16,8,16,128]{3,2,1,0:T(8,128)S(1)}) custom-call(s32[2]{0:T(128)S(1)} %pad_add_fusion.idx, f32[544,128]{1,0:T(8,128)S(1)} %collective-permute-done.refs_0_, f32[544,128]{1,0:T(8,128)S(1)} %collective-permute-done.1.refs_1_, f32[16,8,16,128]{3,2,1,0:T(8,128)S(1)} %get-tuple-element.34.refs_2_, ...), custom_call_target="tpu_custom_call" | custom-call | tf_op jit(solution)/shard_map/moments/pallas_call | solution.py:161
  31.3 8.7 %all-gather = f32[1600,128]{1,0:T(8,128)S(1)} all-gather(f32[400,128]{1,0:T(8,128)S(1)} %get-tuple-element.36), channel_id=2, replica_groups=mesh['vel'=4,'space'=64] {'vel'}, dimensions={0}, use_global_device_ids=true | all-gather | bytes 1024000 | tf_op jit(solution)/shard_map/all_gather | solution.py:741
  40.1 0.6 residual.1
  40.6 20.0 %all_to_all.20 = f32[8,120,128]{2,1,0:T(8,128)S(1)} all-to-all(f32[8,120,128]{2,1,0:T(8,128)S(1)} %residual.1), channel_id=1, replica_groups={{0,1,2,3,4,5,6,7},{8,9,10,11,12,13,14,15},{16,17,18,19,20,21,22,23},{24..., dimensions={0} | all-to-all | bytes 983040 | tf_op jit(solution)/shard_map/all_to_all | solution.py:746
  60.6 0.0 copy-start.5
  60.6 0.8 pack.1
  61.4 0.1 collective-permute-start.2
  61.5 6.2 %collective-permute-start.3 = (f32[500,128]{1,0:T(8,128)S(1)}, f32[500,128]{1,0:T(8,128)S(1)}, u32[]{:S(2)}, u32[]{:S(2)}) collective-permute-start(f32[500,128]{1,0:T(8,128)S(1)} %get-tuple-element.40.refs_3_), channel_id=1, source_target_pairs={{0,56},{1,57},{2,58},{3,59},{4,60},{5,61},{6,62},{7,63},{8,0},{9,1... | collective-permute-start | bytes 768008 | tf_op jit(solution)/shard_map/ppermute | solution.py:730
  67.7 0.0 copy-done.5
  67.7 1.8 %feq.1 = (f32[16,8,16,128]{3,2,1,0:T(8,128)S(1)}, f32[80,128]{1,0:T(8,128)S(1)}) custom-call(s32[2]{0:T(128)S(1)} %pad_add_fusion.idx, f32[4,400,128]{2,1,0:T(8,128)S(1)} %bitcast.5, f32[16,8,16,128]{3,2,1,0:T(8,128)S(1)} %get-tuple-element.41.refs_1_, f32[40,128]{1,0:T(8,128)S(1)} %copy-done.2, f32[4,56,128]{2,1,0:T(8,128)S(1)} %copy-done.5), custom_call_target="tpu_custom_call" | custom-call | tf_op jit(solution)/shard_map/feq/pallas_call | solution.py:161
  69.5 4.3 %collective-permute-done.2.refs_0_ = f32[500,128]{1,0:T(8,128)S(1)} collective-permute-done((f32[500,128]{1,0:T(8,128)S(1)}, f32[500,128]{1,0:T(8,128)S(1)}, u32[]{:S(2)}, u32[]{:S(2)}) %collective-permute-start.2) | collective-permute-done | bytes 256032 | tf_op jit(solution)/shard_map/ppermute | solution.py:730
  73.8 0.0 collective-permute-done.3.refs_2_
  73.8 5.3 %pass1.1 = (f32[80,24,128]{2,1,0:T(8,128)S(1)}, f32[80,24,128]{2,1,0:T(8,128)S(1)}, f32[80,24,128]{2,1,0:T(8,128)S(1)}, f32[80,24,128]{2,1,0:T(8,128)S(1)}, f32[...) custom-call(s32[2]{0:T(128)S(1)} %pad_add_fusion.idx, f32[500,128]{1,0:T(8,128)S(1)} %collective-permute-done.2.refs_0_, ...), custom_call_target="tpu_custom_call" | custom-call | tf_op jit(solution)/shard_map/pass1/pallas_call | solution.py:161
  79.1 14.5 %all_to_all.21.refs_0_ = f32[8,8,128]{2,1,0:T(8,128)S(1)} all-to-all(f32[8,8,128]{2,1,0:T(8,128)S(1)} %get-tuple-element.43), channel_id=1, replica_groups={{0,8,16,24,32,40,48,56},{1,9,17,25,33,41,49,57},{2,10,18,26,34,42,50,58..., dimensions={0} | all-to-all | bytes 65536 | tf_op jit(solution)/shard_map/all_to_all | solution.py:754
  93.5 5.6 %pass2.1 = (f32[80,24,128]{2,1,0:T(8,128)S(1)}, f32[80,24,128]{2,1,0:T(8,128)S(1)}, f32[80,24,128]{2,1,0:T(8,128)S(1)}, f32[80,24,128]{2,1,0:T(8,128)S(1)}, f32[...) custom-call(s32[2]{0:T(128)S(1)} %pad_add_fusion.idx, ...), custom_call_target="tpu_custom_call" | custom-call | tf_op jit(solution)/shard_map/pass2/pallas_call | solution.py:161
  99.1 10.1 %all_to_all.22.refs_0_ = f32[8,8,128]{2,1,0:T(8,128)S(1)} all-to-all(f32[8,8,128]{2,1,0:T(8,128)S(1)} %get-tuple-element.49), channel_id=1, replica_groups={{0,8,16,24,32,40,48,56},{1,9,17,25,33,41,49,57},{2,10,18,26,34,42,50,58..., dimensions={0} | all-to-all | bytes 65536 | tf_op jit(solution)/shard_map/all_to_all | solution.py:754
  109.2 5.5 %pass3.1 = (f32[80,8,128]{2,1,0:T(8,128)S(1)}, f32[80,8,128]{2,1,0:T(8,128)S(1)}, f32[80,8,128]{2,1,0:T(8,128)S(1)}, f32[80,8,128]{2,1,0:T(8,128)S(1)}, f32[8,8,128]{2,1,0:T(8,128)S(1)}) custom-call(s32[2]{0:T(128)S(1)} %pad_add_fusion.idx, f32[8,8,128]{2,1,0:T(8,128)S(1)} %all_to_all.22.refs_0_, f32[80,24,128]{2,1,0:T(8,128)S(1)} %get-tuple-element.50.refs_1_, ...), custom_call_target="tpu_custom_call" | custom-call | tf_op jit(solution)/shard_map/pass3/pallas_call | solution.py:161
  114.8 0.0 copy-start.10
  114.8 10.1 %all_to_all.23.refs_0_ = f32[8,8,128]{2,1,0:T(8,128)S(1)} all-to-all(f32[8,8,128]{2,1,0:T(8,128)S(1)} %get-tuple-element.56), channel_id=1, replica_groups={{0,8,16,24,32,40,48,56},{1,9,17,25,33,41,49,57},{2,10,18,26,34,42,50,58..., dimensions={0} | all-to-all | bytes 65536 | tf_op jit(solution)/shard_map/all_to_all | solution.py:754
  124.9 0.0 copy-done.10
  124.9 3.1 %last.1 = (f32[4,8,64,128]{3,2,1,0:T(8,128)}, f32[5,4,8,64]{3,2,1,0:T(8,128)}) custom-call(s32[2]{0:T(128)S(1)} %pad_add_fusion.idx, f32[8,8,128]{2,1,0:T(8,128)S(1)} %all_to_all.23.refs_0_, f32[80,8,128]{2,1,0:T(8,128)S(1)} %get-tuple-element.57.refs_1_, f32[80,8,128]{2,1,0:T(8,128)S(1)} %get-tuple-element.58.refs_2_, ...), custom_call_target="tpu_custom_call" | custom-call | tf_op jit(solution)/shard_map/last/pallas_call | solution.py:161
Async XLA Ops:
  0.6 0.8 copy-start.3
  1.4 1.2 copy-start
  2.7 0.7 copy-start.11
  3.4 14.1 %copy-start.1 = (f32[64,512]{1,0:T(8,128)S(1)}, f32[64,512]{1,0:T(8,128)}, u32[]{:S(2)}) copy-start(f32[64,512]{1,0:T(8,128)} %constant.51.clone.refs_2_.refs_7_) | copy-start | bytes 393220
  3.4 14.1 %copy-start.4 = (f32[4,48,128]{2,1,0:T(8,128)S(1)}, f32[4,48,128]{2,1,0:T(8,128)}, u32[]{:S(2)}) copy-start(f32[4,48,128]{2,1,0:T(8,128)} %constant.44.clone.refs_5_.refs_8_) | copy-start | bytes 294916
  3.4 14.1 %copy-start.7 = (f32[4,48,128]{2,1,0:T(8,128)S(1)}, f32[4,48,128]{2,1,0:T(8,128)}, u32[]{:S(2)}) copy-start(f32[4,48,128]{2,1,0:T(8,128)} %constant.45.clone.refs_4_) | copy-start | bytes 294916
  3.4 14.1 %copy-start.8 = (f32[3,4,8,64]{3,2,1,0:T(8,128)S(1)}, f32[3,4,8,64]{3,2,1,0:T(8,128)}, u32[]{:S(2)}) copy-start(f32[3,4,8,64]{3,2,1,0:T(8,128)} %refs_1_.2) | copy-start | bytes 73732
  7.4 16.6 %collective-permute-start = (f32[544,128]{1,0:T(8,128)S(1)}, f32[544,128]{1,0:T(8,128)S(1)}, u32[]{:S(2)}, u32[]{:S(2)}) collective-permute-start(f32[544,128]{1,0:T(8,128)S(1)} %get-tuple-element.32), channel_id=1, source_target_pairs={{0,1},{1,2},{2,3},{3,4},{4,5},{5,6},{6,7},{7,8},{8,9},{9,10},{10,1... | collective-permute-start | bytes 835592 | tf_op jit(solution)/shard_map/ppermute | solution.py:730
  9.4 14.6 %copy-start.2 = (f32[40,128]{1,0:T(8,128)S(1)}, f32[40,128]{1,0:T(8,128)}, u32[]{:S(2)}) copy-start(f32[40,128]{1,0:T(8,128)} %constant.49.clone.refs_5_.refs_2_.refs_6_.refs_7_) | copy-start | bytes 61444
  9.4 14.6 %copy-start.6 = (f32[4,48,128]{2,1,0:T(8,128)S(1)}, f32[4,48,128]{2,1,0:T(8,128)}, u32[]{:S(2)}) copy-start(f32[4,48,128]{2,1,0:T(8,128)} %constant.43.clone.refs_7_) | copy-start | bytes 294916
  9.4 14.6 %copy-start.9 = (f32[40,64]{1,0:T(8,128)S(1)}, f32[40,64]{1,0:T(8,128)}, u32[]{:S(2)}) copy-start(f32[40,64]{1,0:T(8,128)} %constant.47.clone.refs_4_) | copy-start | bytes 30724
  9.4 14.6 %collective-permute-start.1 = (f32[544,128]{1,0:T(8,128)S(1)}, f32[544,128]{1,0:T(8,128)S(1)}, u32[]{:S(2)}, u32[]{:S(2)}) collective-permute-start(f32[544,128]{1,0:T(8,128)S(1)} %get-tuple-element.33), channel_id=1, source_target_pairs={{0,63},{1,0},{2,1},{3,2},{4,3},{5,4},{6,5},{7,6},{8,7},{9,8},{10,9... | collective-permute-start | bytes 835592 | tf_op jit(solution)/shard_map/ppermute | solution.py:730
  60.6 7.1 %copy-start.5 = (f32[4,56,128]{2,1,0:T(8,128)S(1)}, f32[4,56,128]{2,1,0:T(8,128)}, u32[]{:S(2)}) copy-start(f32[4,56,128]{2,1,0:T(8,128)} %constant.48.clone.refs_3_) | copy-start | bytes 344068
  61.4 12.3 %collective-permute-start.2 = (f32[500,128]{1,0:T(8,128)S(1)}, f32[500,128]{1,0:T(8,128)S(1)}, u32[]{:S(2)}, u32[]{:S(2)}) collective-permute-start(f32[500,128]{1,0:T(8,128)S(1)} %get-tuple-element.38.refs_4_), channel_id=1, source_target_pairs={{0,8},{1,9},{2,10},{3,11},{4,12},{5,13},{6,14},{7,15},{8,16},{9,17... | collective-permute-start | bytes 768008 | tf_op jit(solution)/shard_map/ppermute | solution.py:730
  61.5 12.3 %collective-permute-start.3 = (f32[500,128]{1,0:T(8,128)S(1)}, f32[500,128]{1,0:T(8,128)S(1)}, u32[]{:S(2)}, u32[]{:S(2)}) collective-permute-start(f32[500,128]{1,0:T(8,128)S(1)} %get-tuple-element.40.refs_3_), channel_id=1, source_target_pairs={{0,56},{1,57},{2,58},{3,59},{4,60},{5,61},{6,62},{7,63},{8,0},{9,1... | collective-permute-start | bytes 768008 | tf_op jit(solution)/shard_map/ppermute | solution.py:730
  114.8 10.2 %copy-start.10 = (f32[4,8,128]{2,1,0:T(8,128)S(1)}, f32[4,8,128]{2,1,0:T(8,128)}, u32[]{:S(2)}) copy-start(f32[4,8,128]{2,1,0:T(8,128)} %constant.50.clone.refs_8_) | copy-start | bytes 49156

commit v3 on v2

--- a/solution.py
+++ b/solution.py
@@ -91,7 +91,7 @@
         vec.append(-DT * 0.5 * x * np.where(ispos > 0, d4[3][jj], d4[0][jj]))
     while len(vec) < 24:
         vec.append(zero)
-    vec = per_rank(np.stack(vec))
+    vec = per_rank(np.concatenate([np.stack(vec), low]))
 
     def moment_rows(start, rows, height):
         out = np.zeros((height, 512))
@@ -101,7 +101,6 @@
     tab2 = moment_rows(0, rows32, 48)
     tab1 = moment_rows(40, low, 48)
     tab0 = moment_rows(32, low, 48)
-    tabr = moment_rows(0, low, 8)
     select = np.zeros((64, 512))
     for n in range(4):
         for la in range(128):
@@ -146,7 +145,7 @@
     while len(rows) < 40:
         rows.append(np.zeros(128))
     lanes = np.stack(rows).astype(np.float32)
-    return dict(vec=vec, tab2=tab2, tab1=tab1, tab0=tab0, tabr=tabr, mix=mix.astype(np.float32),
+    return dict(vec=vec, tab2=tab2, tab1=tab1, tab0=tab0, mix=mix.astype(np.float32),
                 final=final, lanes=lanes, ec=per_rank(ec), select=select.astype(np.float32))
 
 
@@ -198,7 +197,7 @@
                 v = v + vec[0, 6:7] * (pltpu.roll(q[0], 15, 0) - q[3])
             dst[zi, y] = v
         return 0
-    lax.fori_loop(0, 8, over_y, 0)
+    lax.fori_loop(0, 8, over_y, 0, unroll=True)
 
     def over_z(zi, _):
         q = [src[zi, y] for y in range(8)]
@@ -211,7 +210,7 @@
                 v = v + vec[0, 4:5] * (q[(y + 1) % 8] - q[y])
             dst[zi, y] = dst[zi, y] + v
         return 0
-    lax.fori_loop(0, 4, over_z, 0)
+    lax.fori_loop(0, 4, over_z, 0, unroll=True)
 
 
 def every_fourth(h, xi, y, zi):
@@ -220,7 +219,7 @@
     return h[xi, y, pl.ds(zi, 16, stride=4), :]
 
 
-def rim_kernel(idx, h, vec, tabr, up, down, q, t, ends, m):
+def rim_kernel(idx, h, vec, up, down, q, t, ends, m):
     pos = vec[0, 14:15] > 0.5
     for zi in range(4):
         def over_y(y, _):
@@ -234,7 +233,7 @@
                 v = v + vec[0, 15 + j:16 + j] * x[j]
             up[pl.ds(pl.multiple_of((zi * 8 + y) * 16, 16), 16)] = v
             return 0
-        lax.fori_loop(0, 8, over_y, 0)
+        lax.fori_loop(0, 8, over_y, 0, unroll=True)
     layer_yz(q, t, vec)
     right = lax.broadcasted_iota(jnp.int32, (16, 128), 1) >= 64
 
@@ -246,8 +245,8 @@
         up[at] = jnp.where(right, ql, tl)
         down[at] = jnp.where(right, tl, ql)
         return 0
-    lax.fori_loop(0, 32, pack, 0)
-    m[...] = project(ends[...].reshape(1024, 128), tabr[0])
+    lax.fori_loop(0, 32, pack, 0, unroll=8)
+    m[...] = project(ends[...].reshape(1024, 128), vec[0, 24:32])
     for n in range(8):
         zi, out = n % 4, (down, up)[n // 4]
         out[512 + 8 * zi:520 + 8 * zi] = m[128 * n:128 * n + 128].T
@@ -271,7 +270,7 @@
                     v = v + vec[0, 8:9] * own
                 dst[xi * 4 + zi, y] = v
         return 0
-    lax.fori_loop(0, 8, over_y, 0)
+    lax.fori_loop(0, 8, over_y, 0, unroll=2)
 
     def over_c(c, _):
         q = [src[c, y] for y in range(8)]
@@ -284,7 +283,7 @@
                 v = v + vec[0, 4:5] * (q[(y + 1) % 8] - q[y])
             dst[c, y] = dst[c, y] + v
         return 0
-    lax.fori_loop(0, 16, over_c, 0)
+    lax.fori_loop(0, 16, over_c, 0, unroll=4)
 
 
 def row_of_y():
@@ -307,7 +306,7 @@
         def over_y(y, _):
             first[c, y] = every_fourth(h, xi, y, zi)
             return 0
-        lax.fori_loop(0, 8, over_y, 0)
+        lax.fori_loop(0, 8, over_y, 0, unroll=True)
     local_update(first, once, vec)
     local_update(once, twice, vec)
 
@@ -371,7 +370,7 @@
         delta[zi, y] = vec[0, 9:10] * jnp.where(right, u, d)
         extra[zi, y] = vec[0, 9:10] * pltpu.roll(jnp.where(right, d, u), 64, 1)
         return 0
-    lax.fori_loop(0, 32, unpack, 0)
+    lax.fori_loop(0, 32, unpack, 0, unroll=8)
     layer_yz(delta, yz, vec)
     for xi in range(4):
         def over_n(n, _):
@@ -382,7 +381,7 @@
                 v = v + w * (yz[zi, y] + extra[zi, y])
             t2[xi * 4 + zi, y] = v
             return 0
-        lax.fori_loop(0, 32, over_n, 0)
+        lax.fori_loop(0, 32, over_n, 0, unroll=8)
 
     m[...] = project(t2[...].reshape(2048, 128), tab2[0])
     d = delta[...].reshape(512, 128)
@@ -460,27 +459,36 @@
     h2[...] = t2[...] + add.reshape(16, 8, 16, 128)
 
 
-def apply_operator(src, dst, lt):
-    def along_x(zi, _):
-        u = [src[16 + j * 4 + zi] for j in range(4)]
-        p = [src[j * 4 + zi] + src[64 + j * 4 + zi] for j in range(4)]
+def apply_operator(src, dst, lt, own=False):
+    rows = slice(8, 16) if own else slice(0, 24)
+
+    def before(k, add):
+        if own:
+            return src[k, 7:15] + src[k + add, 7:15] if add else src[k, 7:15]
+        return pltpu.roll(src[k] + src[k + add] if add else src[k], 1, 0)
+
+    def after(k, add):
+        if own:
+            return src[k, 9:17] + src[k + add, 9:17] if add else src[k, 9:17]
+        return pltpu.roll(src[k] + src[k + add] if add else src[k], 23, 0)
+
+    for zi in range(4):
+        u = [src[16 + j * 4 + zi, rows] for j in range(4)]
+        p = [src[j * 4 + zi, rows] + src[64 + j * 4 + zi, rows] for j in range(4)]
         for xi in range(4):
             du = combine(CENTRAL[xi], u)
             dp = combine(CENTRAL[xi], p)
             if xi == 0:
-                du = du - 1.5 * pltpu.roll(u[3], 1, 0)
-                dp = dp - 1.5 * pltpu.roll(p[3], 1, 0)
+                du = du - 1.5 * before(28 + zi, 0)
+                dp = dp - 1.5 * before(12 + zi, 64)
             if xi == 3:
-                du = du + 1.5 * pltpu.roll(u[0], 23, 0)
-                dp = dp + 1.5 * pltpu.roll(p[0], 23, 0)
+                du = du + 1.5 * after(16 + zi, 0)
+                dp = dp + 1.5 * after(zi, 64)
             dst[xi * 4 + zi] = du
             dst[16 + xi * 4 + zi] = 2.0 * u[xi] + dp
-        return 0
-    lax.fori_loop(0, 4, along_x, 0, unroll=True)
-
-    def along_z(xi, _):
-        u = [src[48 + xi * 4 + j] for j in range(4)]
-        p = [src[xi * 4 + j] + src[64 + xi * 4 + j] for j in range(4)]
+    for xi in range(4):
+        u = [src[48 + xi * 4 + j, rows] for j in range(4)]
+        p = [src[xi * 4 + j, rows] + src[64 + xi * 4 + j, rows] for j in range(4)]
         for zi in range(4):
             du = combine(CENTRAL[zi], u)
             dp = combine(CENTRAL[zi], p)
@@ -492,17 +500,15 @@
                 dp = dp + 1.5 * z_after(p[0], lt)
             dst[xi * 4 + zi] = dst[xi * 4 + zi] + du
             dst[48 + xi * 4 + zi] = 2.0 * u[zi] + dp
-        return 0
-    lax.fori_loop(0, 4, along_z, 0, unroll=True)
 
     def along_y(c, _):
-        rho, u, t = src[c], src[32 + c], src[64 + c]
+        rho, u, t = src[c, rows], src[32 + c, rows], src[64 + c, rows]
         div = dst[c] + central_y(u, lt)
         dst[32 + c] = 2.0 * u + central_y(rho + t, lt)
         dst[c] = 2.0 * rho + div
         dst[64 + c] = 2.0 * t + div
         return 0
-    lax.fori_loop(0, 16, along_y, 0, unroll=4)
+    lax.fori_loop(0, 16, along_y, 0, unroll=8)
 
 
 def two_level(r, pe, co, lt):
@@ -585,13 +591,14 @@
     return up * lt[23:24], low * lt[23:24]
 
 
-def fine_products(r, m, ar, am, lt):
+def fine_products(r, m, ar, am, lt, own):
+    rows = slice(0, 8) if own else slice(8, 16)
     total = [jnp.zeros((8, 128), jnp.float32) for _ in range(6)]
     for xi in range(4):
         for zi in range(4):
             def over_f(f, acc):
                 k = f * 16 + xi * 4 + zi
-                a, b, c, d = r[k, 8:16], m[k, 8:16], ar[k, 8:16], am[k, 8:16]
+                a, b, c, d = r[k, 8:16], m[k, 8:16], ar[k, rows], am[k, rows]
                 return (acc[0] + a * c, acc[1] + a * d + b * c, acc[2] + b * d,
                         acc[3] + c * c, acc[4] + c * d, acc[5] + d * d)
             zero = jnp.zeros((8, 128), jnp.float32)
@@ -601,12 +608,12 @@
     return [t * lt[22:23] for t in total]
 
 
-def pass_words(r, m, ar, am, pe, co, gram, lt, peers):
+def pass_words(r, m, ar, am, pe, co, gram, lt, peers, own=False):
     two_level(r, pe, co, lt)
     apply_operator(pe, m, lt)
-    apply_operator(r, ar, lt)
-    apply_operator(m, am, lt)
-    products = list(coarse_products(co, lt)) + fine_products(r, m, ar, am, lt)
+    apply_operator(r, ar, lt, own)
+    apply_operator(m, am, lt, own)
+    products = list(coarse_products(co, lt)) + fine_products(r, m, ar, am, lt, own)
     rows = jnp.concatenate([jnp.sum(p, axis=0, keepdims=True) for p in products], axis=0)
     for n in range(peers):
         gram[n] = rows
@@ -677,7 +684,7 @@
         r2[k] = q - a2 * (ar[k] - a1 * am[k])
         return 0
     lax.fori_loop(0, 80, over_k, 0, unroll=4)
-    pass_words(r2, m2, ar2, am2, pe2, co, gram, lt, gram.shape[0])
+    pass_words(r2, m2, ar2, am2, pe2, co, gram, lt, gram.shape[0], own=not first)
 
 
 def third_pass_kernel(idx, sums, r, m, ar, am, pe, acc, lt, ro, mo, po, acc2, gram,
@@ -729,7 +736,7 @@
     def shifted(x, by):
         return lax.ppermute(x, "space", [(i, (i + by) % spaces) for i in range(spaces)])
 
-    up, down = call(rim_kernel, "rims", idx, [distribution], [vec, tables["tabr"]],
+    up, down = call(rim_kernel, "rims", idx, [distribution], [vec],
                     [(544, 128)] * 2, [layer, layer, (8, 8, 16, 128), (1024, 8)])
     up, down = shifted(up, 1), shifted(down, -1)
     twice, moma, force = call(local_kernel, "local", idx, [distribution, forcing, tables["select"]],
@@ -763,7 +770,7 @@
                                        [win] * 5 + [own, part], [co])
     r, m, pe, acc, gram = call(third_pass_kernel, "pass3", idx,
                                [summed(gram), r, m, ar, am, pe, acc, lt], [],
-                               [own] * 4 + [part], [win] * 5 + [co])
+                               [own] * 4 + [part], [win, win, own, own, win, co])
     out, fields = call(last_kernel, "last", idx,
                        [summed(gram), r, m, pe, acc, low, h2, tables["select"]], [tables["ec"]],
                        [(4, 8, 64, 128), (5, 4, 8, 64)], [(640, 128), (8, 2048), (160, 512)])

time: 129 us -> 121 us (0.938)
  Pallas kernels: 40 us -> 31.8 us
    pallas_call x10, Pallas kernels: 40 us -> 31.8 us  [call(): pl.pallas_call(body, name=name, out_shape=[jax.ShapeDtypeStruct(s, jnp.fl...]
    unnamed x24 -> x22, local copies, waits for them, and re-layouts: 2.68 us -> 2.1 us
where the time goes in v3:
time: 121 us; the launch traced here: 120 us
  blocking collectives  63.4 us (52%)
  Pallas kernels  31.8 us (26%)
  starting transfers between devices  16.3 us (13%)
  waiting for transfers between devices  5.82 us (5%)
  local copies, waits for them, and re-layouts  2.1 us (2%)
    all_to_all x3, blocking collectives, summed(): lax.all_to_all(gram, 'space', 0, 0, axis_index_groups=far, tiled=True)  34.7 us
    pallas_call x10, Pallas kernels, call(): pl.pallas_call(body, name=name, out_shape=[jax.ShapeDtypeStruct(s, jnp.fl...  31.8 us
    all_to_all x1, blocking collectives, on_device(): lax.all_to_all(res, 'space', 0, 0, axis_index_groups=near, tiled=True)  20 us
    ppermute x4, starting transfers between devices, shifted(): lax.ppermute(x, 'space', [(i, (i + by) % spaces) for i in range(spaces)])  16.3 us
    all_gather x1, blocking collectives, on_device(): got = lax.all_gather(pay, 'vel')  8.72 us
    ppermute x4, waiting for transfers between devices, shifted(): lax.ppermute(x, 'space', [(i, (i + by) % spaces) for i in range(spaces)])  5.82 us
  transfers between devices with their start and end apart: 4, of which 2 were waited for; matrix products, arithmetic and copies ran while one was open for 0% of the time, Pallas kernels for 6%

profile of v3, /device:TPU:2, one launch (start us, length us, event | category | flops | bytes accessed | tf_op | source)
XLA Modules:
  0.0 120.3 jit_solution(12732050862936770011)
XLA Ops:
  0.6 0.1 pad_add_fusion.idx
  0.7 0.0 copy-start
  0.7 1.2 %copy-done = f32[4,8,64,128]{3,2,1,0:T(8,128)S(1)} copy-done((f32[4,8,64,128]{3,2,1,0:T(8,128)S(1)}, f32[4,8,64,128]{3,2,1,0:T(8,128)}, u32[]{:S(2)}) %copy-start) | copy-done | bytes 1048600
  1.9 0.0 copy-start.1
  1.9 0.8 copy-done.1
  2.8 0.0 copy-start.2
  2.8 0.0 copy-start.4
  2.8 0.0 copy-start.7
  2.8 0.0 copy-start.8
  2.8 1.9 %rims.1 = (f32[544,128]{1,0:T(8,128)S(1)}, f32[544,128]{1,0:T(8,128)S(1)}) custom-call(s32[2]{0:T(128)S(1)} %pad_add_fusion.idx, f32[4,8,64,128]{3,2,1,0:T(8,128)S(1)} %copy-done, f32[4,32,128]{2,1,0:T(8,128)S(1)} %copy-done.1), custom_call_target="tpu_custom_call" | custom-call | tf_op jit(solution)/shard_map/rims/pallas_call | solution.py:160
  4.7 2.0 %collective-permute-start = (f32[544,128]{1,0:T(8,128)S(1)}, f32[544,128]{1,0:T(8,128)S(1)}, u32[]{:S(2)}, u32[]{:S(2)}) collective-permute-start(f32[544,128]{1,0:T(8,128)S(1)} %get-tuple-element.32), channel_id=1, source_target_pairs={{0,1},{1,2},{2,3},{3,4},{4,5},{5,6},{6,7},{7,8},{8,9},{9,10},{10,1... | collective-permute-start | bytes 835592 | tf_op jit(solution)/shard_map/ppermute | solution.py:737
  6.7 0.0 copy-start.3
  6.7 0.0 copy-start.6
  6.7 0.0 copy-start.9
  6.7 8.1 %collective-permute-start.1 = (f32[544,128]{1,0:T(8,128)S(1)}, f32[544,128]{1,0:T(8,128)S(1)}, u32[]{:S(2)}, u32[]{:S(2)}) collective-permute-start(f32[544,128]{1,0:T(8,128)S(1)} %get-tuple-element.33), channel_id=1, source_target_pairs={{0,63},{1,0},{2,1},{3,2},{4,3},{5,4},{6,5},{7,6},{8,7},{9,8},{10,9... | collective-permute-start | bytes 835592 | tf_op jit(solution)/shard_map/ppermute | solution.py:737
  14.7 0.0 copy-done.2
  14.7 0.0 copy-done.4
  14.7 0.0 copy-done.7
  14.7 0.0 copy-done.8
  14.7 5.0 %local.1 = (f32[16,8,16,128]{3,2,1,0:T(8,128)S(1)}, f32[16,16,128]{2,1,0:T(8,128)S(1)}, f32[80,128]{1,0:T(8,128)S(1)}) custom-call(s32[2]{0:T(128)S(1)} %pad_add_fusion.idx, f32[4,8,64,128]{3,2,1,0:T(8,128)S(1)} %copy-done, f32[3,4,8,64]{3,2,1,0:T(8,128)S(1)} %copy-done.8, f32[64,512]{1,0:T(8,128)S(1)} %copy-done.2, f32[4,32,128]{2,1,0:T(8,128)S(1)} %copy-done.1, ...), custom_call_target="tpu_custom_call" | custom-call | tf_op jit(solution)/shard_map/local/pallas_call | solution.py:160
  19.7 1.5 %collective-permute-done.refs_0_ = f32[544,128]{1,0:T(8,128)S(1)} collective-permute-done((f32[544,128]{1,0:T(8,128)S(1)}, f32[544,128]{1,0:T(8,128)S(1)}, u32[]{:S(2)}, u32[]{:S(2)}) %collective-permute-start) | collective-permute-done | bytes 278560 | tf_op jit(solution)/shard_map/ppermute | solution.py:737
  21.3 0.0 collective-permute-done.1.refs_1_
  21.3 0.0 copy-done.3
  21.3 0.0 copy-done.6
  21.3 0.0 copy-done.9
  21.3 4.6 %moments.1 = (f32[400,128]{1,0:T(8,128)S(1)}, f32[16,8,16,128]{3,2,1,0:T(8,128)S(1)}) custom-call(s32[2]{0:T(128)S(1)} %pad_add_fusion.idx, f32[544,128]{1,0:T(8,128)S(1)} %collective-permute-done.refs_0_, f32[544,128]{1,0:T(8,128)S(1)} %collective-permute-done.1.refs_1_, f32[16,8,16,128]{3,2,1,0:T(8,128)S(1)} %get-tuple-element.34.refs_2_, ...), custom_call_target="tpu_custom_call" | custom-call | tf_op jit(solution)/shard_map/moments/pallas_call | solution.py:160
  25.9 8.7 %all-gather = f32[1600,128]{1,0:T(8,128)S(1)} all-gather(f32[400,128]{1,0:T(8,128)S(1)} %get-tuple-element.36), channel_id=2, replica_groups=mesh['vel'=4,'space'=64] {'vel'}, dimensions={0}, use_global_device_ids=true | all-gather | bytes 1024000 | tf_op jit(solution)/shard_map/all_gather | solution.py:748
  34.6 0.6 residual.1
  35.2 20.0 %all_to_all.20 = f32[8,120,128]{2,1,0:T(8,128)S(1)} all-to-all(f32[8,120,128]{2,1,0:T(8,128)S(1)} %residual.1), channel_id=1, replica_groups={{0,1,2,3,4,5,6,7},{8,9,10,11,12,13,14,15},{16,17,18,19,20,21,22,23},{24..., dimensions={0} | all-to-all | bytes 983040 | tf_op jit(solution)/shard_map/all_to_all | solution.py:753
  55.2 0.0 copy-start.5
  55.2 0.8 pack.1
  56.0 0.1 collective-permute-start.2
  56.1 6.2 %collective-permute-start.3 = (f32[500,128]{1,0:T(8,128)S(1)}, f32[500,128]{1,0:T(8,128)S(1)}, u32[]{:S(2)}, u32[]{:S(2)}) collective-permute-start(f32[500,128]{1,0:T(8,128)S(1)} %get-tuple-element.40.refs_3_), channel_id=1, source_target_pairs={{0,56},{1,57},{2,58},{3,59},{4,60},{5,61},{6,62},{7,63},{8,0},{9,1... | collective-permute-start | bytes 768008 | tf_op jit(solution)/shard_map/ppermute | solution.py:737
  62.2 0.0 copy-done.5
  62.2 1.8 %feq.1 = (f32[16,8,16,128]{3,2,1,0:T(8,128)S(1)}, f32[80,128]{1,0:T(8,128)S(1)}) custom-call(s32[2]{0:T(128)S(1)} %pad_add_fusion.idx, f32[4,400,128]{2,1,0:T(8,128)S(1)} %bitcast.5, f32[16,8,16,128]{3,2,1,0:T(8,128)S(1)} %get-tuple-element.41.refs_1_, f32[40,128]{1,0:T(8,128)S(1)} %copy-done.3, f32[4,56,128]{2,1,0:T(8,128)S(1)} %copy-done.5), custom_call_target="tpu_custom_call" | custom-call | tf_op jit(solution)/shard_map/feq/pallas_call | solution.py:160
  64.0 4.3 %collective-permute-done.2.refs_0_ = f32[500,128]{1,0:T(8,128)S(1)} collective-permute-done((f32[500,128]{1,0:T(8,128)S(1)}, f32[500,128]{1,0:T(8,128)S(1)}, u32[]{:S(2)}, u32[]{:S(2)}) %collective-permute-start.2) | collective-permute-done | bytes 256032 | tf_op jit(solution)/shard_map/ppermute | solution.py:737
  68.3 0.0 collective-permute-done.3.refs_2_
  68.3 4.9 %pass1.1 = (f32[80,24,128]{2,1,0:T(8,128)S(1)}, f32[80,24,128]{2,1,0:T(8,128)S(1)}, f32[80,24,128]{2,1,0:T(8,128)S(1)}, f32[80,24,128]{2,1,0:T(8,128)S(1)}, f32[...) custom-call(s32[2]{0:T(128)S(1)} %pad_add_fusion.idx, f32[500,128]{1,0:T(8,128)S(1)} %collective-permute-done.2.refs_0_, ...), custom_call_target="tpu_custom_call" | custom-call | tf_op jit(solution)/shard_map/pass1/pallas_call | solution.py:160
  73.2 14.5 %all_to_all.21.refs_0_ = f32[8,8,128]{2,1,0:T(8,128)S(1)} all-to-all(f32[8,8,128]{2,1,0:T(8,128)S(1)} %get-tuple-element.43), channel_id=1, replica_groups={{0,8,16,24,32,40,48,56},{1,9,17,25,33,41,49,57},{2,10,18,26,34,42,50,58..., dimensions={0} | all-to-all | bytes 65536 | tf_op jit(solution)/shard_map/all_to_all | solution.py:761
  87.7 5.1 %pass2.1 = (f32[80,24,128]{2,1,0:T(8,128)S(1)}, f32[80,24,128]{2,1,0:T(8,128)S(1)}, f32[80,24,128]{2,1,0:T(8,128)S(1)}, f32[80,24,128]{2,1,0:T(8,128)S(1)}, f32[...) custom-call(s32[2]{0:T(128)S(1)} %pad_add_fusion.idx, ...), custom_call_target="tpu_custom_call" | custom-call | tf_op jit(solution)/shard_map/pass2/pallas_call | solution.py:160
  92.8 10.1 %all_to_all.22.refs_0_ = f32[8,8,128]{2,1,0:T(8,128)S(1)} all-to-all(f32[8,8,128]{2,1,0:T(8,128)S(1)} %get-tuple-element.49), channel_id=1, replica_groups={{0,8,16,24,32,40,48,56},{1,9,17,25,33,41,49,57},{2,10,18,26,34,42,50,58..., dimensions={0} | all-to-all | bytes 65536 | tf_op jit(solution)/shard_map/all_to_all | solution.py:761
  102.9 4.0 %pass3.1 = (f32[80,8,128]{2,1,0:T(8,128)S(1)}, f32[80,8,128]{2,1,0:T(8,128)S(1)}, f32[80,8,128]{2,1,0:T(8,128)S(1)}, f32[80,8,128]{2,1,0:T(8,128)S(1)}, f32[8,8,128]{2,1,0:T(8,128)S(1)}) custom-call(s32[2]{0:T(128)S(1)} %pad_add_fusion.idx, f32[8,8,128]{2,1,0:T(8,128)S(1)} %all_to_all.22.refs_0_, f32[80,24,128]{2,1,0:T(8,128)S(1)} %get-tuple-element.50.refs_1_, ...), custom_call_target="tpu_custom_call" | custom-call | tf_op jit(solution)/shard_map/pass3/pallas_call | solution.py:160
  107.0 0.0 copy-start.10
  107.0 10.1 %all_to_all.23.refs_0_ = f32[8,8,128]{2,1,0:T(8,128)S(1)} all-to-all(f32[8,8,128]{2,1,0:T(8,128)S(1)} %get-tuple-element.56), channel_id=1, replica_groups={{0,8,16,24,32,40,48,56},{1,9,17,25,33,41,49,57},{2,10,18,26,34,42,50,58..., dimensions={0} | all-to-all | bytes 65536 | tf_op jit(solution)/shard_map/all_to_all | solution.py:761
  117.1 0.0 copy-done.10
  117.1 3.1 %last.1 = (f32[4,8,64,128]{3,2,1,0:T(8,128)}, f32[5,4,8,64]{3,2,1,0:T(8,128)}) custom-call(s32[2]{0:T(128)S(1)} %pad_add_fusion.idx, f32[8,8,128]{2,1,0:T(8,128)S(1)} %all_to_all.23.refs_0_, f32[80,8,128]{2,1,0:T(8,128)S(1)} %get-tuple-element.57.refs_1_, f32[80,8,128]{2,1,0:T(8,128)S(1)} %get-tuple-element.58.refs_2_, ...), custom_call_target="tpu_custom_call" | custom-call | tf_op jit(solution)/shard_map/last/pallas_call | solution.py:160
Async XLA Ops:
  0.7 1.2 %copy-start = (f32[4,8,64,128]{3,2,1,0:T(8,128)S(1)}, f32[4,8,64,128]{3,2,1,0:T(8,128)}, u32[]{:S(2)}) copy-start(f32[4,8,64,128]{3,2,1,0:T(8,128)} %refs_0_.3) | copy-start | bytes 3145732
  1.9 0.8 copy-start.1
  2.8 11.9 %copy-start.2 = (f32[64,512]{1,0:T(8,128)S(1)}, f32[64,512]{1,0:T(8,128)}, u32[]{:S(2)}) copy-start(f32[64,512]{1,0:T(8,128)} %constant.48.clone.refs_2_.refs_7_) | copy-start | bytes 393220
  2.8 11.9 %copy-start.4 = (f32[4,48,128]{2,1,0:T(8,128)S(1)}, f32[4,48,128]{2,1,0:T(8,128)}, u32[]{:S(2)}) copy-start(f32[4,48,128]{2,1,0:T(8,128)} %constant.42.clone.refs_5_.refs_8_) | copy-start | bytes 294916
  2.8 12.0 %copy-start.7 = (f32[4,48,128]{2,1,0:T(8,128)S(1)}, f32[4,48,128]{2,1,0:T(8,128)}, u32[]{:S(2)}) copy-start(f32[4,48,128]{2,1,0:T(8,128)} %constant.43.clone.refs_4_) | copy-start | bytes 294916
  2.8 12.0 %copy-start.8 = (f32[3,4,8,64]{3,2,1,0:T(8,128)S(1)}, f32[3,4,8,64]{3,2,1,0:T(8,128)}, u32[]{:S(2)}) copy-start(f32[3,4,8,64]{3,2,1,0:T(8,128)} %refs_1_.2) | copy-start | bytes 73732
  4.7 16.6 %collective-permute-start = (f32[544,128]{1,0:T(8,128)S(1)}, f32[544,128]{1,0:T(8,128)S(1)}, u32[]{:S(2)}, u32[]{:S(2)}) collective-permute-start(f32[544,128]{1,0:T(8,128)S(1)} %get-tuple-element.32), channel_id=1, source_target_pairs={{0,1},{1,2},{2,3},{3,4},{4,5},{5,6},{6,7},{7,8},{8,9},{9,10},{10,1... | collective-permute-start | bytes 835592 | tf_op jit(solution)/shard_map/ppermute | solution.py:737
  6.7 14.6 %copy-start.3 = (f32[40,128]{1,0:T(8,128)S(1)}, f32[40,128]{1,0:T(8,128)}, u32[]{:S(2)}) copy-start(f32[40,128]{1,0:T(8,128)} %constant.46.clone.refs_5_.refs_2_.refs_6_.refs_7_) | copy-start | bytes 61444
  6.7 14.6 %copy-start.6 = (f32[4,48,128]{2,1,0:T(8,128)S(1)}, f32[4,48,128]{2,1,0:T(8,128)}, u32[]{:S(2)}) copy-start(f32[4,48,128]{2,1,0:T(8,128)} %constant.41.clone.refs_7_) | copy-start | bytes 294916
  6.7 14.6 %copy-start.9 = (f32[40,64]{1,0:T(8,128)S(1)}, f32[40,64]{1,0:T(8,128)}, u32[]{:S(2)}) copy-start(f32[40,64]{1,0:T(8,128)} %constant.44.clone.refs_4_) | copy-start | bytes 30724
  6.7 14.6 %collective-permute-start.1 = (f32[544,128]{1,0:T(8,128)S(1)}, f32[544,128]{1,0:T(8,128)S(1)}, u32[]{:S(2)}, u32[]{:S(2)}) collective-permute-start(f32[544,128]{1,0:T(8,128)S(1)} %get-tuple-element.33), channel_id=1, source_target_pairs={{0,63},{1,0},{2,1},{3,2},{4,3},{5,4},{6,5},{7,6},{8,7},{9,8},{10,9... | collective-permute-start | bytes 835592 | tf_op jit(solution)/shard_map/ppermute | solution.py:737
  55.2 7.1 %copy-start.5 = (f32[4,56,128]{2,1,0:T(8,128)S(1)}, f32[4,56,128]{2,1,0:T(8,128)}, u32[]{:S(2)}) copy-start(f32[4,56,128]{2,1,0:T(8,128)} %constant.45.clone.refs_3_) | copy-start | bytes 344068
  56.0 12.3 %collective-permute-start.2 = (f32[500,128]{1,0:T(8,128)S(1)}, f32[500,128]{1,0:T(8,128)S(1)}, u32[]{:S(2)}, u32[]{:S(2)}) collective-permute-start(f32[500,128]{1,0:T(8,128)S(1)} %get-tuple-element.38.refs_4_), channel_id=1, source_target_pairs={{0,8},{1,9},{2,10},{3,11},{4,12},{5,13},{6,14},{7,15},{8,16},{9,17... | collective-permute-start | bytes 768008 | tf_op jit(solution)/shard_map/ppermute | solution.py:737
  56.1 12.3 %collective-permute-start.3 = (f32[500,128]{1,0:T(8,128)S(1)}, f32[500,128]{1,0:T(8,128)S(1)}, u32[]{:S(2)}, u32[]{:S(2)}) collective-permute-start(f32[500,128]{1,0:T(8,128)S(1)} %get-tuple-element.40.refs_3_), channel_id=1, source_target_pairs={{0,56},{1,57},{2,58},{3,59},{4,60},{5,61},{6,62},{7,63},{8,0},{9,1... | collective-permute-start | bytes 768008 | tf_op jit(solution)/shard_map/ppermute | solution.py:737
  107.0 10.2 %copy-start.10 = (f32[4,8,128]{2,1,0:T(8,128)S(1)}, f32[4,8,128]{2,1,0:T(8,128)}, u32[]{:S(2)}) copy-start(f32[4,8,128]{2,1,0:T(8,128)} %constant.47.clone.refs_8_) | copy-start | bytes 49156

commit v4 on v3

--- a/solution.py
+++ b/solution.py
@@ -299,7 +299,8 @@
         for c in range(16):
             n = 8 * (f * 4 + c // 4)
             v = spread[n:n + 8, 128 * (c % 4):128 * (c % 4) + 128] * here
-            force[5 * c + f + 1:5 * c + f + 2] = jnp.sum(v, axis=0, keepdims=True)
+            at = 5 * (c // 4) + f + 1
+            force[c % 4, at:at + 1] = jnp.sum(v, axis=0, keepdims=True)
     for c in range(16):
         xi, zi = c // 4, c % 4
 
@@ -358,7 +359,7 @@
 CENTRAL = [[0.0 if i == j else 0.5 * D4[i][j] for j in range(4)] for i in range(4)]
 
 
-def moment_kernel(idx, up, down, twice, moma, mix, lt, vec, tab2, tab1, pay, t2,
+def moment_kernel(idx, up, down, twice, moma, mix, lt, vec, tab2, tab1, pay, rest, t2,
                   delta, yz, extra, mom, full, m, stack):
     right = lax.broadcasted_iota(jnp.int32, (16, 128), 1) >= 64
     pos = vec[0, 14:15]
@@ -416,23 +417,23 @@
             r = r - 1.5 * z_before(full[xi * 4 + 3, 24:32], lt)
         if zi == 3:
             r = r + 1.5 * z_after(full[xi * 4, 24:32], lt)
-        pay[5 * c:5 * c + 5] = -r[0:5]
-        pay[120 + 5 * c:125 + 5 * c] = full[c, 0:5]
-        pay[200 + 5 * c:205 + 5 * c] = mom[c, 32:37]
-        pay[280 + 5 * c:285 + 5 * c] = full[c, 32:37]
+        pay[zi, 5 * xi:5 * xi + 5] = -r[0:5]
+        rest[5 * c:5 * c + 5] = full[c, 0:5]
+        rest[80 + 5 * c:85 + 5 * c] = mom[c, 32:37]
+        rest[160 + 5 * c:165 + 5 * c] = full[c, 32:37]
     for zi in range(4):
-        pay[80 + 5 * zi:85 + 5 * zi] = full[zi, 8:13]
-        pay[100 + 5 * zi:105 + 5 * zi] = full[12 + zi, 8:13]
-        pay[360 + 5 * zi:365 + 5 * zi] = up[512 + 8 * zi:517 + 8 * zi]
-        pay[380 + 5 * zi:385 + 5 * zi] = down[512 + 8 * zi:517 + 8 * zi]
-
-
-def residual_kernel(idx, got, force, out, peers):
-    t = got[0, 0:120] + got[1, 0:120] + got[2, 0:120] + got[3, 0:120]
-    v = t[0:80] + force[...]
-    for n in range(peers):
-        out[n, 0:80] = v
-        out[n, 80:120] = t[80:120]
+        pay[zi, 20:25] = full[zi, 8:13]
+        pay[zi, 25:30] = full[12 + zi, 8:13]
+        rest[240 + 5 * zi:245 + 5 * zi] = up[512 + 8 * zi:517 + 8 * zi]
+        rest[260 + 5 * zi:265 + 5 * zi] = down[512 + 8 * zi:517 + 8 * zi]
+
+
+def residual_kernel(idx, got, force, out):
+    t = got[0] + got[1] + got[2] + got[3]
+    v = t[0:20] + force[idx[0]]
+    for n in range(8):
+        out[n, 0:20] = v
+        out[n, 20:30] = t[20:30]
 
 
 def feq_kernel(idx, got, t2, lt, final, h2, low, s0, lo, hi, stack):
@@ -443,14 +444,14 @@
     lo[...] = jnp.zeros_like(lo)
     hi[...] = jnp.zeros_like(hi)
     for c in range(16):
-        s0[c, 0:5] = total(200 + 5 * c, 5)
+        s0[c, 0:5] = total(80 + 5 * c, 5)
     for zi in range(4):
-        lo[zi, 0:5] = total(360 + 5 * zi, 5)
-        hi[zi, 0:5] = total(380 + 5 * zi, 5)
-    low[...] = total(120, 80)
+        lo[zi, 0:5] = total(240 + 5 * zi, 5)
+        hi[zi, 0:5] = total(260 + 5 * zi, 5)
+    low[...] = total(0, 80)
     pad = jnp.zeros((3, 128), jnp.float32)
     for c in range(16):
-        z = jnp.concatenate([0.2 * total(280 + 5 * c, 5), pad], axis=0) + 0.16 * s0[c]
+        z = jnp.concatenate([0.2 * total(160 + 5 * c, 5), pad], axis=0) + 0.16 * s0[c]
         six = one_sided(lambda k: s0[k], lambda zi: lo[zi], lambda zi: hi[zi], c, lt)
         for n, v in enumerate([z] + six):
             stack[8 * n:8 * n + 8, 128 * c:128 * c + 128] = v
@@ -623,39 +624,44 @@
     first = lax.broadcasted_iota(jnp.int32, (8, 128), 0) == 0
     last = lax.broadcasted_iota(jnp.int32, (8, 128), 0) == 7
     for f in range(5):
-        for zi in range(4):
-            high = mine[pl.ds(100 + 5 * zi + f, 8, stride=120), :]
-            low = mine[pl.ds(80 + 5 * zi + f, 8, stride=120), :]
-            for xi in range(4):
-                c = xi * 4 + zi
-                k = f * 16 + c
-                v = mine[pl.ds(5 * c + f, 8, stride=120), :]
-                if xi == 0:
-                    v = v + 1.5 * jnp.where(first, 0.0, pltpu.roll(high, 1, 0))
-                if xi == 3:
-                    v = v - 1.5 * jnp.where(last, 0.0, pltpu.roll(low, 7, 0))
-                own[k] = v
-                to_upper[pl.ds(k, 6, stride=80), :] = v[2:8]
-                to_lower[pl.ds(k, 6, stride=80), :] = v[0:6]
-            to_upper[480 + f * 4 + zi:481 + f * 4 + zi] = high[7:8]
-            to_lower[480 + f * 4 + zi:481 + f * 4 + zi] = low[0:1]
-
-
-def first_pass_kernel(idx, lower, own, upper, edge_low, edge_high, after, lt, r, m, ar, am, pe, gram, co):
+        low = mine[pl.ds(20 + f, 8, stride=30), :]
+        high = mine[pl.ds(25 + f, 8, stride=30), :]
+        for xi in range(4):
+            k = f * 4 + xi
+            v = mine[pl.ds(5 * xi + f, 8, stride=30), :]
+            if xi == 0:
+                v = v + 1.5 * jnp.where(first, 0.0, pltpu.roll(high, 1, 0))
+            if xi == 3:
+                v = v - 1.5 * jnp.where(last, 0.0, pltpu.roll(low, 7, 0))
+            own[k] = v
+            to_upper[pl.ds(k, 6, stride=20), :] = v[2:8]
+            to_lower[pl.ds(k, 6, stride=20), :] = v[0:6]
+        to_upper[120 + f:121 + f] = high[7:8]
+        to_lower[120 + f:121 + f] = low[0:1]
+
+
+def window_kernel(idx, lower, own, upper, edge_low, edge_high, after, win):
     zero = jnp.zeros((2, 128), jnp.float32)
     for f in range(5):
-        for c in range(16):
-            xi, zi = c // 4, c % 4
-            k, e = f * 16 + c, f * 4 + zi
-            r[k, 0:8] = jnp.concatenate([zero, lower[pl.ds(k, 6, stride=80), :]], axis=0)
-            r[k, 8:16] = own[k]
-            r[k, 16:24] = jnp.concatenate([upper[pl.ds(k, 6, stride=80), :], zero], axis=0)
+        e = 120 + f
+        for xi in range(4):
+            k = f * 4 + xi
+            win[k, 0:8] = jnp.concatenate([zero, lower[pl.ds(k, 6, stride=20), :]], axis=0)
+            win[k, 8:16] = own[k]
+            win[k, 16:24] = jnp.concatenate([upper[pl.ds(k, 6, stride=20), :], zero], axis=0)
             if xi == 0:
-                r[k, 8:9] = r[k, 8:9] + 1.5 * lower[480 + e:481 + e]
-                r[k, 16:17] = r[k, 16:17] + 1.5 * edge_high[480 + e:481 + e]
+                win[k, 8:9] = win[k, 8:9] + 1.5 * lower[e:e + 1]
+                win[k, 16:17] = win[k, 16:17] + 1.5 * edge_high[e:e + 1]
             if xi == 3:
-                r[k, 15:16] = r[k, 15:16] - 1.5 * upper[480 + e:481 + e]
-                r[k, 7:8] = r[k, 7:8] - 1.5 * edge_low[480 + e:481 + e]
+                win[k, 15:16] = win[k, 15:16] - 1.5 * upper[e:e + 1]
+                win[k, 7:8] = win[k, 7:8] - 1.5 * edge_low[e:e + 1]
+
+
+def first_pass_kernel(idx, quarters, lt, r, m, ar, am, pe, gram, co):
+    for f in range(5):
+        for xi in range(4):
+            for zi in range(4):
+                r[f * 16 + xi * 4 + zi] = quarters[zi, f * 4 + xi]
     pass_words(r, m, ar, am, pe, co, gram, lt, gram.shape[0])
 
 
@@ -741,29 +747,32 @@
     up, down = shifted(up, 1), shifted(down, -1)
     twice, moma, force = call(local_kernel, "local", idx, [distribution, forcing, tables["select"]],
                               [vec, tables["tab0"], tables["tab1"]],
-                              [wide, (16, 16, 128), (80, 128)], [wide, wide, (2048, 48)])
-    pay, t2 = call(moment_kernel, "moments", idx, [up, down, twice, moma, tables["mix"], lt],
-                   [vec, tables["tab2"], tables["tab1"]], [(400, 128), wide],
-                   [layer, layer, layer, (16, 48, 128), (16, 40, 128), (2048, 48), (64, 2048)])
-    got = lax.all_gather(pay, "vel")
-    (res,) = call(lambda i, g, fo, o: residual_kernel(i, g, fo, o, 8), "residual", idx,
-                  [got, force], [], [(8, 120, 128)])
+                              [wide, (16, 16, 128), (4, 20, 128)], [wide, wide, (2048, 48)])
+    pay, rest, t2 = call(moment_kernel, "moments", idx, [up, down, twice, moma, tables["mix"], lt],
+                         [vec, tables["tab2"], tables["tab1"]], [(4, 30, 128), (280, 128), wide],
+                         [layer, layer, layer, (16, 48, 128), (16, 40, 128), (2048, 48), (64, 2048)])
+    got = lax.all_to_all(pay, "vel", 0, 0, tiled=True)
+    (res,) = call(residual_kernel, "residual", idx, [got, force], [], [(8, 30, 128)])
     near = [[a * 8 + b for b in range(8)] for a in range(blocks)]
     far = [[a * 8 + b for a in range(blocks)] for b in range(8)]
-    mine = lax.all_to_all(res, "space", 0, 0, axis_index_groups=near, tiled=True).reshape(960, 128)
+    mine = lax.all_to_all(res, "space", 0, 0, axis_index_groups=near, tiled=True).reshape(240, 128)
     own_r, to_upper, to_lower = call(pack_kernel, "pack", idx, [mine], [],
-                                     [(80, 8, 128), (500, 128), (500, 128)])
+                                     [(20, 8, 128), (125, 128), (125, 128)])
     lower, upper = shifted(to_upper, 8), shifted(to_lower, -8)
-    h2, low = call(feq_kernel, "feq", idx, [got, t2, lt], [tables["final"]],
+    rest, own_r = lax.optimization_barrier((rest, own_r))
+    others = lax.all_gather(rest, "vel")
+    h2, low = call(feq_kernel, "feq", idx, [others, t2, lt], [tables["final"]],
                    [wide, (80, 128)], [(16, 8, 128), (4, 8, 128), (4, 8, 128), (56, 2048)])
+    (quarter,) = call(window_kernel, "window", idx, [lower, own_r, upper, to_lower, to_upper, low], [],
+                      [(20, 24, 128)])
+    quarters = lax.all_gather(quarter, "vel")
 
     def summed(gram):
         return lax.all_to_all(gram, "space", 0, 0, axis_index_groups=far, tiled=True)
 
     win, own, part = (80, 24, 128), (80, 8, 128), (blocks, 8, 128)
     co = (40, 24, 128)
-    r, m, ar, am, pe, gram = call(first_pass_kernel, "pass1", idx,
-                                  [lower, own_r, upper, to_lower, to_upper, low, lt], [],
+    r, m, ar, am, pe, gram = call(first_pass_kernel, "pass1", idx, [quarters, lt], [],
                                   [win] * 5 + [part], [co])
     r, m, ar, am, pe, acc, gram = call(functools.partial(next_pass_kernel, True), "pass2", idx,
                                        [summed(gram), r, m, ar, am, pe, lt], [],

time: 121 us -> 120 us (level)
  waiting for transfers between devices: 5.82 us -> 1.53 us
  blocking collectives: 63.4 us -> 66.6 us
    all_gather x1 -> x2, blocking collectives: 8.72 us -> 18.6 us  [the longest x1 9.97 us: on_device(): quarters = lax.all_gather(quarter, 'vel')]
    all_to_all x1, blocking collectives: 20 us -> 11.5 us  [on_device(): lax.all_to_all(res, 'space', 0, 0, axis_index_groups=near, tiled=True)]
    all_to_all x0 -> x1, blocking collectives: none -> 6.06 us  [on_device(): got = lax.all_to_all(pay, 'vel', 0, 0, tiled=True)]
    all_to_all x3, blocking collectives: 34.7 us -> 30.4 us  [summed(): lax.all_to_all(gram, 'space', 0, 0, axis_index_groups=far, tiled=True)]
    ppermute x4, waiting for transfers between devices: 5.82 us -> 1.53 us  [shifted(): lax.ppermute(x, 'space', [(i, (i + by) % spaces) for i in range(spaces)])]
    pallas_call x10 -> x11, Pallas kernels: 31.8 us -> 31.9 us  [call(): pl.pallas_call(body, name=name, out_shape=[jax.ShapeDtypeStruct(s, jnp.fl...]
  transfers between devices with their start and end apart: 4 -> 4, of which waited for: 2 -> 1; matrix products, arithmetic and copies ran while one was open for 0% -> 0% of each run, Pallas kernels for 6% -> 6%
where the time goes in v4:
time: 120 us; the launch traced here: 119 us
  blocking collectives  66.6 us (55%)
  Pallas kernels  31.9 us (27%)
  starting transfers between devices  16.4 us (14%)
  local copies, waits for them, and re-layouts  2.11 us (2%)
  waiting for transfers between devices  1.53 us (1%)
    pallas_call x11, Pallas kernels, call(): pl.pallas_call(body, name=name, out_shape=[jax.ShapeDtypeStruct(s, jnp.fl...  31.9 us
    all_to_all x3, blocking collectives, summed(): lax.all_to_all(gram, 'space', 0, 0, axis_index_groups=far, tiled=True)  30.4 us
    ppermute x4, starting transfers between devices, shifted(): lax.ppermute(x, 'space', [(i, (i + by) % spaces) for i in range(spaces)])  16.4 us
    all_to_all x1, blocking collectives, on_device(): lax.all_to_all(res, 'space', 0, 0, axis_index_groups=near, tiled=True)  11.5 us
    all_gather x1, blocking collectives, on_device(): quarters = lax.all_gather(quarter, 'vel')  9.97 us
    all_gather x1, blocking collectives, on_device(): others = lax.all_gather(rest, 'vel')  8.64 us
    all_to_all x1, blocking collectives, on_device(): got = lax.all_to_all(pay, 'vel', 0, 0, tiled=True)  6.06 us
  transfers between devices with their start and end apart: 4, of which 1 were waited for; matrix products, arithmetic and copies ran while one was open for 0% of the time, Pallas kernels for 6%

profile of v4, /device:TPU:2, one launch (start us, length us, event | category | flops | bytes accessed | tf_op | source)
XLA Modules:
  0.0 119.3 jit_solution(9654639962390455512)
XLA Ops:
  0.6 0.1 pad_add_fusion.idx
  0.7 0.0 copy-start
  0.7 1.2 %copy-done = f32[4,8,64,128]{3,2,1,0:T(8,128)S(1)} copy-done((f32[4,8,64,128]{3,2,1,0:T(8,128)S(1)}, f32[4,8,64,128]{3,2,1,0:T(8,128)}, u32[]{:S(2)}) %copy-start) | copy-done | bytes 1048600
  1.9 0.0 copy-start.1
  1.9 0.8 copy-done.1
  2.8 0.0 copy-start.2
  2.8 0.0 copy-start.4
  2.8 0.0 copy-start.7
  2.8 0.0 copy-start.8
  2.8 1.9 %rims.1 = (f32[544,128]{1,0:T(8,128)S(1)}, f32[544,128]{1,0:T(8,128)S(1)}) custom-call(s32[2]{0:T(128)S(1)} %pad_add_fusion.idx, f32[4,8,64,128]{3,2,1,0:T(8,128)S(1)} %copy-done, f32[4,32,128]{2,1,0:T(8,128)S(1)} %copy-done.1), custom_call_target="tpu_custom_call" | custom-call | tf_op jit(solution)/shard_map/rims/pallas_call | solution.py:160
  4.7 2.0 %collective-permute-start = (f32[544,128]{1,0:T(8,128)S(1)}, f32[544,128]{1,0:T(8,128)S(1)}, u32[]{:S(2)}, u32[]{:S(2)}) collective-permute-start(f32[544,128]{1,0:T(8,128)S(1)} %get-tuple-element.35), channel_id=1, source_target_pairs={{0,1},{1,2},{2,3},{3,4},{4,5},{5,6},{6,7},{7,8},{8,9},{9,10},{10,1... | collective-permute-start | bytes 835592 | tf_op jit(solution)/shard_map/ppermute | solution.py:743
  6.7 0.0 copy-start.3
  6.7 0.0 copy-start.6
  6.7 0.0 copy-start.9
  6.7 8.1 %collective-permute-start.1 = (f32[544,128]{1,0:T(8,128)S(1)}, f32[544,128]{1,0:T(8,128)S(1)}, u32[]{:S(2)}, u32[]{:S(2)}) collective-permute-start(f32[544,128]{1,0:T(8,128)S(1)} %get-tuple-element.36), channel_id=1, source_target_pairs={{0,63},{1,0},{2,1},{3,2},{4,3},{5,4},{6,5},{7,6},{8,7},{9,8},{10,9... | collective-permute-start | bytes 835592 | tf_op jit(solution)/shard_map/ppermute | solution.py:743
  14.7 0.0 copy-done.2
  14.7 0.0 copy-done.4
  14.7 0.0 copy-done.7
  14.7 0.0 copy-done.8
  14.7 5.0 %local.1 = (f32[16,8,16,128]{3,2,1,0:T(8,128)S(1)}, f32[16,16,128]{2,1,0:T(8,128)S(1)}, f32[4,20,128]{2,1,0:T(8,128)S(1)}) custom-call(s32[2]{0:T(128)S(1)} %pad_add_fusion.idx, f32[4,8,64,128]{3,2,1,0:T(8,128)S(1)} %copy-done, f32[3,4,8,64]{3,2,1,0:T(8,128)S(1)} %copy-done.8, f32[64,512]{1,0:T(8,128)S(1)} %copy-done.2, f32[4,32,128]{2,1,0:T(8,128)S(1)} %copy-done.1, ...), custom_call_target="tpu_custom_call" | custom-call | tf_op jit(solution)/shard_map/local/pallas_call | solution.py:160
  19.7 1.5 %collective-permute-done.refs_0_ = f32[544,128]{1,0:T(8,128)S(1)} collective-permute-done((f32[544,128]{1,0:T(8,128)S(1)}, f32[544,128]{1,0:T(8,128)S(1)}, u32[]{:S(2)}, u32[]{:S(2)}) %collective-permute-start) | collective-permute-done | bytes 278560 | tf_op jit(solution)/shard_map/ppermute | solution.py:743
  21.3 0.0 collective-permute-done.1.refs_1_
  21.3 0.0 copy-done.3
  21.3 0.0 copy-done.6
  21.3 0.0 copy-done.9
  21.3 4.6 %moments.1 = (f32[4,30,128]{2,1,0:T(8,128)S(1)}, f32[280,128]{1,0:T(8,128)S(1)}, f32[16,8,16,128]{3,2,1,0:T(8,128)S(1)}) custom-call(s32[2]{0:T(128)S(1)} %pad_add_fusion.idx, f32[544,128]{1,0:T(8,128)S(1)} %collective-permute-done.refs_0_, f32[544,128]{1,0:T(8,128)S(1)} %collective-permute-done.1.refs_1_, f32[16,8,16,128]{3,2,1,0:T(8,128)S(1)} %get-tuple-element.37.refs_2_, ...), custom_call_target="tpu_custom_call" | custom-call | tf_op jit(solution)/shard_map/moments/pallas_call | solution.py:160
  25.9 6.1 %all_to_all.25.refs_0_ = f32[4,30,128]{2,1,0:T(8,128)S(1)} all-to-all(f32[4,30,128]{2,1,0:T(8,128)S(1)} %get-tuple-element.39), channel_id=1, replica_groups=mesh['vel'=4,'space'=64] {'vel'}, dimensions={0} | all-to-all | bytes 122880 | tf_op jit(solution)/shard_map/all_to_all | solution.py:754
  31.9 0.6 residual.1
  32.5 11.5 %all_to_all.26 = f32[8,30,128]{2,1,0:T(8,128)S(1)} all-to-all(f32[8,30,128]{2,1,0:T(8,128)S(1)} %residual.1), channel_id=1, replica_groups={{0,1,2,3,4,5,6,7},{8,9,10,11,12,13,14,15},{16,17,18,19,20,21,22,23},{24..., dimensions={0} | all-to-all | bytes 245760 | tf_op jit(solution)/shard_map/all_to_all | solution.py:758
  44.1 0.6 pack.1
  44.6 0.1 collective-permute-start.2
  44.8 6.2 %collective-permute-start.3 = (f32[125,128]{1,0:T(8,128)S(1)}, f32[125,128]{1,0:T(8,128)S(1)}, u32[]{:S(2)}, u32[]{:S(2)}) collective-permute-start(f32[125,128]{1,0:T(8,128)S(1)} %get-tuple-element.45.refs_3_), channel_id=1, source_target_pairs={{0,56},{1,57},{2,58},{3,59},{4,60},{5,61},{6,62},{7,63},{8,0},{9,1... | collective-permute-start | bytes 192008 | tf_op jit(solution)/shard_map/ppermute | solution.py:743
  51.0 8.6 %all-gather = f32[1120,128]{1,0:T(8,128)S(1)} all-gather(f32[280,128]{1,0:T(8,128)S(1)} %get-tuple-element.46), channel_id=2, replica_groups=mesh['vel'=4,'space'=64] {'vel'}, dimensions={0}, use_global_device_ids=true | all-gather | bytes 716800 | tf_op jit(solution)/shard_map/all_gather | solution.py:763
  59.6 0.0 copy-done.5
  59.6 1.8 %feq.1 = (f32[16,8,16,128]{3,2,1,0:T(8,128)S(1)}, f32[80,128]{1,0:T(8,128)S(1)}) custom-call(s32[2]{0:T(128)S(1)} %pad_add_fusion.idx, f32[4,280,128]{2,1,0:T(8,128)S(1)} %bitcast.5, f32[16,8,16,128]{3,2,1,0:T(8,128)S(1)} %get-tuple-element.47.refs_1_, f32[40,128]{1,0:T(8,128)S(1)} %copy-done.3, f32[4,56,128]{2,1,0:T(8,128)S(1)} %copy-done.5), custom_call_target="tpu_custom_call" | custom-call | tf_op jit(solution)/shard_map/feq/pallas_call | solution.py:160
  61.4 0.0 collective-permute-done.2.refs_0_
  61.4 0.0 collective-permute-done.3.refs_2_
  61.4 0.6 window.1
  62.0 10.0 %all-gather.1 = f32[80,24,128]{2,1,0:T(8,128)S(1)} all-gather(f32[20,24,128]{2,1,0:T(8,128)S(1)} %window.1), channel_id=3, replica_groups=mesh['vel'=4,'space'=64] {'vel'}, dimensions={0}, use_global_device_ids=true | all-gather | bytes 1228800 | tf_op jit(solution)/shard_map/all_gather | solution.py:768
  72.0 4.7 %pass1.1 = (f32[80,24,128]{2,1,0:T(8,128)S(1)}, f32[80,24,128]{2,1,0:T(8,128)S(1)}, f32[80,24,128]{2,1,0:T(8,128)S(1)}, f32[80,24,128]{2,1,0:T(8,128)S(1)}, f32[...) custom-call(s32[2]{0:T(128)S(1)} %pad_add_fusion.idx, f32[4,20,24,128]{3,2,1,0:T(8,128)S(1)} %bitcast.4, ...), custom_call_target="tpu_custom_call" | custom-call | tf_op jit(solution)/shard_map/pass1/pallas_call | solution.py:160
  76.6 10.1 %all_to_all.27.refs_0_ = f32[8,8,128]{2,1,0:T(8,128)S(1)} all-to-all(f32[8,8,128]{2,1,0:T(8,128)S(1)} %get-tuple-element.49), channel_id=1, replica_groups={{0,8,16,24,32,40,48,56},{1,9,17,25,33,41,49,57},{2,10,18,26,34,42,50,58..., dimensions={0} | all-to-all | bytes 65536 | tf_op jit(solution)/shard_map/all_to_all | solution.py:771
  86.8 5.1 %pass2.1 = (f32[80,24,128]{2,1,0:T(8,128)S(1)}, f32[80,24,128]{2,1,0:T(8,128)S(1)}, f32[80,24,128]{2,1,0:T(8,128)S(1)}, f32[80,24,128]{2,1,0:T(8,128)S(1)}, f32[...) custom-call(s32[2]{0:T(128)S(1)} %pad_add_fusion.idx, ...), custom_call_target="tpu_custom_call" | custom-call | tf_op jit(solution)/shard_map/pass2/pallas_call | solution.py:160
  91.9 10.1 %all_to_all.28.refs_0_ = f32[8,8,128]{2,1,0:T(8,128)S(1)} all-to-all(f32[8,8,128]{2,1,0:T(8,128)S(1)} %get-tuple-element.55), channel_id=1, replica_groups={{0,8,16,24,32,40,48,56},{1,9,17,25,33,41,49,57},{2,10,18,26,34,42,50,58..., dimensions={0} | all-to-all | bytes 65536 | tf_op jit(solution)/shard_map/all_to_all | solution.py:771
  102.0 4.0 %pass3.1 = (f32[80,8,128]{2,1,0:T(8,128)S(1)}, f32[80,8,128]{2,1,0:T(8,128)S(1)}, f32[80,8,128]{2,1,0:T(8,128)S(1)}, f32[80,8,128]{2,1,0:T(8,128)S(1)}, f32[8,8,128]{2,1,0:T(8,128)S(1)}) custom-call(s32[2]{0:T(128)S(1)} %pad_add_fusion.idx, f32[8,8,128]{2,1,0:T(8,128)S(1)} %all_to_all.28.refs_0_, f32[80,24,128]{2,1,0:T(8,128)S(1)} %get-tuple-element.56.refs_1_, ...), custom_call_target="tpu_custom_call" | custom-call | tf_op jit(solution)/shard_map/pass3/pallas_call | solution.py:160
  106.0 0.0 copy-start.10
  106.0 10.1 %all_to_all.29.refs_0_ = f32[8,8,128]{2,1,0:T(8,128)S(1)} all-to-all(f32[8,8,128]{2,1,0:T(8,128)S(1)} %get-tuple-element.62), channel_id=1, replica_groups={{0,8,16,24,32,40,48,56},{1,9,17,25,33,41,49,57},{2,10,18,26,34,42,50,58..., dimensions={0} | all-to-all | bytes 65536 | tf_op jit(solution)/shard_map/all_to_all | solution.py:771
  116.2 0.0 copy-done.10
  116.2 3.1 %last.1 = (f32[4,8,64,128]{3,2,1,0:T(8,128)}, f32[5,4,8,64]{3,2,1,0:T(8,128)}) custom-call(s32[2]{0:T(128)S(1)} %pad_add_fusion.idx, f32[8,8,128]{2,1,0:T(8,128)S(1)} %all_to_all.29.refs_0_, f32[80,8,128]{2,1,0:T(8,128)S(1)} %get-tuple-element.63.refs_1_, f32[80,8,128]{2,1,0:T(8,128)S(1)} %get-tuple-element.64.refs_2_, ...), custom_call_target="tpu_custom_call" | custom-call | tf_op jit(solution)/shard_map/last/pallas_call | solution.py:160
  (2 shorter events, 0.0 us)
Async XLA Ops:
  0.7 1.2 %copy-start = (f32[4,8,64,128]{3,2,1,0:T(8,128)S(1)}, f32[4,8,64,128]{3,2,1,0:T(8,128)}, u32[]{:S(2)}) copy-start(f32[4,8,64,128]{3,2,1,0:T(8,128)} %refs_0_.3) | copy-start | bytes 3145732
  1.9 0.8 copy-start.1
  2.8 11.9 %copy-start.2 = (f32[64,512]{1,0:T(8,128)S(1)}, f32[64,512]{1,0:T(8,128)}, u32[]{:S(2)}) copy-start(f32[64,512]{1,0:T(8,128)} %constant.48.clone.refs_2_.refs_7_) | copy-start | bytes 393220
  2.8 11.9 %copy-start.4 = (f32[4,48,128]{2,1,0:T(8,128)S(1)}, f32[4,48,128]{2,1,0:T(8,128)}, u32[]{:S(2)}) copy-start(f32[4,48,128]{2,1,0:T(8,128)} %constant.42.clone.refs_5_.refs_8_) | copy-start | bytes 294916
  2.8 12.0 %copy-start.7 = (f32[4,48,128]{2,1,0:T(8,128)S(1)}, f32[4,48,128]{2,1,0:T(8,128)}, u32[]{:S(2)}) copy-start(f32[4,48,128]{2,1,0:T(8,128)} %constant.43.clone.refs_4_) | copy-start | bytes 294916
  2.8 12.0 %copy-start.8 = (f32[3,4,8,64]{3,2,1,0:T(8,128)S(1)}, f32[3,4,8,64]{3,2,1,0:T(8,128)}, u32[]{:S(2)}) copy-start(f32[3,4,8,64]{3,2,1,0:T(8,128)} %refs_1_.3) | copy-start | bytes 73732
  4.7 16.6 %collective-permute-start = (f32[544,128]{1,0:T(8,128)S(1)}, f32[544,128]{1,0:T(8,128)S(1)}, u32[]{:S(2)}, u32[]{:S(2)}) collective-permute-start(f32[544,128]{1,0:T(8,128)S(1)} %get-tuple-element.35), channel_id=1, source_target_pairs={{0,1},{1,2},{2,3},{3,4},{4,5},{5,6},{6,7},{7,8},{8,9},{9,10},{10,1... | collective-permute-start | bytes 835592 | tf_op jit(solution)/shard_map/ppermute | solution.py:743
  6.7 14.6 %copy-start.3 = (f32[40,128]{1,0:T(8,128)S(1)}, f32[40,128]{1,0:T(8,128)}, u32[]{:S(2)}) copy-start(f32[40,128]{1,0:T(8,128)} %constant.46.clone.refs_5_.refs_2_.refs_1_.refs_6_.refs_7_) | copy-start | bytes 61444
  6.7 14.6 %copy-start.6 = (f32[4,48,128]{2,1,0:T(8,128)S(1)}, f32[4,48,128]{2,1,0:T(8,128)}, u32[]{:S(2)}) copy-start(f32[4,48,128]{2,1,0:T(8,128)} %constant.41.clone.refs_7_) | copy-start | bytes 294916
  6.7 14.6 %copy-start.9 = (f32[40,64]{1,0:T(8,128)S(1)}, f32[40,64]{1,0:T(8,128)}, u32[]{:S(2)}) copy-start(f32[40,64]{1,0:T(8,128)} %constant.44.clone.refs_4_) | copy-start | bytes 30724
  6.7 14.6 %collective-permute-start.1 = (f32[544,128]{1,0:T(8,128)S(1)}, f32[544,128]{1,0:T(8,128)S(1)}, u32[]{:S(2)}, u32[]{:S(2)}) collective-permute-start(f32[544,128]{1,0:T(8,128)S(1)} %get-tuple-element.36), channel_id=1, source_target_pairs={{0,63},{1,0},{2,1},{3,2},{4,3},{5,4},{6,5},{7,6},{8,7},{9,8},{10,9... | collective-permute-start | bytes 835592 | tf_op jit(solution)/shard_map/ppermute | solution.py:743
  44.6 16.7 %collective-permute-start.2 = (f32[125,128]{1,0:T(8,128)S(1)}, f32[125,128]{1,0:T(8,128)S(1)}, u32[]{:S(2)}, u32[]{:S(2)}) collective-permute-start(f32[125,128]{1,0:T(8,128)S(1)} %get-tuple-element.41.refs_4_), channel_id=1, source_target_pairs={{0,8},{1,9},{2,10},{3,11},{4,12},{5,13},{6,14},{7,15},{8,16},{9,17... | collective-permute-start | bytes 192008 | tf_op jit(solution)/shard_map/ppermute | solution.py:743
  44.8 14.9 %copy-start.5 = (f32[4,56,128]{2,1,0:T(8,128)S(1)}, f32[4,56,128]{2,1,0:T(8,128)}, u32[]{:S(2)}) copy-start(f32[4,56,128]{2,1,0:T(8,128)} %constant.45.clone.refs_3_) | copy-start | bytes 344068
  44.8 16.6 %collective-permute-start.3 = (f32[125,128]{1,0:T(8,128)S(1)}, f32[125,128]{1,0:T(8,128)S(1)}, u32[]{:S(2)}, u32[]{:S(2)}) collective-permute-start(f32[125,128]{1,0:T(8,128)S(1)} %get-tuple-element.45.refs_3_), channel_id=1, source_target_pairs={{0,56},{1,57},{2,58},{3,59},{4,60},{5,61},{6,62},{7,63},{8,0},{9,1... | collective-permute-start | bytes 192008 | tf_op jit(solution)/shard_map/ppermute | solution.py:743
  106.0 10.2 %copy-start.10 = (f32[4,8,128]{2,1,0:T(8,128)S(1)}, f32[4,8,128]{2,1,0:T(8,128)}, u32[]{:S(2)}) copy-start(f32[4,8,128]{2,1,0:T(8,128)} %constant.47.clone.refs_8_) | copy-start | bytes 49156

commit v5 on v4

--- a/solution.py
+++ b/solution.py
@@ -219,7 +219,32 @@
     return h[xi, y, pl.ds(zi, 16, stride=4), :]
 
 
-def rim_kernel(idx, h, vec, up, down, q, t, ends, m):
+def speed_rows(idx, vec):
+    j = lax.broadcasted_iota(jnp.int32, (1, 128), 1)
+    m = ((idx[0] * 64 + (j & 63)) * 5179 + 7) & 16383
+    s = j >> 6
+    x, y, z = [-4.0 + 0.25 * (n.astype(jnp.float32) + 0.5)
+               for n in (16 * s + (m >> 10), (m >> 5) & 31, m & 31)]
+    pos = s > 0
+    rows = {0: -DT * 0.5 * x, 1: -DT * 0.5 * y, 2: -DT * 0.5 * z,
+            3: -3 * DT * jnp.maximum(y, 0.0), 4: -3 * DT * jnp.minimum(y, 0.0),
+            5: -3 * DT * jnp.maximum(z, 0.0), 6: -3 * DT * jnp.minimum(z, 0.0),
+            14: pos.astype(jnp.float32)}
+    for n in range(4):
+        rows[15 + n] = -DT * 0.5 * x * jnp.where(pos, D4[3][n], D4[0][n])
+    rows[24], rows[25], rows[26], rows[27] = jnp.ones_like(x), x, y, z
+    rows[28] = 2.0 * (x * x + y * y + z * z) / 3.0 - 1.0
+    vec[...] = jnp.zeros_like(vec)
+    for n, v in rows.items():
+        vec[0, n:n + 1] = v
+
+
+def rim_kernel(idx, h, up, down, q, t, ends, m, vec):
+    speed_rows(idx, vec)
+    transport_rims(idx, h, vec, up, down, q, t, ends, m)
+
+
+def transport_rims(idx, h, vec, up, down, q, t, ends, m):
     pos = vec[0, 14:15] > 0.5
     for zi in range(4):
         def over_y(y, _):
@@ -359,7 +384,7 @@
 CENTRAL = [[0.0 if i == j else 0.5 * D4[i][j] for j in range(4)] for i in range(4)]
 
 
-def moment_kernel(idx, up, down, twice, moma, mix, lt, vec, tab2, tab1, pay, rest, t2,
+def moment_kernel(idx, up, down, twice, moma, mix, lt, vec, tab2, tab1, pay, t2,
                   delta, yz, extra, mom, full, m, stack):
     right = lax.broadcasted_iota(jnp.int32, (16, 128), 1) >= 64
     pos = vec[0, 14:15]
@@ -417,19 +442,22 @@
             r = r - 1.5 * z_before(full[xi * 4 + 3, 24:32], lt)
         if zi == 3:
             r = r + 1.5 * z_after(full[xi * 4, 24:32], lt)
-        pay[zi, 5 * xi:5 * xi + 5] = -r[0:5]
-        rest[5 * c:5 * c + 5] = full[c, 0:5]
-        rest[80 + 5 * c:85 + 5 * c] = mom[c, 32:37]
-        rest[160 + 5 * c:165 + 5 * c] = full[c, 32:37]
+        q = 32 * zi + 5 * xi
+        pay[q:q + 5] = -r[0:5]
+        pay[128 + 5 * c:133 + 5 * c] = full[c, 0:5]
+        pay[208 + 5 * c:213 + 5 * c] = mom[c, 32:37]
+        pay[288 + 5 * c:293 + 5 * c] = full[c, 32:37]
     for zi in range(4):
-        pay[zi, 20:25] = full[zi, 8:13]
-        pay[zi, 25:30] = full[12 + zi, 8:13]
-        rest[240 + 5 * zi:245 + 5 * zi] = up[512 + 8 * zi:517 + 8 * zi]
-        rest[260 + 5 * zi:265 + 5 * zi] = down[512 + 8 * zi:517 + 8 * zi]
+        pay[32 * zi + 20:32 * zi + 25] = full[zi, 8:13]
+        pay[32 * zi + 25:32 * zi + 30] = full[12 + zi, 8:13]
+        pay[32 * zi + 30:32 * zi + 32] = jnp.zeros((2, 128), jnp.float32)
+        pay[368 + 5 * zi:373 + 5 * zi] = up[512 + 8 * zi:517 + 8 * zi]
+        pay[388 + 5 * zi:393 + 5 * zi] = down[512 + 8 * zi:517 + 8 * zi]
 
 
 def residual_kernel(idx, got, force, out):
-    t = got[0] + got[1] + got[2] + got[3]
+    at = pl.ds(pl.multiple_of(32 * idx[0], 32), 32)
+    t = got[0, at] + got[1, at] + got[2, at] + got[3, at]
     v = t[0:20] + force[idx[0]]
     for n in range(8):
         out[n, 0:20] = v
@@ -444,14 +472,14 @@
     lo[...] = jnp.zeros_like(lo)
     hi[...] = jnp.zeros_like(hi)
     for c in range(16):
-        s0[c, 0:5] = total(80 + 5 * c, 5)
+        s0[c, 0:5] = total(208 + 5 * c, 5)
     for zi in range(4):
-        lo[zi, 0:5] = total(240 + 5 * zi, 5)
-        hi[zi, 0:5] = total(260 + 5 * zi, 5)
-    low[...] = total(0, 80)
+        lo[zi, 0:5] = total(368 + 5 * zi, 5)
+        hi[zi, 0:5] = total(388 + 5 * zi, 5)
+    low[...] = total(128, 80)
     pad = jnp.zeros((3, 128), jnp.float32)
     for c in range(16):
-        z = jnp.concatenate([0.2 * total(160 + 5 * c, 5), pad], axis=0) + 0.16 * s0[c]
+        z = jnp.concatenate([0.2 * total(288 + 5 * c, 5), pad], axis=0) + 0.16 * s0[c]
         six = one_sided(lambda k: s0[k], lambda zi: lo[zi], lambda zi: hi[zi], c, lt)
         for n, v in enumerate([z] + six):
             stack[8 * n:8 * n + 8, 128 * c:128 * c + 128] = v
@@ -641,27 +669,33 @@
 
 
 def window_kernel(idx, lower, own, upper, edge_low, edge_high, after, win):
-    zero = jnp.zeros((2, 128), jnp.float32)
     for f in range(5):
         e = 120 + f
         for xi in range(4):
             k = f * 4 + xi
-            win[k, 0:8] = jnp.concatenate([zero, lower[pl.ds(k, 6, stride=20), :]], axis=0)
-            win[k, 8:16] = own[k]
-            win[k, 16:24] = jnp.concatenate([upper[pl.ds(k, 6, stride=20), :], zero], axis=0)
+            at = 20 * k
+            low, mid, high = lower[pl.ds(k, 6, stride=20), :], own[k], upper[pl.ds(k, 6, stride=20), :]
+            win[at:at + 6] = low
+            win[at + 6:at + 14] = mid
+            win[at + 14:at + 20] = high
             if xi == 0:
-                win[k, 8:9] = win[k, 8:9] + 1.5 * lower[e:e + 1]
-                win[k, 16:17] = win[k, 16:17] + 1.5 * edge_high[e:e + 1]
+                win[at + 6:at + 7] = mid[0:1] + 1.5 * lower[e:e + 1]
+                win[at + 14:at + 15] = high[0:1] + 1.5 * edge_high[e:e + 1]
             if xi == 3:
-                win[k, 15:16] = win[k, 15:16] - 1.5 * upper[e:e + 1]
-                win[k, 7:8] = win[k, 7:8] - 1.5 * edge_low[e:e + 1]
+                win[at + 13:at + 14] = mid[7:8] - 1.5 * upper[e:e + 1]
+                win[at + 5:at + 6] = low[5:6] - 1.5 * edge_low[e:e + 1]
 
 
 def first_pass_kernel(idx, quarters, lt, r, m, ar, am, pe, gram, co):
+    zero = jnp.zeros((2, 128), jnp.float32)
     for f in range(5):
         for xi in range(4):
             for zi in range(4):
-                r[f * 16 + xi * 4 + zi] = quarters[zi, f * 4 + xi]
+                k = f * 16 + xi * 4 + zi
+                at = 20 * (f * 4 + xi)
+                r[k, 0:2] = zero
+                r[k, 2:22] = quarters[zi, at:at + 20]
+                r[k, 22:24] = zero
     pass_words(r, m, ar, am, pe, co, gram, lt, gram.shape[0])
 
 
@@ -742,16 +776,16 @@
     def shifted(x, by):
         return lax.ppermute(x, "space", [(i, (i + by) % spaces) for i in range(spaces)])
 
-    up, down = call(rim_kernel, "rims", idx, [distribution], [vec],
-                    [(544, 128)] * 2, [layer, layer, (8, 8, 16, 128), (1024, 8)])
+    up, down = call(rim_kernel, "rims", idx, [distribution], [],
+                    [(544, 128)] * 2, [layer, layer, (8, 8, 16, 128), (1024, 8), (1, 32, 128)])
     up, down = shifted(up, 1), shifted(down, -1)
     twice, moma, force = call(local_kernel, "local", idx, [distribution, forcing, tables["select"]],
                               [vec, tables["tab0"], tables["tab1"]],
                               [wide, (16, 16, 128), (4, 20, 128)], [wide, wide, (2048, 48)])
-    pay, rest, t2 = call(moment_kernel, "moments", idx, [up, down, twice, moma, tables["mix"], lt],
-                         [vec, tables["tab2"], tables["tab1"]], [(4, 30, 128), (280, 128), wide],
-                         [layer, layer, layer, (16, 48, 128), (16, 40, 128), (2048, 48), (64, 2048)])
-    got = lax.all_to_all(pay, "vel", 0, 0, tiled=True)
+    pay, t2 = call(moment_kernel, "moments", idx, [up, down, twice, moma, tables["mix"], lt],
+                   [vec, tables["tab2"], tables["tab1"]], [(408, 128), wide],
+                   [layer, layer, layer, (16, 48, 128), (16, 40, 128), (2048, 48), (64, 2048)])
+    got = lax.all_gather(pay, "vel")
     (res,) = call(residual_kernel, "residual", idx, [got, force], [], [(8, 30, 128)])
     near = [[a * 8 + b for b in range(8)] for a in range(blocks)]
     far = [[a * 8 + b for a in range(blocks)] for b in range(8)]
@@ -759,12 +793,10 @@
     own_r, to_upper, to_lower = call(pack_kernel, "pack", idx, [mine], [],
                                      [(20, 8, 128), (125, 128), (125, 128)])
     lower, upper = shifted(to_upper, 8), shifted(to_lower, -8)
-    rest, own_r = lax.optimization_barrier((rest, own_r))
-    others = lax.all_gather(rest, "vel")
-    h2, low = call(feq_kernel, "feq", idx, [others, t2, lt], [tables["final"]],
+    h2, low = call(feq_kernel, "feq", idx, [got, t2, lt], [tables["final"]],
                    [wide, (80, 128)], [(16, 8, 128), (4, 8, 128), (4, 8, 128), (56, 2048)])
     (quarter,) = call(window_kernel, "window", idx, [lower, own_r, upper, to_lower, to_upper, low], [],
-                      [(20, 24, 128)])
+                      [(400, 128)])
     quarters = lax.all_gather(quarter, "vel")
 
     def summed(gram):

time: 120 us -> 117 us (0.975)
  blocking collectives: 66.6 us -> 64.5 us
    all_to_all x1 -> x0, blocking collectives: 6.06 us -> none  [on_device(): got = lax.all_to_all(pay, 'vel', 0, 0, tiled=True)]
    all_to_all x3, blocking collectives: 30.4 us -> 34.2 us  [summed(): lax.all_to_all(gram, 'space', 0, 0, axis_index_groups=far, tiled=True)]
  transfers between devices with their start and end apart: 4 -> 4, of which waited for: 1 -> 2; matrix products, arithmetic and copies ran while one was open for 0% -> 0% of each run, Pallas kernels for 6% -> 6%
where the time goes in v5:
time: 117 us
  blocking collectives  64.5 us (55%)
  Pallas kernels  31.9 us (27%)
  starting transfers between devices  16.2 us (14%)
  waiting for transfers between devices  1.9 us (2%)
  local copies, waits for them, and re-layouts  1.28 us (1%)
    all_to_all x3, blocking collectives, summed(): lax.all_to_all(gram, 'space', 0, 0, axis_index_groups=far, tiled=True)  34.2 us
    pallas_call x11, Pallas kernels, call(): pl.pallas_call(body, name=name, out_shape=[jax.ShapeDtypeStruct(s, jnp.fl...  31.9 us
    ppermute x4, starting transfers between devices, shifted(): lax.ppermute(x, 'space', [(i, (i + by) % spaces) for i in range(spaces)])  16.2 us
    all_to_all x1, blocking collectives, on_device(): lax.all_to_all(res, 'space', 0, 0, axis_index_groups=near, tiled=True)  12.2 us
    all_gather x1, blocking collectives, on_device(): quarters = lax.all_gather(quarter, 'vel')  9.27 us
    all_gather x1, blocking collectives, on_device(): got = lax.all_gather(pay, 'vel')  8.81 us
  transfers between devices with their start and end apart: 4, of which 2 were waited for; matrix products, arithmetic and copies ran while one was open for 0% of the time, Pallas kernels for 6%

profile of v5, /device:TPU:2, one launch (start us, length us, event | category | flops | bytes accessed | tf_op | source)
XLA Modules:
  0.0 116.6 jit_solution(16910945605882783284)
XLA Ops:
  0.6 0.1 pad_add_fusion.idx
  0.7 0.0 copy-start
  0.7 1.2 %copy-done = f32[4,8,64,128]{3,2,1,0:T(8,128)S(1)} copy-done((f32[4,8,64,128]{3,2,1,0:T(8,128)S(1)}, f32[4,8,64,128]{3,2,1,0:T(8,128)}, u32[]{:S(2)}) %copy-start) | copy-done | bytes 1048600
  1.9 0.0 copy-start.1
  1.9 0.0 copy-start.3
  1.9 0.0 copy-start.4
  1.9 0.0 copy-start.7
  2.0 0.0 copy-start.8
  2.0 1.9 %rims.1 = (f32[544,128]{1,0:T(8,128)S(1)}, f32[544,128]{1,0:T(8,128)S(1)}) custom-call(s32[2]{0:T(128)S(1)} %pad_add_fusion.idx, f32[4,8,64,128]{3,2,1,0:T(8,128)S(1)} %copy-done), custom_call_target="tpu_custom_call" | custom-call | tf_op jit(solution)/shard_map/rims/pallas_call | solution.py:160
  3.9 2.0 %collective-permute-start = (f32[544,128]{1,0:T(8,128)S(1)}, f32[544,128]{1,0:T(8,128)S(1)}, u32[]{:S(2)}, u32[]{:S(2)}) collective-permute-start(f32[544,128]{1,0:T(8,128)S(1)} %get-tuple-element.32), channel_id=1, source_target_pairs={{0,1},{1,2},{2,3},{3,4},{4,5},{5,6},{6,7},{7,8},{8,9},{9,10},{10,1... | collective-permute-start | bytes 835592 | tf_op jit(solution)/shard_map/ppermute | solution.py:777
  5.8 0.0 copy-start.2
  5.8 0.0 copy-start.6
  5.8 0.0 copy-start.9
  5.8 8.1 %collective-permute-start.1 = (f32[544,128]{1,0:T(8,128)S(1)}, f32[544,128]{1,0:T(8,128)S(1)}, u32[]{:S(2)}, u32[]{:S(2)}) collective-permute-start(f32[544,128]{1,0:T(8,128)S(1)} %get-tuple-element.33), channel_id=1, source_target_pairs={{0,63},{1,0},{2,1},{3,2},{4,3},{5,4},{6,5},{7,6},{8,7},{9,8},{10,9... | collective-permute-start | bytes 835592 | tf_op jit(solution)/shard_map/ppermute | solution.py:777
  13.9 0.0 copy-done.1
  13.9 0.0 copy-done.3
  13.9 0.0 copy-done.4
  13.9 0.0 copy-done.7
  13.9 0.0 copy-done.8
  13.9 5.0 %local.1 = (f32[16,8,16,128]{3,2,1,0:T(8,128)S(1)}, f32[16,16,128]{2,1,0:T(8,128)S(1)}, f32[4,20,128]{2,1,0:T(8,128)S(1)}) custom-call(s32[2]{0:T(128)S(1)} %pad_add_fusion.idx, f32[4,8,64,128]{3,2,1,0:T(8,128)S(1)} %copy-done, f32[3,4,8,64]{3,2,1,0:T(8,128)S(1)} %copy-done.8, f32[64,512]{1,0:T(8,128)S(1)} %copy-done.1, f32[4,32,128]{2,1,0:T(8,128)S(1)} %copy-done.4, ...), custom_call_target="tpu_custom_call" | custom-call | tf_op jit(solution)/shard_map/local/pallas_call | solution.py:160
  18.9 1.5 %collective-permute-done.refs_0_ = f32[544,128]{1,0:T(8,128)S(1)} collective-permute-done((f32[544,128]{1,0:T(8,128)S(1)}, f32[544,128]{1,0:T(8,128)S(1)}, u32[]{:S(2)}, u32[]{:S(2)}) %collective-permute-start) | collective-permute-done | bytes 278560 | tf_op jit(solution)/shard_map/ppermute | solution.py:777
  20.4 0.0 collective-permute-done.1.refs_1_
  20.4 0.0 copy-done.2
  20.4 0.0 copy-done.6
  20.5 0.0 copy-done.9
  20.5 4.6 %moments.1 = (f32[408,128]{1,0:T(8,128)S(1)}, f32[16,8,16,128]{3,2,1,0:T(8,128)S(1)}) custom-call(s32[2]{0:T(128)S(1)} %pad_add_fusion.idx, f32[544,128]{1,0:T(8,128)S(1)} %collective-permute-done.refs_0_, f32[544,128]{1,0:T(8,128)S(1)} %collective-permute-done.1.refs_1_, f32[16,8,16,128]{3,2,1,0:T(8,128)S(1)} %get-tuple-element.34.refs_2_, ...), custom_call_target="tpu_custom_call" | custom-call | tf_op jit(solution)/shard_map/moments/pallas_call | solution.py:160
  25.1 8.8 %all-gather = f32[1632,128]{1,0:T(8,128)S(1)} all-gather(f32[408,128]{1,0:T(8,128)S(1)} %get-tuple-element.36), channel_id=2, replica_groups=mesh['vel'=4,'space'=64] {'vel'}, dimensions={0}, use_global_device_ids=true | all-gather | bytes 1044480 | tf_op jit(solution)/shard_map/all_gather | solution.py:788
  33.9 0.6 residual.1
  34.4 12.2 %all_to_all.20 = f32[8,30,128]{2,1,0:T(8,128)S(1)} all-to-all(f32[8,30,128]{2,1,0:T(8,128)S(1)} %residual.1), channel_id=1, replica_groups={{0,1,2,3,4,5,6,7},{8,9,10,11,12,13,14,15},{16,17,18,19,20,21,22,23},{24..., dimensions={0} | all-to-all | bytes 245760 | tf_op jit(solution)/shard_map/all_to_all | solution.py:792
  46.7 0.0 copy-start.5
  46.7 0.6 pack.1
  47.3 0.1 collective-permute-start.2
  47.4 6.0 %collective-permute-start.3 = (f32[125,128]{1,0:T(8,128)S(1)}, f32[125,128]{1,0:T(8,128)S(1)}, u32[]{:S(2)}, u32[]{:S(2)}) collective-permute-start(f32[125,128]{1,0:T(8,128)S(1)} %get-tuple-element.40.refs_3_), channel_id=1, source_target_pairs={{0,56},{1,57},{2,58},{3,59},{4,60},{5,61},{6,62},{7,63},{8,0},{9,1... | collective-permute-start | bytes 192008 | tf_op jit(solution)/shard_map/ppermute | solution.py:777
  53.4 0.0 copy-done.5
  53.4 1.8 %feq.1 = (f32[16,8,16,128]{3,2,1,0:T(8,128)S(1)}, f32[80,128]{1,0:T(8,128)S(1)}) custom-call(s32[2]{0:T(128)S(1)} %pad_add_fusion.idx, f32[4,408,128]{2,1,0:T(8,128)S(1)} %bitcast.5, f32[16,8,16,128]{3,2,1,0:T(8,128)S(1)} %get-tuple-element.41.refs_1_, f32[40,128]{1,0:T(8,128)S(1)} %copy-done.2, f32[4,56,128]{2,1,0:T(8,128)S(1)} %copy-done.5), custom_call_target="tpu_custom_call" | custom-call | tf_op jit(solution)/shard_map/feq/pallas_call | solution.py:160
  55.2 0.4 collective-permute-done.2.refs_0_
  55.6 0.0 collective-permute-done.3.refs_2_
  55.6 0.6 window.1
  56.1 9.3 %all-gather.1 = f32[1600,128]{1,0:T(8,128)S(1)} all-gather(f32[400,128]{1,0:T(8,128)S(1)} %window.1), channel_id=3, replica_groups=mesh['vel'=4,'space'=64] {'vel'}, dimensions={0}, use_global_device_ids=true | all-gather | bytes 1024000 | tf_op jit(solution)/shard_map/all_gather | solution.py:800
  65.4 4.7 %pass1.1 = (f32[80,24,128]{2,1,0:T(8,128)S(1)}, f32[80,24,128]{2,1,0:T(8,128)S(1)}, f32[80,24,128]{2,1,0:T(8,128)S(1)}, f32[80,24,128]{2,1,0:T(8,128)S(1)}, f32[...) custom-call(s32[2]{0:T(128)S(1)} %pad_add_fusion.idx, f32[4,400,128]{2,1,0:T(8,128)S(1)} %bitcast.6, f32[40,128]{1,0:T(8,128)S(1)} %copy-done.2), custom_call_target="tpu_custom_call" | custom-call | tf_op jit(solution)/shard_map/pass1/pallas_call | solution.py:160
  70.1 14.0 %all_to_all.21.refs_0_ = f32[8,8,128]{2,1,0:T(8,128)S(1)} all-to-all(f32[8,8,128]{2,1,0:T(8,128)S(1)} %get-tuple-element.43), channel_id=1, replica_groups={{0,8,16,24,32,40,48,56},{1,9,17,25,33,41,49,57},{2,10,18,26,34,42,50,58..., dimensions={0} | all-to-all | bytes 65536 | tf_op jit(solution)/shard_map/all_to_all | solution.py:803
  84.1 5.1 %pass2.1 = (f32[80,24,128]{2,1,0:T(8,128)S(1)}, f32[80,24,128]{2,1,0:T(8,128)S(1)}, f32[80,24,128]{2,1,0:T(8,128)S(1)}, f32[80,24,128]{2,1,0:T(8,128)S(1)}, f32[...) custom-call(s32[2]{0:T(128)S(1)} %pad_add_fusion.idx, ...), custom_call_target="tpu_custom_call" | custom-call | tf_op jit(solution)/shard_map/pass2/pallas_call | solution.py:160
  89.2 10.1 %all_to_all.22.refs_0_ = f32[8,8,128]{2,1,0:T(8,128)S(1)} all-to-all(f32[8,8,128]{2,1,0:T(8,128)S(1)} %get-tuple-element.49), channel_id=1, replica_groups={{0,8,16,24,32,40,48,56},{1,9,17,25,33,41,49,57},{2,10,18,26,34,42,50,58..., dimensions={0} | all-to-all | bytes 65536 | tf_op jit(solution)/shard_map/all_to_all | solution.py:803
  99.3 4.0 %pass3.1 = (f32[80,8,128]{2,1,0:T(8,128)S(1)}, f32[80,8,128]{2,1,0:T(8,128)S(1)}, f32[80,8,128]{2,1,0:T(8,128)S(1)}, f32[80,8,128]{2,1,0:T(8,128)S(1)}, f32[8,8,128]{2,1,0:T(8,128)S(1)}) custom-call(s32[2]{0:T(128)S(1)} %pad_add_fusion.idx, f32[8,8,128]{2,1,0:T(8,128)S(1)} %all_to_all.22.refs_0_, f32[80,24,128]{2,1,0:T(8,128)S(1)} %get-tuple-element.50.refs_1_, ...), custom_call_target="tpu_custom_call" | custom-call | tf_op jit(solution)/shard_map/pass3/pallas_call | solution.py:160
  103.3 0.0 copy-start.10
  103.3 10.1 %all_to_all.23.refs_0_ = f32[8,8,128]{2,1,0:T(8,128)S(1)} all-to-all(f32[8,8,128]{2,1,0:T(8,128)S(1)} %get-tuple-element.56), channel_id=1, replica_groups={{0,8,16,24,32,40,48,56},{1,9,17,25,33,41,49,57},{2,10,18,26,34,42,50,58..., dimensions={0} | all-to-all | bytes 65536 | tf_op jit(solution)/shard_map/all_to_all | solution.py:803
  113.5 0.0 copy-done.10
  113.5 3.1 %last.1 = (f32[4,8,64,128]{3,2,1,0:T(8,128)}, f32[5,4,8,64]{3,2,1,0:T(8,128)}) custom-call(s32[2]{0:T(128)S(1)} %pad_add_fusion.idx, f32[8,8,128]{2,1,0:T(8,128)S(1)} %all_to_all.23.refs_0_, f32[80,8,128]{2,1,0:T(8,128)S(1)} %get-tuple-element.57.refs_1_, f32[80,8,128]{2,1,0:T(8,128)S(1)} %get-tuple-element.58.refs_2_, ...), custom_call_target="tpu_custom_call" | custom-call | tf_op jit(solution)/shard_map/last/pallas_call | solution.py:160
  (1 shorter events, 0.0 us)
Async XLA Ops:
  0.7 1.2 %copy-start = (f32[4,8,64,128]{3,2,1,0:T(8,128)S(1)}, f32[4,8,64,128]{3,2,1,0:T(8,128)}, u32[]{:S(2)}) copy-start(f32[4,8,64,128]{3,2,1,0:T(8,128)} %refs_0_.3) | copy-start | bytes 3145732
  1.9 12.0 %copy-start.1 = (f32[64,512]{1,0:T(8,128)S(1)}, f32[64,512]{1,0:T(8,128)}, u32[]{:S(2)}) copy-start(f32[64,512]{1,0:T(8,128)} %constant.48.clone.refs_2_.refs_7_) | copy-start | bytes 393220
  1.9 12.0 %copy-start.3 = (f32[4,48,128]{2,1,0:T(8,128)S(1)}, f32[4,48,128]{2,1,0:T(8,128)}, u32[]{:S(2)}) copy-start(f32[4,48,128]{2,1,0:T(8,128)} %constant.42.clone.refs_5_.refs_8_) | copy-start | bytes 294916
  1.9 12.0 %copy-start.4 = (f32[4,32,128]{2,1,0:T(8,128)S(1)}, f32[4,32,128]{2,1,0:T(8,128)}, u32[]{:S(2)}) copy-start(f32[4,32,128]{2,1,0:T(8,128)} %constant.40.clone.refs_3_.refs_6_) | copy-start | bytes 196612
  1.9 12.0 %copy-start.7 = (f32[4,48,128]{2,1,0:T(8,128)S(1)}, f32[4,48,128]{2,1,0:T(8,128)}, u32[]{:S(2)}) copy-start(f32[4,48,128]{2,1,0:T(8,128)} %constant.43.clone.refs_4_) | copy-start | bytes 294916
  2.0 12.0 %copy-start.8 = (f32[3,4,8,64]{3,2,1,0:T(8,128)S(1)}, f32[3,4,8,64]{3,2,1,0:T(8,128)}, u32[]{:S(2)}) copy-start(f32[3,4,8,64]{3,2,1,0:T(8,128)} %refs_1_.2) | copy-start | bytes 73732
  3.9 16.6 %collective-permute-start = (f32[544,128]{1,0:T(8,128)S(1)}, f32[544,128]{1,0:T(8,128)S(1)}, u32[]{:S(2)}, u32[]{:S(2)}) collective-permute-start(f32[544,128]{1,0:T(8,128)S(1)} %get-tuple-element.32), channel_id=1, source_target_pairs={{0,1},{1,2},{2,3},{3,4},{4,5},{5,6},{6,7},{7,8},{8,9},{9,10},{10,1... | collective-permute-start | bytes 835592 | tf_op jit(solution)/shard_map/ppermute | solution.py:777
  5.8 14.6 %copy-start.2 = (f32[40,128]{1,0:T(8,128)S(1)}, f32[40,128]{1,0:T(8,128)}, u32[]{:S(2)}) copy-start(f32[40,128]{1,0:T(8,128)} %constant.46.clone.refs_5_.refs_2_.refs_1_.refs_6_.refs_7_) | copy-start | bytes 61444
  5.8 14.6 %copy-start.6 = (f32[4,48,128]{2,1,0:T(8,128)S(1)}, f32[4,48,128]{2,1,0:T(8,128)}, u32[]{:S(2)}) copy-start(f32[4,48,128]{2,1,0:T(8,128)} %constant.41.clone.refs_7_) | copy-start | bytes 294916
  5.8 14.6 %copy-start.9 = (f32[40,64]{1,0:T(8,128)S(1)}, f32[40,64]{1,0:T(8,128)}, u32[]{:S(2)}) copy-start(f32[40,64]{1,0:T(8,128)} %constant.44.clone.refs_4_) | copy-start | bytes 30724
  5.8 14.6 %collective-permute-start.1 = (f32[544,128]{1,0:T(8,128)S(1)}, f32[544,128]{1,0:T(8,128)S(1)}, u32[]{:S(2)}, u32[]{:S(2)}) collective-permute-start(f32[544,128]{1,0:T(8,128)S(1)} %get-tuple-element.33), channel_id=1, source_target_pairs={{0,63},{1,0},{2,1},{3,2},{4,3},{5,4},{6,5},{7,6},{8,7},{9,8},{10,9... | collective-permute-start | bytes 835592 | tf_op jit(solution)/shard_map/ppermute | solution.py:777
  46.7 6.7 %copy-start.5 = (f32[4,56,128]{2,1,0:T(8,128)S(1)}, f32[4,56,128]{2,1,0:T(8,128)}, u32[]{:S(2)}) copy-start(f32[4,56,128]{2,1,0:T(8,128)} %constant.45.clone.refs_3_) | copy-start | bytes 344068
  47.3 8.3 %collective-permute-start.2 = (f32[125,128]{1,0:T(8,128)S(1)}, f32[125,128]{1,0:T(8,128)S(1)}, u32[]{:S(2)}, u32[]{:S(2)}) collective-permute-start(f32[125,128]{1,0:T(8,128)S(1)} %get-tuple-element.38.refs_4_), channel_id=1, source_target_pairs={{0,8},{1,9},{2,10},{3,11},{4,12},{5,13},{6,14},{7,15},{8,16},{9,17... | collective-permute-start | bytes 192008 | tf_op jit(solution)/shard_map/ppermute | solution.py:777
  47.4 8.2 %collective-permute-start.3 = (f32[125,128]{1,0:T(8,128)S(1)}, f32[125,128]{1,0:T(8,128)S(1)}, u32[]{:S(2)}, u32[]{:S(2)}) collective-permute-start(f32[125,128]{1,0:T(8,128)S(1)} %get-tuple-element.40.refs_3_), channel_id=1, source_target_pairs={{0,56},{1,57},{2,58},{3,59},{4,60},{5,61},{6,62},{7,63},{8,0},{9,1... | collective-permute-start | bytes 192008 | tf_op jit(solution)/shard_map/ppermute | solution.py:777
  103.3 10.2 %copy-start.10 = (f32[4,8,128]{2,1,0:T(8,128)S(1)}, f32[4,8,128]{2,1,0:T(8,128)}, u32[]{:S(2)}) copy-start(f32[4,8,128]{2,1,0:T(8,128)} %constant.47.clone.refs_8_) | copy-start | bytes 49156

commit v6 on v5

--- a/solution.py
+++ b/solution.py
@@ -488,7 +488,7 @@
     h2[...] = t2[...] + add.reshape(16, 8, 16, 128)
 
 
-def apply_operator(src, dst, lt, own=False):
+def apply_k(src, dst, lt, own=False):
     rows = slice(8, 16) if own else slice(0, 24)
 
     def before(k, add):
@@ -514,7 +514,7 @@
                 du = du + 1.5 * after(16 + zi, 0)
                 dp = dp + 1.5 * after(zi, 64)
             dst[xi * 4 + zi] = du
-            dst[16 + xi * 4 + zi] = 2.0 * u[xi] + dp
+            dst[16 + xi * 4 + zi] = dp
     for xi in range(4):
         u = [src[48 + xi * 4 + j, rows] for j in range(4)]
         p = [src[xi * 4 + j, rows] + src[64 + xi * 4 + j, rows] for j in range(4)]
@@ -528,14 +528,14 @@
                 du = du + 1.5 * z_after(u[0], lt)
                 dp = dp + 1.5 * z_after(p[0], lt)
             dst[xi * 4 + zi] = dst[xi * 4 + zi] + du
-            dst[48 + xi * 4 + zi] = 2.0 * u[zi] + dp
+            dst[48 + xi * 4 + zi] = dp
 
     def along_y(c, _):
         rho, u, t = src[c, rows], src[32 + c, rows], src[64 + c, rows]
         div = dst[c] + central_y(u, lt)
-        dst[32 + c] = 2.0 * u + central_y(rho + t, lt)
-        dst[c] = 2.0 * rho + div
-        dst[64 + c] = 2.0 * t + div
+        dst[32 + c] = central_y(rho + t, lt)
+        dst[c] = div
+        dst[64 + c] = div
         return 0
     lax.fori_loop(0, 16, along_y, 0, unroll=8)
 
@@ -598,8 +598,7 @@
         w = pltpu.roll(v, 64, 1)
         return 0.25 * (v - w) if ya == 0 else 0.25 * (w - v)
 
-    up = jnp.zeros((8, 128), jnp.float32)
-    low = jnp.zeros((8, 128), jnp.float32)
+    total = [jnp.zeros((8, 128), jnp.float32)] * 3
     for xa in range(2):
         for za in range(2):
             for ya in range(2):
@@ -611,41 +610,58 @@
                 e = [own(at(f, xa, za, ya)) for f in range(5)]
                 div = (dx(field(1), xa, za, ya) + dy(field(2), xa, za, ya)
                        + dz(field(3), xa, za, ya))
-                g = [2.0 * e[0] + div, 2.0 * e[1] + dx(pressure, xa, za, ya),
-                     2.0 * e[2] + dy(pressure, xa, za, ya),
-                     2.0 * e[3] + dz(pressure, xa, za, ya), 2.0 * e[4] + div]
+                v = [div, dx(pressure, xa, za, ya), dy(pressure, xa, za, ya),
+                     dz(pressure, xa, za, ya), div]
                 for f in range(5):
-                    up = up + e[f] * g[f]
-                    low = low + g[f] * g[f]
-    return up * lt[23:24], low * lt[23:24]
-
-
-def fine_products(r, m, ar, am, lt, own):
+                    total = [total[0] + e[f] * e[f], total[1] + e[f] * v[f], total[2] + v[f] * v[f]]
+    return [t * lt[23:24] for t in total]
+
+
+PAIRS = [(i, j) for i in range(3) for j in range(i, 3)]
+
+
+def fine_products(e, s, t, ke, kt, lt, own):
     rows = slice(0, 8) if own else slice(8, 16)
-    total = [jnp.zeros((8, 128), jnp.float32) for _ in range(6)]
+    zero = jnp.zeros((8, 128), jnp.float32)
+    total = [zero] * 18
     for xi in range(4):
         for zi in range(4):
-            def over_f(f, acc):
+            acc = [zero] * 18
+            for f in range(5):
                 k = f * 16 + xi * 4 + zi
-                a, b, c, d = r[k, 8:16], m[k, 8:16], ar[k, rows], am[k, rows]
-                return (acc[0] + a * c, acc[1] + a * d + b * c, acc[2] + b * d,
-                        acc[3] + c * c, acc[4] + c * d, acc[5] + d * d)
-            zero = jnp.zeros((8, 128), jnp.float32)
-            acc = lax.fori_loop(0, 5, over_f, (zero,) * 6, unroll=True)
+                x = [e[k, 8:16], s[k, 8:16], t[k, 8:16]]
+                y = [ke[k, rows], x[2], kt[k, rows]]
+                for n, (i, j) in enumerate(PAIRS):
+                    acc[n] = acc[n] + x[i] * x[j]
+                    mixed = x[i] * y[j] if i == j else x[i] * y[j] + x[j] * y[i]
+                    acc[6 + n] = acc[6 + n] + mixed
+                    acc[12 + n] = acc[12 + n] + y[i] * y[j]
             w = WEIGHTS[xi] * WEIGHTS[zi]
-            total = [t + w * a for t, a in zip(total, acc)]
-    return [t * lt[22:23] for t in total]
-
-
-def pass_words(r, m, ar, am, pe, co, gram, lt, peers, own=False):
-    two_level(r, pe, co, lt)
-    apply_operator(pe, m, lt)
-    apply_operator(r, ar, lt, own)
-    apply_operator(m, am, lt, own)
-    products = list(coarse_products(co, lt)) + fine_products(r, m, ar, am, lt, own)
-    rows = jnp.concatenate([jnp.sum(p, axis=0, keepdims=True) for p in products], axis=0)
-    for n in range(peers):
-        gram[n] = rows
+            total = [a + w * b for a, b in zip(total, acc)]
+    return [a * lt[22:23] for a in total]
+
+
+def diagonal():
+    return (lax.broadcasted_iota(jnp.int32, (24, 128), 0)
+            == lax.broadcasted_iota(jnp.int32, (24, 128), 1))
+
+
+def pass_words(e, s, t, ke, kt, co, gram, lt, own=False):
+    two_level(e, s, co, lt)
+    apply_k(s, t, lt)
+
+    def over_k(k, _):
+        e[k] = e[k] - s[k]
+        return 0
+    lax.fori_loop(0, 80, over_k, 0, unroll=8)
+    apply_k(e, ke, lt, own)
+    apply_k(t, kt, lt, own)
+    products = coarse_products(co, lt) + fine_products(e, s, t, ke, kt, lt, own)
+    rows = [jnp.sum(p, axis=0, keepdims=True) for p in products] + [jnp.zeros((3, 128), jnp.float32)]
+    total = jnp.sum(jnp.concatenate(rows, axis=0), axis=1, keepdims=True)
+    line = jnp.sum(jnp.where(diagonal(), total, 0.0), axis=0, keepdims=True)
+    for n in range(gram.shape[0]):
+        gram[n] = jnp.broadcast_to(line, (8, 128))
 
 
 def pack_kernel(idx, mine, own, to_upper, to_lower):
@@ -686,7 +702,7 @@
                 win[at + 5:at + 6] = low[5:6] - 1.5 * edge_low[e:e + 1]
 
 
-def first_pass_kernel(idx, quarters, lt, r, m, ar, am, pe, gram, co):
+def first_pass_kernel(idx, quarters, lt, r, s, t, ke, kt, gram, co):
     zero = jnp.zeros((2, 128), jnp.float32)
     for f in range(5):
         for xi in range(4):
@@ -696,51 +712,67 @@
                 r[k, 0:2] = zero
                 r[k, 2:22] = quarters[zi, at:at + 20]
                 r[k, 22:24] = zero
-    pass_words(r, m, ar, am, pe, co, gram, lt, gram.shape[0])
-
-
-def step_sizes(sums, peers):
-    s = sums[0]
-    for n in range(1, peers):
-        s = s + sums[n]
-    s = jnp.broadcast_to(jnp.sum(s, axis=1, keepdims=True), (8, 128))
-    a1 = s[0:1] / (s[1:2] + EPS)
-    up = s[2:3] - a1 * s[3:4] + a1 * a1 * s[4:5]
-    low = s[5:6] - 2.0 * a1 * s[6:7] + a1 * a1 * s[7:8]
-    return a1, up / (low + EPS)
-
-
-def next_pass_kernel(first, idx, sums, r, m, ar, am, pe, *rest):
+    pass_words(r, s, t, ke, kt, co, gram, lt)
+
+
+def step_sizes(sums):
+    line = sums[0, 0:1]
+    for n in range(1, sums.shape[0]):
+        line = line + sums[n, 0:1]
+    v = jnp.sum(jnp.where(diagonal(), line, 0.0), axis=1, keepdims=True)
+    v = jnp.broadcast_to(v, (24, 128))
+    c0, c1, c2 = v[0:1], v[1:2], v[2:3]
+    den = 4.0 * c0 + 4.0 * c1 + c2 + EPS
+    a1, b1 = (2.0 * c0 + c1) / den, (2.0 * c1 + c2 + EPS) / den
+    d = [jnp.ones_like(a1), b1, -a1]
+
+    def form(base, twice):
+        total = None
+        for n, (i, j) in enumerate(PAIRS):
+            term = d[i] * d[j] * v[base + n:base + n + 1]
+            if twice and i != j:
+                term = 2.0 * term
+            total = term if total is None else total + term
+        return total
+    rr, kk = jnp.maximum(form(3, True), 0.0), jnp.maximum(form(15, True), 0.0)
+    bound = jnp.sqrt(rr) * jnp.sqrt(kk)
+    rk = jnp.clip(form(9, False), -bound, bound)
+    den = 4.0 * rr + 4.0 * rk + kk + EPS
+    return a1, b1, (2.0 * rr + rk) / den, (2.0 * rk + kk + EPS) / den
+
+
+def next_pass_kernel(first, idx, sums, e, s, t, ke, kt, *rest):
     if first:
-        lt, r2, m2, ar2, am2, pe2, acc2, gram, co = rest
+        lt, r2, s2, t2, ke2, kt2, acc2, gram, co = rest
     else:
-        acc, lt, r2, m2, ar2, am2, pe2, acc2, gram, co = rest
-    a1, a2 = step_sizes(sums, gram.shape[0])
+        acc, lt, r2, s2, t2, ke2, kt2, acc2, gram, co = rest
+    a1, b1, a2, b2 = step_sizes(sums)
 
     def over_k(k, _):
-        q = r[k] - a1 * m[k]
-        v = a1 * pe[k, 8:16] + a2 * q[8:16]
+        sk, tk = s[k], t[k]
+        r1 = e[k] + b1 * sk - a1 * tk
+        v = a1 * sk[8:16] + a2 * r1[8:16]
         acc2[k] = v if first else acc[k] + v
-        r2[k] = q - a2 * (ar[k] - a1 * am[k])
+        r2[k] = b2 * r1 - a2 * (ke[k] + b1 * tk - a1 * kt[k])
         return 0
     lax.fori_loop(0, 80, over_k, 0, unroll=4)
-    pass_words(r2, m2, ar2, am2, pe2, co, gram, lt, gram.shape[0], own=not first)
-
-
-def third_pass_kernel(idx, sums, r, m, ar, am, pe, acc, lt, ro, mo, po, acc2, gram,
-                      r2, m2, ar2, am2, pe2, co):
-    next_pass_kernel(False, idx, sums, r, m, ar, am, pe, acc, lt, r2, m2, ar2, am2, pe2, acc2, gram, co)
-    ro[...] = r2[:, 8:16]
-    mo[...] = m2[:, 8:16]
-    po[...] = pe2[:, 8:16]
-
-
-def last_kernel(idx, sums, r, m, pe, acc, low, h2, select, ec, out, fields, change, stack, rows):
-    a1, a2 = step_sizes(sums, sums.shape[0])
+    pass_words(r2, s2, t2, ke2, kt2, co, gram, lt, own=not first)
+
+
+def third_pass_kernel(idx, sums, e, s, t, ke, kt, acc, lt, eo, so, to, acc2, gram,
+                      r2, s2, t2, ke2, kt2, co):
+    next_pass_kernel(False, idx, sums, e, s, t, ke, kt, acc, lt, r2, s2, t2, ke2, kt2, acc2, gram, co)
+    eo[...] = r2[:, 8:16]
+    so[...] = s2[:, 8:16]
+    to[...] = t2[:, 8:16]
+
+
+def last_kernel(idx, sums, e, s, t, acc, low, h2, select, ec, out, fields, change, stack, rows):
+    a1, b1, a2, _ = step_sizes(sums)
 
     def over_k(k, _):
-        q = r[k] - a1 * m[k]
-        change[pl.ds(pl.multiple_of(k * 8, 8), 8)] = acc[k] + a1 * pe[k] + a2 * q
+        r1 = e[k] + b1 * s[k] - a1 * t[k]
+        change[pl.ds(pl.multiple_of(k * 8, 8), 8)] = acc[k] + a1 * s[k] + a2 * r1
         return 0
     lax.fori_loop(0, 80, over_k, 0, unroll=4)
     z = idx[1]
@@ -804,16 +836,16 @@
 
     win, own, part = (80, 24, 128), (80, 8, 128), (blocks, 8, 128)
     co = (40, 24, 128)
-    r, m, ar, am, pe, gram = call(first_pass_kernel, "pass1", idx, [quarters, lt], [],
+    e, s, t, ke, kt, gram = call(first_pass_kernel, "pass1", idx, [quarters, lt], [],
                                   [win] * 5 + [part], [co])
-    r, m, ar, am, pe, acc, gram = call(functools.partial(next_pass_kernel, True), "pass2", idx,
-                                       [summed(gram), r, m, ar, am, pe, lt], [],
+    e, s, t, ke, kt, acc, gram = call(functools.partial(next_pass_kernel, True), "pass2", idx,
+                                       [summed(gram), e, s, t, ke, kt, lt], [],
                                        [win] * 5 + [own, part], [co])
-    r, m, pe, acc, gram = call(third_pass_kernel, "pass3", idx,
-                               [summed(gram), r, m, ar, am, pe, acc, lt], [],
-                               [own] * 4 + [part], [win, win, own, own, win, co])
+    e, s, t, acc, gram = call(third_pass_kernel, "pass3", idx,
+                               [summed(gram), e, s, t, ke, kt, acc, lt], [],
+                               [own] * 4 + [part], [win, win, win, own, own, co])
     out, fields = call(last_kernel, "last", idx,
-                       [summed(gram), r, m, pe, acc, low, h2, tables["select"]], [tables["ec"]],
+                       [summed(gram), e, s, t, acc, low, h2, tables["select"]], [tables["ec"]],
                        [(4, 8, 64, 128), (5, 4, 8, 64)], [(640, 128), (8, 2048), (160, 512)])
     return out, fields
 

time: 117 us -> 119 us (1.017)
  Pallas kernels: 31.9 us -> 33.4 us
    pallas_call x11, Pallas kernels: 31.9 us -> 33.4 us  [call(): pl.pallas_call(body, name=name, out_shape=[jax.ShapeDtypeStruct(s, jnp.fl...]
where the time goes in v6:
time: 119 us; the launch traced here: 118 us
  blocking collectives  64.7 us (54%)
  Pallas kernels  33.4 us (28%)
  starting transfers between devices  16.2 us (14%)
  waiting for transfers between devices  1.9 us (2%)
  local copies, waits for them, and re-layouts  1.28 us (1%)
    all_to_all x3, blocking collectives, summed(): lax.all_to_all(gram, 'space', 0, 0, axis_index_groups=far, tiled=True)  34.3 us
    pallas_call x11, Pallas kernels, call(): pl.pallas_call(body, name=name, out_shape=[jax.ShapeDtypeStruct(s, jnp.fl...  33.4 us
    ppermute x4, starting transfers between devices, shifted(): lax.ppermute(x, 'space', [(i, (i + by) % spaces) for i in range(spaces)])  16.2 us
    all_to_all x1, blocking collectives, on_device(): lax.all_to_all(res, 'space', 0, 0, axis_index_groups=near, tiled=True)  12.2 us
    all_gather x1, blocking collectives, on_device(): quarters = lax.all_gather(quarter, 'vel')  9.27 us
    all_gather x1, blocking collectives, on_device(): got = lax.all_gather(pay, 'vel')  8.81 us
  transfers between devices with their start and end apart: 4, of which 2 were waited for; matrix products, arithmetic and copies ran while one was open for 0% of the time, Pallas kernels for 6%

profile of v6, /device:TPU:2, one launch (start us, length us, event | category | flops | bytes accessed | tf_op | source)
XLA Modules:
  0.0 118.2 jit_solution(17494091597223178863)
XLA Ops:
  0.6 0.1 pad_add_fusion.idx
  0.7 0.0 copy-start
  0.7 1.2 %copy-done = f32[4,8,64,128]{3,2,1,0:T(8,128)S(1)} copy-done((f32[4,8,64,128]{3,2,1,0:T(8,128)S(1)}, f32[4,8,64,128]{3,2,1,0:T(8,128)}, u32[]{:S(2)}) %copy-start) | copy-done | bytes 1048600
  1.9 0.0 copy-start.1
  1.9 0.0 copy-start.3
  1.9 0.0 copy-start.4
  1.9 0.0 copy-start.7
  2.0 0.0 copy-start.8
  2.0 1.9 %rims.1 = (f32[544,128]{1,0:T(8,128)S(1)}, f32[544,128]{1,0:T(8,128)S(1)}) custom-call(s32[2]{0:T(128)S(1)} %pad_add_fusion.idx, f32[4,8,64,128]{3,2,1,0:T(8,128)S(1)} %copy-done), custom_call_target="tpu_custom_call" | custom-call | tf_op jit(solution)/shard_map/rims/pallas_call | solution.py:160
  3.9 2.0 %collective-permute-start = (f32[544,128]{1,0:T(8,128)S(1)}, f32[544,128]{1,0:T(8,128)S(1)}, u32[]{:S(2)}, u32[]{:S(2)}) collective-permute-start(f32[544,128]{1,0:T(8,128)S(1)} %get-tuple-element.32), channel_id=1, source_target_pairs={{0,1},{1,2},{2,3},{3,4},{4,5},{5,6},{6,7},{7,8},{8,9},{9,10},{10,1... | collective-permute-start | bytes 835592 | tf_op jit(solution)/shard_map/ppermute | solution.py:809
  5.8 0.0 copy-start.2
  5.8 0.0 copy-start.6
  5.8 0.0 copy-start.9
  5.8 8.1 %collective-permute-start.1 = (f32[544,128]{1,0:T(8,128)S(1)}, f32[544,128]{1,0:T(8,128)S(1)}, u32[]{:S(2)}, u32[]{:S(2)}) collective-permute-start(f32[544,128]{1,0:T(8,128)S(1)} %get-tuple-element.33), channel_id=1, source_target_pairs={{0,63},{1,0},{2,1},{3,2},{4,3},{5,4},{6,5},{7,6},{8,7},{9,8},{10,9... | collective-permute-start | bytes 835592 | tf_op jit(solution)/shard_map/ppermute | solution.py:809
  13.9 0.0 copy-done.1
  13.9 0.0 copy-done.3
  13.9 0.0 copy-done.4
  13.9 0.0 copy-done.7
  13.9 0.0 copy-done.8
  13.9 5.0 %local.1 = (f32[16,8,16,128]{3,2,1,0:T(8,128)S(1)}, f32[16,16,128]{2,1,0:T(8,128)S(1)}, f32[4,20,128]{2,1,0:T(8,128)S(1)}) custom-call(s32[2]{0:T(128)S(1)} %pad_add_fusion.idx, f32[4,8,64,128]{3,2,1,0:T(8,128)S(1)} %copy-done, f32[3,4,8,64]{3,2,1,0:T(8,128)S(1)} %copy-done.8, f32[64,512]{1,0:T(8,128)S(1)} %copy-done.1, f32[4,32,128]{2,1,0:T(8,128)S(1)} %copy-done.4, ...), custom_call_target="tpu_custom_call" | custom-call | tf_op jit(solution)/shard_map/local/pallas_call | solution.py:160
  18.9 1.5 %collective-permute-done.refs_0_ = f32[544,128]{1,0:T(8,128)S(1)} collective-permute-done((f32[544,128]{1,0:T(8,128)S(1)}, f32[544,128]{1,0:T(8,128)S(1)}, u32[]{:S(2)}, u32[]{:S(2)}) %collective-permute-start) | collective-permute-done | bytes 278560 | tf_op jit(solution)/shard_map/ppermute | solution.py:809
  20.4 0.0 collective-permute-done.1.refs_1_
  20.4 0.0 copy-done.2
  20.4 0.0 copy-done.6
  20.5 0.0 copy-done.9
  20.5 4.6 %moments.1 = (f32[408,128]{1,0:T(8,128)S(1)}, f32[16,8,16,128]{3,2,1,0:T(8,128)S(1)}) custom-call(s32[2]{0:T(128)S(1)} %pad_add_fusion.idx, f32[544,128]{1,0:T(8,128)S(1)} %collective-permute-done.refs_0_, f32[544,128]{1,0:T(8,128)S(1)} %collective-permute-done.1.refs_1_, f32[16,8,16,128]{3,2,1,0:T(8,128)S(1)} %get-tuple-element.34.refs_2_, ...), custom_call_target="tpu_custom_call" | custom-call | tf_op jit(solution)/shard_map/moments/pallas_call | solution.py:160
  25.1 8.8 %all-gather = f32[1632,128]{1,0:T(8,128)S(1)} all-gather(f32[408,128]{1,0:T(8,128)S(1)} %get-tuple-element.36), channel_id=2, replica_groups=mesh['vel'=4,'space'=64] {'vel'}, dimensions={0}, use_global_device_ids=true | all-gather | bytes 1044480 | tf_op jit(solution)/shard_map/all_gather | solution.py:820
  33.9 0.6 residual.1
  34.4 12.2 %all_to_all.20 = f32[8,30,128]{2,1,0:T(8,128)S(1)} all-to-all(f32[8,30,128]{2,1,0:T(8,128)S(1)} %residual.1), channel_id=1, replica_groups={{0,1,2,3,4,5,6,7},{8,9,10,11,12,13,14,15},{16,17,18,19,20,21,22,23},{24..., dimensions={0} | all-to-all | bytes 245760 | tf_op jit(solution)/shard_map/all_to_all | solution.py:824
  46.7 0.0 copy-start.5
  46.7 0.6 pack.1
  47.3 0.1 collective-permute-start.2
  47.4 6.0 %collective-permute-start.3 = (f32[125,128]{1,0:T(8,128)S(1)}, f32[125,128]{1,0:T(8,128)S(1)}, u32[]{:S(2)}, u32[]{:S(2)}) collective-permute-start(f32[125,128]{1,0:T(8,128)S(1)} %get-tuple-element.40.refs_3_), channel_id=1, source_target_pairs={{0,56},{1,57},{2,58},{3,59},{4,60},{5,61},{6,62},{7,63},{8,0},{9,1... | collective-permute-start | bytes 192008 | tf_op jit(solution)/shard_map/ppermute | solution.py:809
  53.4 0.0 copy-done.5
  53.4 1.8 %feq.1 = (f32[16,8,16,128]{3,2,1,0:T(8,128)S(1)}, f32[80,128]{1,0:T(8,128)S(1)}) custom-call(s32[2]{0:T(128)S(1)} %pad_add_fusion.idx, f32[4,408,128]{2,1,0:T(8,128)S(1)} %bitcast.5, f32[16,8,16,128]{3,2,1,0:T(8,128)S(1)} %get-tuple-element.41.refs_1_, f32[40,128]{1,0:T(8,128)S(1)} %copy-done.2, f32[4,56,128]{2,1,0:T(8,128)S(1)} %copy-done.5), custom_call_target="tpu_custom_call" | custom-call | tf_op jit(solution)/shard_map/feq/pallas_call | solution.py:160
  55.2 0.4 collective-permute-done.2.refs_0_
  55.6 0.0 collective-permute-done.3.refs_2_
  55.6 0.6 window.1
  56.1 9.3 %all-gather.1 = f32[1600,128]{1,0:T(8,128)S(1)} all-gather(f32[400,128]{1,0:T(8,128)S(1)} %window.1), channel_id=3, replica_groups=mesh['vel'=4,'space'=64] {'vel'}, dimensions={0}, use_global_device_ids=true | all-gather | bytes 1024000 | tf_op jit(solution)/shard_map/all_gather | solution.py:832
  65.4 5.1 %pass1.1 = (f32[80,24,128]{2,1,0:T(8,128)S(1)}, f32[80,24,128]{2,1,0:T(8,128)S(1)}, f32[80,24,128]{2,1,0:T(8,128)S(1)}, f32[80,24,128]{2,1,0:T(8,128)S(1)}, f32[...) custom-call(s32[2]{0:T(128)S(1)} %pad_add_fusion.idx, f32[4,400,128]{2,1,0:T(8,128)S(1)} %bitcast.6, f32[40,128]{1,0:T(8,128)S(1)} %copy-done.2), custom_call_target="tpu_custom_call" | custom-call | tf_op jit(solution)/shard_map/pass1/pallas_call | solution.py:160
  70.5 13.9 %all_to_all.21.refs_0_ = f32[8,8,128]{2,1,0:T(8,128)S(1)} all-to-all(f32[8,8,128]{2,1,0:T(8,128)S(1)} %get-tuple-element.43), channel_id=1, replica_groups={{0,8,16,24,32,40,48,56},{1,9,17,25,33,41,49,57},{2,10,18,26,34,42,50,58..., dimensions={0} | all-to-all | bytes 65536 | tf_op jit(solution)/shard_map/all_to_all | solution.py:835
  84.5 5.6 %pass2.1 = (f32[80,24,128]{2,1,0:T(8,128)S(1)}, f32[80,24,128]{2,1,0:T(8,128)S(1)}, f32[80,24,128]{2,1,0:T(8,128)S(1)}, f32[80,24,128]{2,1,0:T(8,128)S(1)}, f32[...) custom-call(s32[2]{0:T(128)S(1)} %pad_add_fusion.idx, ...), custom_call_target="tpu_custom_call" | custom-call | tf_op jit(solution)/shard_map/pass2/pallas_call | solution.py:160
  90.1 10.1 %all_to_all.22.refs_0_ = f32[8,8,128]{2,1,0:T(8,128)S(1)} all-to-all(f32[8,8,128]{2,1,0:T(8,128)S(1)} %get-tuple-element.49), channel_id=1, replica_groups={{0,8,16,24,32,40,48,56},{1,9,17,25,33,41,49,57},{2,10,18,26,34,42,50,58..., dimensions={0} | all-to-all | bytes 65536 | tf_op jit(solution)/shard_map/all_to_all | solution.py:835
  100.2 4.5 %pass3.1 = (f32[80,8,128]{2,1,0:T(8,128)S(1)}, f32[80,8,128]{2,1,0:T(8,128)S(1)}, f32[80,8,128]{2,1,0:T(8,128)S(1)}, f32[80,8,128]{2,1,0:T(8,128)S(1)}, f32[8,8,128]{2,1,0:T(8,128)S(1)}) custom-call(s32[2]{0:T(128)S(1)} %pad_add_fusion.idx, f32[8,8,128]{2,1,0:T(8,128)S(1)} %all_to_all.22.refs_0_, f32[80,24,128]{2,1,0:T(8,128)S(1)} %get-tuple-element.50.refs_1_, ...), custom_call_target="tpu_custom_call" | custom-call | tf_op jit(solution)/shard_map/pass3/pallas_call | solution.py:160
  104.8 0.0 copy-start.10
  104.8 10.3 %all_to_all.23.refs_0_ = f32[8,8,128]{2,1,0:T(8,128)S(1)} all-to-all(f32[8,8,128]{2,1,0:T(8,128)S(1)} %get-tuple-element.56), channel_id=1, replica_groups={{0,8,16,24,32,40,48,56},{1,9,17,25,33,41,49,57},{2,10,18,26,34,42,50,58..., dimensions={0} | all-to-all | bytes 65536 | tf_op jit(solution)/shard_map/all_to_all | solution.py:835
  115.0 0.0 copy-done.10
  115.1 3.2 %last.1 = (f32[4,8,64,128]{3,2,1,0:T(8,128)}, f32[5,4,8,64]{3,2,1,0:T(8,128)}) custom-call(s32[2]{0:T(128)S(1)} %pad_add_fusion.idx, f32[8,8,128]{2,1,0:T(8,128)S(1)} %all_to_all.23.refs_0_, f32[80,8,128]{2,1,0:T(8,128)S(1)} %get-tuple-element.57.refs_1_, f32[80,8,128]{2,1,0:T(8,128)S(1)} %get-tuple-element.58.refs_2_, ...), custom_call_target="tpu_custom_call" | custom-call | tf_op jit(solution)/shard_map/last/pallas_call | solution.py:160
  (1 shorter events, 0.0 us)
Async XLA Ops:
  0.7 1.2 %copy-start = (f32[4,8,64,128]{3,2,1,0:T(8,128)S(1)}, f32[4,8,64,128]{3,2,1,0:T(8,128)}, u32[]{:S(2)}) copy-start(f32[4,8,64,128]{3,2,1,0:T(8,128)} %refs_0_.3) | copy-start | bytes 3145732
  1.9 12.0 %copy-start.1 = (f32[64,512]{1,0:T(8,128)S(1)}, f32[64,512]{1,0:T(8,128)}, u32[]{:S(2)}) copy-start(f32[64,512]{1,0:T(8,128)} %constant.48.clone.refs_2_.refs_7_) | copy-start | bytes 393220
  1.9 12.0 %copy-start.3 = (f32[4,48,128]{2,1,0:T(8,128)S(1)}, f32[4,48,128]{2,1,0:T(8,128)}, u32[]{:S(2)}) copy-start(f32[4,48,128]{2,1,0:T(8,128)} %constant.42.clone.refs_5_.refs_8_) | copy-start | bytes 294916
  1.9 12.0 %copy-start.4 = (f32[4,32,128]{2,1,0:T(8,128)S(1)}, f32[4,32,128]{2,1,0:T(8,128)}, u32[]{:S(2)}) copy-start(f32[4,32,128]{2,1,0:T(8,128)} %constant.40.clone.refs_3_.refs_6_) | copy-start | bytes 196612
  1.9 12.0 %copy-start.7 = (f32[4,48,128]{2,1,0:T(8,128)S(1)}, f32[4,48,128]{2,1,0:T(8,128)}, u32[]{:S(2)}) copy-start(f32[4,48,128]{2,1,0:T(8,128)} %constant.43.clone.refs_4_) | copy-start | bytes 294916
  2.0 12.0 %copy-start.8 = (f32[3,4,8,64]{3,2,1,0:T(8,128)S(1)}, f32[3,4,8,64]{3,2,1,0:T(8,128)}, u32[]{:S(2)}) copy-start(f32[3,4,8,64]{3,2,1,0:T(8,128)} %refs_1_.2) | copy-start | bytes 73732
  3.9 16.6 %collective-permute-start = (f32[544,128]{1,0:T(8,128)S(1)}, f32[544,128]{1,0:T(8,128)S(1)}, u32[]{:S(2)}, u32[]{:S(2)}) collective-permute-start(f32[544,128]{1,0:T(8,128)S(1)} %get-tuple-element.32), channel_id=1, source_target_pairs={{0,1},{1,2},{2,3},{3,4},{4,5},{5,6},{6,7},{7,8},{8,9},{9,10},{10,1... | collective-permute-start | bytes 835592 | tf_op jit(solution)/shard_map/ppermute | solution.py:809
  5.8 14.6 %copy-start.2 = (f32[40,128]{1,0:T(8,128)S(1)}, f32[40,128]{1,0:T(8,128)}, u32[]{:S(2)}) copy-start(f32[40,128]{1,0:T(8,128)} %constant.46.clone.refs_5_.refs_2_.refs_1_.refs_6_.refs_7_) | copy-start | bytes 61444
  5.8 14.6 %copy-start.6 = (f32[4,48,128]{2,1,0:T(8,128)S(1)}, f32[4,48,128]{2,1,0:T(8,128)}, u32[]{:S(2)}) copy-start(f32[4,48,128]{2,1,0:T(8,128)} %constant.41.clone.refs_7_) | copy-start | bytes 294916
  5.8 14.6 %copy-start.9 = (f32[40,64]{1,0:T(8,128)S(1)}, f32[40,64]{1,0:T(8,128)}, u32[]{:S(2)}) copy-start(f32[40,64]{1,0:T(8,128)} %constant.44.clone.refs_4_) | copy-start | bytes 30724
  5.8 14.6 %collective-permute-start.1 = (f32[544,128]{1,0:T(8,128)S(1)}, f32[544,128]{1,0:T(8,128)S(1)}, u32[]{:S(2)}, u32[]{:S(2)}) collective-permute-start(f32[544,128]{1,0:T(8,128)S(1)} %get-tuple-element.33), channel_id=1, source_target_pairs={{0,63},{1,0},{2,1},{3,2},{4,3},{5,4},{6,5},{7,6},{8,7},{9,8},{10,9... | collective-permute-start | bytes 835592 | tf_op jit(solution)/shard_map/ppermute | solution.py:809
  46.7 6.7 %copy-start.5 = (f32[4,56,128]{2,1,0:T(8,128)S(1)}, f32[4,56,128]{2,1,0:T(8,128)}, u32[]{:S(2)}) copy-start(f32[4,56,128]{2,1,0:T(8,128)} %constant.45.clone.refs_3_) | copy-start | bytes 344068
  47.3 8.3 %collective-permute-start.2 = (f32[125,128]{1,0:T(8,128)S(1)}, f32[125,128]{1,0:T(8,128)S(1)}, u32[]{:S(2)}, u32[]{:S(2)}) collective-permute-start(f32[125,128]{1,0:T(8,128)S(1)} %get-tuple-element.38.refs_4_), channel_id=1, source_target_pairs={{0,8},{1,9},{2,10},{3,11},{4,12},{5,13},{6,14},{7,15},{8,16},{9,17... | collective-permute-start | bytes 192008 | tf_op jit(solution)/shard_map/ppermute | solution.py:809
  47.4 8.2 %collective-permute-start.3 = (f32[125,128]{1,0:T(8,128)S(1)}, f32[125,128]{1,0:T(8,128)S(1)}, u32[]{:S(2)}, u32[]{:S(2)}) collective-permute-start(f32[125,128]{1,0:T(8,128)S(1)} %get-tuple-element.40.refs_3_), channel_id=1, source_target_pairs={{0,56},{1,57},{2,58},{3,59},{4,60},{5,61},{6,62},{7,63},{8,0},{9,1... | collective-permute-start | bytes 192008 | tf_op jit(solution)/shard_map/ppermute | solution.py:809
  104.8 10.3 %copy-start.10 = (f32[4,8,128]{2,1,0:T(8,128)S(1)}, f32[4,8,128]{2,1,0:T(8,128)}, u32[]{:S(2)}) copy-start(f32[4,8,128]{2,1,0:T(8,128)} %constant.47.clone.refs_8_) | copy-start | bytes 49156

commit v7 on v6

--- a/solution.py
+++ b/solution.py
@@ -86,6 +86,7 @@
         if i == 3:
             kap = kap + (1 - ispos) * (0.8 - 3 * DT * ax)
         vec.append(kap)
+    kappa = vec[10:14]
     vec.append(ispos)
     for jj in range(4):
         vec.append(-DT * 0.5 * x * np.where(ispos > 0, d4[3][jj], d4[0][jj]))
@@ -101,10 +102,18 @@
     tab2 = moment_rows(0, rows32, 48)
     tab1 = moment_rows(40, low, 48)
     tab0 = moment_rows(32, low, 48)
+    tabd = per_rank(np.concatenate([v * rows32 for v in kappa] + [ispos * low, (1 - ispos) * low]))
+    tabs = per_rank(np.concatenate([ispos * rows32, (1 - ispos) * rows32]))
     select = np.zeros((64, 512))
     for n in range(4):
         for la in range(128):
             select[4 * (la % 16) + n, 128 * n + la] = 1.0
+    import ml_dtypes
+    pieces, left = [], per_rank(ec)
+    for _ in range(3):
+        pieces.append(left.astype(ml_dtypes.bfloat16))
+        left = left - pieces[-1].astype(np.float32)
+    split = np.concatenate([pieces[n].astype(np.float32) for n in (0, 1, 0, 2, 1, 0)], axis=1)
     g = rows32 @ ec.T
     g5 = g[:8]
     mix = np.zeros((40, 64))
@@ -146,7 +155,7 @@
         rows.append(np.zeros(128))
     lanes = np.stack(rows).astype(np.float32)
     return dict(vec=vec, tab2=tab2, tab1=tab1, tab0=tab0, mix=mix.astype(np.float32),
-                final=final, lanes=lanes, ec=per_rank(ec), select=select.astype(np.float32))
+                final=final, lanes=lanes, split=split, tabd=tabd, tabs=tabs, select=select.astype(np.float32))
 
 
 def call(kernel, name, idx, full, ranked, outs, scratch=(), limit=24):
@@ -316,7 +325,7 @@
     return (lax.broadcasted_iota(jnp.int32, (8, 128), 1) // 16 == y).astype(jnp.float32)
 
 
-def local_kernel(idx, h, forcing, select, vec, tab0, tab1, twice, mom, force, first, once, m):
+def local_kernel(idx, h, forcing, select, vec, tab0, tab1, tab2, twice, mom, force, first, once, m):
     spread = exact_dot(forcing[...].reshape(96, 64), select[...])
     here = row_of_y()
     force[...] = jnp.zeros_like(force)
@@ -338,8 +347,9 @@
 
     m[...] = project(first[...].reshape(2048, 128), tab0[0])
     m[...] = m[...] + project(once[...].reshape(2048, 128), tab1[0])
-    for c in range(16):
-        mom[c] = m[128 * c:128 * c + 128].T[32:48]
+    m[...] = m[...] + project(twice[...].reshape(2048, 128), tab2[0])
+    for c in range(16):
+        mom[c] = m[128 * c:128 * c + 128].T
 
 
 def z_before(q, lt):
@@ -384,39 +394,36 @@
 CENTRAL = [[0.0 if i == j else 0.5 * D4[i][j] for j in range(4)] for i in range(4)]
 
 
-def moment_kernel(idx, up, down, twice, moma, mix, lt, vec, tab2, tab1, pay, t2,
-                  delta, yz, extra, mom, full, m, stack):
+def moment_kernel(idx, up, down, moma, mix, lt, vec, tabd, tabs, pay, delta, inflow,
+                  yz, mom, full, stack):
     right = lax.broadcasted_iota(jnp.int32, (16, 128), 1) >= 64
-    pos = vec[0, 14:15]
 
     def unpack(n, _):
         at = pl.ds(pl.multiple_of(n * 16, 16), 16)
         u, d = up[at], down[at]
         zi, y = n // 8, n % 8
         delta[zi, y] = vec[0, 9:10] * jnp.where(right, u, d)
-        extra[zi, y] = vec[0, 9:10] * pltpu.roll(jnp.where(right, d, u), 64, 1)
+        inflow[zi, y] = vec[0, 9:10] * pltpu.roll(jnp.where(right, d, u), 64, 1)
         return 0
     lax.fori_loop(0, 32, unpack, 0, unroll=8)
     layer_yz(delta, yz, vec)
-    for xi in range(4):
-        def over_n(n, _):
-            zi, y = n // 8, n % 8
-            v = twice[xi * 4 + zi, y] + vec[0, 10 + xi:11 + xi] * delta[zi, y]
-            if xi in (0, 3):
-                w = pos if xi == 0 else 1.0 - pos
-                v = v + w * (yz[zi, y] + extra[zi, y])
-            t2[xi * 4 + zi, y] = v
-            return 0
-        lax.fori_loop(0, 32, over_n, 0, unroll=8)
-
-    m[...] = project(t2[...].reshape(2048, 128), tab2[0])
-    d = delta[...].reshape(512, 128)
-    m[0:512] = m[0:512] + project(d * pos, tab1[0])
-    m[1536:2048] = m[1536:2048] + project(d * (1.0 - pos), tab1[0])
-    for c in range(16):
-        t = m[128 * c:128 * c + 128].T
-        mom[c, 0:32] = t[0:32]
-        mom[c, 32:48] = t[32:48] + moma[c]
+    inflow[...] = inflow[...] + yz[...]
+    md = project(delta[...].reshape(512, 128), tabd[0])
+    ms = project(inflow[...].reshape(512, 128), tabs[0])
+    for zi in range(4):
+        at = slice(128 * zi, 128 * zi + 128)
+        t, u, v = md[at, 0:128].T, md[at, 128:144].T, ms[at].T
+        for xi in range(4):
+            c = xi * 4 + zi
+            q = moma[c, 0:32] + t[32 * xi:32 * xi + 32]
+            once = moma[c, 40:48]
+            if xi == 0:
+                q, once = q + v[0:32], once + u[0:8]
+            if xi == 3:
+                q, once = q + v[32:64], once + u[8:16]
+            mom[c, 0:32] = q
+            mom[c, 32:40] = moma[c, 32:40]
+            mom[c, 40:48] = once
 
     def load0(c):
         return mom[c, 32:40]
@@ -464,7 +471,7 @@
         out[n, 20:30] = t[20:30]
 
 
-def feq_kernel(idx, got, t2, lt, final, h2, low, s0, lo, hi, stack):
+def feq_kernel(idx, got, twice, delta, inflow, lt, vec, final, h2, low, s0, lo, hi, stack):
     def total(a, n):
         return got[0, a:a + n] + got[1, a:a + n] + got[2, a:a + n] + got[3, a:a + n]
 
@@ -485,39 +492,45 @@
             stack[8 * n:8 * n + 8, 128 * c:128 * c + 128] = v
     add = lax.dot_general(stack[...], final[0], (((0,), (0,)), ((), ())), precision=HI,
                           preferred_element_type=jnp.float32)
-    h2[...] = t2[...] + add.reshape(16, 8, 16, 128)
-
-
-def apply_k(src, dst, lt, own=False):
+    add = add.reshape(16, 8, 16, 128)
+    pos = vec[0, 14:15]
+    for c in range(16):
+        xi, zi = c // 4, c % 4
+        v = twice[c] + add[c] + vec[0, 10 + xi:11 + xi] * delta[zi]
+        if xi in (0, 3):
+            v = v + (pos if xi == 0 else 1.0 - pos) * inflow[zi]
+        h2[c] = v
+
+
+def apply_k(src, dst, lt, own=False, four=False):
     rows = slice(8, 16) if own else slice(0, 24)
 
-    def before(k, add):
-        if own:
-            return src[k, 7:15] + src[k + add, 7:15] if add else src[k, 7:15]
-        return pltpu.roll(src[k] + src[k + add] if add else src[k], 1, 0)
-
-    def after(k, add):
-        if own:
-            return src[k, 9:17] + src[k + add, 9:17] if add else src[k, 9:17]
-        return pltpu.roll(src[k] + src[k + add] if add else src[k], 23, 0)
+    def pressure(k, at):
+        return 2.0 * src[k, at] if four else src[k, at] + src[64 + k, at]
+
+    def before(load):
+        return load(slice(7, 15)) if own else pltpu.roll(load(rows), 1, 0)
+
+    def after(load):
+        return load(slice(9, 17)) if own else pltpu.roll(load(rows), 23, 0)
 
     for zi in range(4):
         u = [src[16 + j * 4 + zi, rows] for j in range(4)]
-        p = [src[j * 4 + zi, rows] + src[64 + j * 4 + zi, rows] for j in range(4)]
+        p = [pressure(j * 4 + zi, rows) for j in range(4)]
         for xi in range(4):
             du = combine(CENTRAL[xi], u)
             dp = combine(CENTRAL[xi], p)
             if xi == 0:
-                du = du - 1.5 * before(28 + zi, 0)
-                dp = dp - 1.5 * before(12 + zi, 64)
+                du = du - 1.5 * before(lambda at: src[28 + zi, at])
+                dp = dp - 1.5 * before(lambda at: pressure(12 + zi, at))
             if xi == 3:
-                du = du + 1.5 * after(16 + zi, 0)
-                dp = dp + 1.5 * after(zi, 64)
+                du = du + 1.5 * after(lambda at: src[16 + zi, at])
+                dp = dp + 1.5 * after(lambda at: pressure(zi, at))
             dst[xi * 4 + zi] = du
             dst[16 + xi * 4 + zi] = dp
     for xi in range(4):
         u = [src[48 + xi * 4 + j, rows] for j in range(4)]
-        p = [src[xi * 4 + j, rows] + src[64 + xi * 4 + j, rows] for j in range(4)]
+        p = [pressure(xi * 4 + j, rows) for j in range(4)]
         for zi in range(4):
             du = combine(CENTRAL[zi], u)
             dp = combine(CENTRAL[zi], p)
@@ -531,11 +544,8 @@
             dst[48 + xi * 4 + zi] = dp
 
     def along_y(c, _):
-        rho, u, t = src[c, rows], src[32 + c, rows], src[64 + c, rows]
-        div = dst[c] + central_y(u, lt)
-        dst[32 + c] = central_y(rho + t, lt)
-        dst[c] = div
-        dst[64 + c] = div
+        dst[c] = dst[c] + central_y(src[32 + c, rows], lt)
+        dst[32 + c] = central_y(pressure(c, rows), lt)
         return 0
     lax.fori_loop(0, 16, along_y, 0, unroll=8)
 
@@ -627,15 +637,23 @@
     for xi in range(4):
         for zi in range(4):
             acc = [zero] * 18
-            for f in range(5):
-                k = f * 16 + xi * 4 + zi
+            c = xi * 4 + zi
+            for f in range(4):
+                k = f * 16 + c
                 x = [e[k, 8:16], s[k, 8:16], t[k, 8:16]]
                 y = [ke[k, rows], x[2], kt[k, rows]]
+                z = x
+                if f == 0:
+                    last = [e[64 + c, 8:16], s[64 + c, 8:16], x[2]]
+                    z = [x[0] + last[0], x[1] + last[1], x[2] + x[2]]
                 for n, (i, j) in enumerate(PAIRS):
-                    acc[n] = acc[n] + x[i] * x[j]
-                    mixed = x[i] * y[j] if i == j else x[i] * y[j] + x[j] * y[i]
-                    acc[6 + n] = acc[6 + n] + mixed
-                    acc[12 + n] = acc[12 + n] + y[i] * y[j]
+                    v = x[i] * x[j]
+                    if f == 0:
+                        v = v + last[i] * last[j]
+                    acc[n] = acc[n] + v
+                    acc[6 + n] = acc[6 + n] + (z[i] * y[j] if i == j else z[i] * y[j] + z[j] * y[i])
+                    v = y[i] * y[j]
+                    acc[12 + n] = acc[12 + n] + (2.0 * v if f == 0 else v)
             w = WEIGHTS[xi] * WEIGHTS[zi]
             total = [a + w * b for a, b in zip(total, acc)]
     return [a * lt[22:23] for a in total]
@@ -655,7 +673,7 @@
         return 0
     lax.fori_loop(0, 80, over_k, 0, unroll=8)
     apply_k(e, ke, lt, own)
-    apply_k(t, kt, lt, own)
+    apply_k(t, kt, lt, own, four=True)
     products = coarse_products(co, lt) + fine_products(e, s, t, ke, kt, lt, own)
     rows = [jnp.sum(p, axis=0, keepdims=True) for p in products] + [jnp.zeros((3, 128), jnp.float32)]
     total = jnp.sum(jnp.concatenate(rows, axis=0), axis=1, keepdims=True)
@@ -748,14 +766,26 @@
         acc, lt, r2, s2, t2, ke2, kt2, acc2, gram, co = rest
     a1, b1, a2, b2 = step_sizes(sums)
 
-    def over_k(k, _):
-        sk, tk = s[k], t[k]
+    def put(k, tk, kr):
+        sk = s[k]
         r1 = e[k] + b1 * sk - a1 * tk
         v = a1 * sk[8:16] + a2 * r1[8:16]
         acc2[k] = v if first else acc[k] + v
-        r2[k] = b2 * r1 - a2 * (ke[k] + b1 * tk - a1 * kt[k])
-        return 0
-    lax.fori_loop(0, 80, over_k, 0, unroll=4)
+        r2[k] = b2 * r1 - a2 * kr
+
+    def over_k(k, _):
+        tk = t[k]
+        kr = ke[k] + b1 * tk - a1 * kt[k]
+        put(k, tk, kr)
+        put(64 + k, tk, kr)
+        return 0
+    lax.fori_loop(0, 16, over_k, 0, unroll=4)
+
+    def rest_k(k, _):
+        tk = t[k]
+        put(k, tk, ke[k] + b1 * tk - a1 * kt[k])
+        return 0
+    lax.fori_loop(16, 64, rest_k, 0, unroll=4)
     pass_words(r2, s2, t2, ke2, kt2, co, gram, lt, own=not first)
 
 
@@ -767,11 +797,11 @@
     to[...] = t2[:, 8:16]
 
 
-def last_kernel(idx, sums, e, s, t, acc, low, h2, select, ec, out, fields, change, stack, rows):
+def last_kernel(idx, sums, e, s, t, acc, low, h2, select, split, out, fields, change, stack, rows):
     a1, b1, a2, _ = step_sizes(sums)
 
     def over_k(k, _):
-        r1 = e[k] + b1 * s[k] - a1 * t[k]
+        r1 = e[k] + b1 * s[k] - a1 * t[k % 64]
         change[pl.ds(pl.multiple_of(k * 8, 8), 8)] = acc[k] + a1 * s[k] + a2 * r1
         return 0
     lax.fori_loop(0, 80, over_k, 0, unroll=4)
@@ -786,7 +816,12 @@
             n = 8 * (k // 4)
             rows[n:n + 8, 128 * (c % 4):128 * (c % 4) + 128] = (low[5 * c + f:5 * c + f + 1] + d) * here
     fields[...] = project(rows[...], select[...]).reshape(5, 4, 8, 64)
-    add = lax.dot_general(stack[...], ec[0], (((0,), (0,)), ((), ())), precision=HI,
+    whole = stack[...]
+    d1 = whole.astype(jnp.bfloat16).astype(jnp.float32)
+    d2 = (whole - d1).astype(jnp.bfloat16).astype(jnp.float32)
+    d3 = whole - d1 - d2
+    parts = jnp.concatenate([d1, d1, d2, d1, d2, d3], axis=0).astype(jnp.bfloat16)
+    add = lax.dot_general(parts, split[0].astype(jnp.bfloat16), (((0,), (0,)), ((), ())),
                           preferred_element_type=jnp.float32).reshape(16, 8, 16, 128)
     for c in range(16):
         xi, zi = c // 4, c % 4
@@ -812,11 +847,11 @@
                     [(544, 128)] * 2, [layer, layer, (8, 8, 16, 128), (1024, 8), (1, 32, 128)])
     up, down = shifted(up, 1), shifted(down, -1)
     twice, moma, force = call(local_kernel, "local", idx, [distribution, forcing, tables["select"]],
-                              [vec, tables["tab0"], tables["tab1"]],
-                              [wide, (16, 16, 128), (4, 20, 128)], [wide, wide, (2048, 48)])
-    pay, t2 = call(moment_kernel, "moments", idx, [up, down, twice, moma, tables["mix"], lt],
-                   [vec, tables["tab2"], tables["tab1"]], [(408, 128), wide],
-                   [layer, layer, layer, (16, 48, 128), (16, 40, 128), (2048, 48), (64, 2048)])
+                              [vec, tables["tab0"], tables["tab1"], tables["tab2"]],
+                              [wide, (16, 48, 128), (4, 20, 128)], [wide, wide, (2048, 48)])
+    pay, delta, inflow = call(moment_kernel, "moments", idx, [up, down, moma, tables["mix"], lt],
+                              [vec, tables["tabd"], tables["tabs"]], [(408, 128), layer, layer],
+                              [layer, (16, 48, 128), (16, 40, 128), (64, 2048)])
     got = lax.all_gather(pay, "vel")
     (res,) = call(residual_kernel, "residual", idx, [got, force], [], [(8, 30, 128)])
     near = [[a * 8 + b for b in range(8)] for a in range(blocks)]
@@ -825,7 +860,8 @@
     own_r, to_upper, to_lower = call(pack_kernel, "pack", idx, [mine], [],
                                      [(20, 8, 128), (125, 128), (125, 128)])
     lower, upper = shifted(to_upper, 8), shifted(to_lower, -8)
-    h2, low = call(feq_kernel, "feq", idx, [got, t2, lt], [tables["final"]],
+    h2, low = call(feq_kernel, "feq", idx, [got, twice, delta, inflow, lt],
+                   [vec, tables["final"]],
                    [wide, (80, 128)], [(16, 8, 128), (4, 8, 128), (4, 8, 128), (56, 2048)])
     (quarter,) = call(window_kernel, "window", idx, [lower, own_r, upper, to_lower, to_upper, low], [],
                       [(400, 128)])
@@ -835,17 +871,18 @@
         return lax.all_to_all(gram, "space", 0, 0, axis_index_groups=far, tiled=True)
 
     win, own, part = (80, 24, 128), (80, 8, 128), (blocks, 8, 128)
+    four, own4 = (64, 24, 128), (64, 8, 128)
     co = (40, 24, 128)
     e, s, t, ke, kt, gram = call(first_pass_kernel, "pass1", idx, [quarters, lt], [],
-                                  [win] * 5 + [part], [co])
+                                  [win, win, four, four, four, part], [co])
     e, s, t, ke, kt, acc, gram = call(functools.partial(next_pass_kernel, True), "pass2", idx,
                                        [summed(gram), e, s, t, ke, kt, lt], [],
-                                       [win] * 5 + [own, part], [co])
+                                       [win, win, four, four, four, own, part], [co])
     e, s, t, acc, gram = call(third_pass_kernel, "pass3", idx,
                                [summed(gram), e, s, t, ke, kt, acc, lt], [],
-                               [own] * 4 + [part], [win, win, win, own, own, co])
+                               [own, own, own4, own, part], [win, win, four, own4, own4, co])
     out, fields = call(last_kernel, "last", idx,
-                       [summed(gram), e, s, t, acc, low, h2, tables["select"]], [tables["ec"]],
+                       [summed(gram), e, s, t, acc, low, h2, tables["select"]], [tables["split"]],
                        [(4, 8, 64, 128), (5, 4, 8, 64)], [(640, 128), (8, 2048), (160, 512)])
     return out, fields
 

time: 119 us -> 116 us (0.975)
  Pallas kernels: 33.4 us -> 31.7 us
    pallas_call x11, Pallas kernels: 33.4 us -> 31.7 us  [call(): pl.pallas_call(body, name=name, out_shape=[jax.ShapeDtypeStruct(s, jnp.fl...]
  transfers between devices with their start and end apart: 4 -> 4, of which waited for: 2 -> 2; matrix products, arithmetic and copies ran while one was open for 0% -> 0% of each run, Pallas kernels for 6% -> 7%
where the time goes in v7:
time: 116 us; the launch traced here: 115 us
  blocking collectives  64.5 us (56%)
  Pallas kernels  31.7 us (27%)
  starting transfers between devices  16.2 us (14%)
  local copies, waits for them, and re-layouts  1.29 us (1%)
    all_to_all x3, blocking collectives, summed(): lax.all_to_all(gram, 'space', 0, 0, axis_index_groups=far, tiled=True)  34.2 us
    pallas_call x11, Pallas kernels, call(): pl.pallas_call(body, name=name, out_shape=[jax.ShapeDtypeStruct(s, jnp.fl...  31.7 us
    ppermute x4, starting transfers between devices, shifted(): lax.ppermute(x, 'space', [(i, (i + by) % spaces) for i in range(spaces)])  16.2 us
    all_to_all x1, blocking collectives, on_device(): lax.all_to_all(res, 'space', 0, 0, axis_index_groups=near, tiled=True)  12.2 us
    all_gather x1, blocking collectives, on_device(): quarters = lax.all_gather(quarter, 'vel')  9.27 us
    all_gather x1, blocking collectives, on_device(): got = lax.all_gather(pay, 'vel')  8.81 us
  transfers between devices with their start and end apart: 4, of which 2 were waited for; matrix products, arithmetic and copies ran while one was open for 0% of the time, Pallas kernels for 7%

profile of v7, /device:TPU:2, one launch (start us, length us, event | category | flops | bytes accessed | tf_op | source)
XLA Modules:
  0.0 115.5 jit_solution(15060233700038067166)
XLA Ops:
  0.6 0.1 pad_add_fusion.idx
  0.7 0.0 copy-start
  0.7 1.2 %copy-done = f32[4,8,64,128]{3,2,1,0:T(8,128)S(1)} copy-done((f32[4,8,64,128]{3,2,1,0:T(8,128)S(1)}, f32[4,8,64,128]{3,2,1,0:T(8,128)}, u32[]{:S(2)}) %copy-start) | copy-done | bytes 1048600
  1.9 0.0 copy-start.1
  1.9 0.0 copy-start.2
  1.9 0.0 copy-start.8
  1.9 0.0 copy-start.9
  2.0 0.0 copy-start.10
  2.0 0.0 copy-start.11
  2.0 1.9 %rims.1 = (f32[544,128]{1,0:T(8,128)S(1)}, f32[544,128]{1,0:T(8,128)S(1)}) custom-call(s32[2]{0:T(128)S(1)} %pad_add_fusion.idx, f32[4,8,64,128]{3,2,1,0:T(8,128)S(1)} %copy-done), custom_call_target="tpu_custom_call" | custom-call | tf_op jit(solution)/shard_map/rims/pallas_call | solution.py:169
  3.9 2.0 %collective-permute-start = (f32[544,128]{1,0:T(8,128)S(1)}, f32[544,128]{1,0:T(8,128)S(1)}, u32[]{:S(2)}, u32[]{:S(2)}) collective-permute-start(f32[544,128]{1,0:T(8,128)S(1)} %get-tuple-element.33), channel_id=1, source_target_pairs={{0,1},{1,2},{2,3},{3,4},{4,5},{5,6},{6,7},{7,8},{8,9},{9,10},{10,1... | collective-permute-start | bytes 835592 | tf_op jit(solution)/shard_map/ppermute | solution.py:844
  5.8 0.0 copy-start.3
  5.9 8.1 %collective-permute-start.1 = (f32[544,128]{1,0:T(8,128)S(1)}, f32[544,128]{1,0:T(8,128)S(1)}, u32[]{:S(2)}, u32[]{:S(2)}) collective-permute-start(f32[544,128]{1,0:T(8,128)S(1)} %get-tuple-element.34), channel_id=1, source_target_pairs={{0,63},{1,0},{2,1},{3,2},{4,3},{5,4},{6,5},{7,6},{8,7},{9,8},{10,9... | collective-permute-start | bytes 835592 | tf_op jit(solution)/shard_map/ppermute | solution.py:844
  13.9 0.0 copy-done.1
  13.9 0.0 copy-done.2
  13.9 0.0 copy-done.8
  13.9 0.0 copy-done.9
  14.0 0.0 copy-done.10
  14.0 0.0 copy-done.11
  14.0 5.9 %local.1 = (f32[16,8,16,128]{3,2,1,0:T(8,128)S(1)}, f32[16,48,128]{2,1,0:T(8,128)S(1)}, f32[4,20,128]{2,1,0:T(8,128)S(1)}) custom-call(s32[2]{0:T(128)S(1)} %pad_add_fusion.idx, f32[4,8,64,128]{3,2,1,0:T(8,128)S(1)} %copy-done, f32[3,4,8,64]{3,2,1,0:T(8,128)S(1)} %copy-done.11, f32[64,512]{1,0:T(8,128)S(1)} %copy-done.2, f32[4,32,128]{2,1,0:T(8,128)S(1)} %copy-done.1, ...), custom_call_target="tpu_custom_call" | custom-call | tf_op jit(solution)/shard_map/local/pallas_call | solution.py:169
  19.9 0.6 collective-permute-done.refs_0_
  20.5 0.0 collective-permute-done.1.refs_1_
  20.5 0.0 copy-done.3
  20.5 0.0 copy-done.4
  20.5 0.0 copy-done.5
  20.5 0.0 copy-done.12
  20.5 2.6 %moments.1 = (f32[408,128]{1,0:T(8,128)S(1)}, f32[4,8,16,128]{3,2,1,0:T(8,128)S(1)}, f32[4,8,16,128]{3,2,1,0:T(8,128)S(1)}) custom-call(s32[2]{0:T(128)S(1)} %pad_add_fusion.idx, f32[544,128]{1,0:T(8,128)S(1)} %collective-permute-done.refs_0_, f32[544,128]{1,0:T(8,128)S(1)} %collective-permute-done.1.refs_1_, f32[16,48,128]{2,1,0:T(8,128)S(1)} %get-tuple-element.35.refs_2_, ...), custom_call_target="tpu_custom_call" | custom-call | tf_op jit(solution)/shard_map/moments/pallas_call | solution.py:169
  23.1 8.8 %all-gather = f32[1632,128]{1,0:T(8,128)S(1)} all-gather(f32[408,128]{1,0:T(8,128)S(1)} %get-tuple-element.36), channel_id=2, replica_groups=mesh['vel'=4,'space'=64] {'vel'}, dimensions={0}, use_global_device_ids=true | all-gather | bytes 1044480 | tf_op jit(solution)/shard_map/all_gather | solution.py:855
  31.9 0.6 residual.1
  32.4 12.2 %all_to_all.20 = f32[8,30,128]{2,1,0:T(8,128)S(1)} all-to-all(f32[8,30,128]{2,1,0:T(8,128)S(1)} %residual.1), channel_id=1, replica_groups={{0,1,2,3,4,5,6,7},{8,9,10,11,12,13,14,15},{16,17,18,19,20,21,22,23},{24..., dimensions={0} | all-to-all | bytes 245760 | tf_op jit(solution)/shard_map/all_to_all | solution.py:859
  44.7 0.0 copy-start.6
  44.7 0.6 pack.1
  45.3 0.1 collective-permute-start.2
  45.4 6.0 %collective-permute-start.3 = (f32[125,128]{1,0:T(8,128)S(1)}, f32[125,128]{1,0:T(8,128)S(1)}, u32[]{:S(2)}, u32[]{:S(2)}) collective-permute-start(f32[125,128]{1,0:T(8,128)S(1)} %get-tuple-element.40.refs_3_), channel_id=1, source_target_pairs={{0,56},{1,57},{2,58},{3,59},{4,60},{5,61},{6,62},{7,63},{8,0},{9,1... | collective-permute-start | bytes 192008 | tf_op jit(solution)/shard_map/ppermute | solution.py:844
  51.4 0.0 copy-done.6
  51.4 1.8 %feq.1 = (f32[16,8,16,128]{3,2,1,0:T(8,128)S(1)}, f32[80,128]{1,0:T(8,128)S(1)}) custom-call(s32[2]{0:T(128)S(1)} %pad_add_fusion.idx, f32[4,408,128]{2,1,0:T(8,128)S(1)} %bitcast.5, f32[16,8,16,128]{3,2,1,0:T(8,128)S(1)} %get-tuple-element.41.refs_1_, f32[4,8,16,128]{3,2,1,0:T(8,128)S(1)} %get-tuple-element.42.refs_2_, ...), custom_call_target="tpu_custom_call" | custom-call | tf_op jit(solution)/shard_map/feq/pallas_call | solution.py:169
  53.2 0.3 collective-permute-done.2.refs_0_
  53.6 0.0 collective-permute-done.3.refs_2_
  53.6 0.6 window.1
  54.2 9.3 %all-gather.1 = f32[1600,128]{1,0:T(8,128)S(1)} all-gather(f32[400,128]{1,0:T(8,128)S(1)} %window.1), channel_id=3, replica_groups=mesh['vel'=4,'space'=64] {'vel'}, dimensions={0}, use_global_device_ids=true | all-gather | bytes 1024000 | tf_op jit(solution)/shard_map/all_gather | solution.py:868
  63.4 5.1 %pass1.1 = (f32[80,24,128]{2,1,0:T(8,128)S(1)}, f32[80,24,128]{2,1,0:T(8,128)S(1)}, f32[64,24,128]{2,1,0:T(8,128)S(1)}, f32[64,24,128]{2,1,0:T(8,128)S(1)}, f32[...) custom-call(s32[2]{0:T(128)S(1)} %pad_add_fusion.idx, f32[4,400,128]{2,1,0:T(8,128)S(1)} %bitcast.6, f32[40,128]{1,0:T(8,128)S(1)} %copy-done.3), custom_call_target="tpu_custom_call" | custom-call | tf_op jit(solution)/shard_map/pass1/pallas_call | solution.py:169
  68.5 13.9 %all_to_all.21.refs_0_ = f32[8,8,128]{2,1,0:T(8,128)S(1)} all-to-all(f32[8,8,128]{2,1,0:T(8,128)S(1)} %get-tuple-element.45), channel_id=1, replica_groups={{0,8,16,24,32,40,48,56},{1,9,17,25,33,41,49,57},{2,10,18,26,34,42,50,58..., dimensions={0} | all-to-all | bytes 65536 | tf_op jit(solution)/shard_map/all_to_all | solution.py:871
  82.5 5.6 %pass2.1 = (f32[80,24,128]{2,1,0:T(8,128)S(1)}, f32[80,24,128]{2,1,0:T(8,128)S(1)}, f32[64,24,128]{2,1,0:T(8,128)S(1)}, f32[64,24,128]{2,1,0:T(8,128)S(1)}, f32[...) custom-call(s32[2]{0:T(128)S(1)} %pad_add_fusion.idx, ...), custom_call_target="tpu_custom_call" | custom-call | tf_op jit(solution)/shard_map/pass2/pallas_call | solution.py:169
  88.1 10.1 %all_to_all.22.refs_0_ = f32[8,8,128]{2,1,0:T(8,128)S(1)} all-to-all(f32[8,8,128]{2,1,0:T(8,128)S(1)} %get-tuple-element.51), channel_id=1, replica_groups={{0,8,16,24,32,40,48,56},{1,9,17,25,33,41,49,57},{2,10,18,26,34,42,50,58..., dimensions={0} | all-to-all | bytes 65536 | tf_op jit(solution)/shard_map/all_to_all | solution.py:871
  98.2 4.5 %pass3.1 = (f32[80,8,128]{2,1,0:T(8,128)S(1)}, f32[80,8,128]{2,1,0:T(8,128)S(1)}, f32[64,8,128]{2,1,0:T(8,128)S(1)}, f32[80,8,128]{2,1,0:T(8,128)S(1)}, f32[8,8,128]{2,1,0:T(8,128)S(1)}) custom-call(s32[2]{0:T(128)S(1)} %pad_add_fusion.idx, f32[8,8,128]{2,1,0:T(8,128)S(1)} %all_to_all.22.refs_0_, f32[80,24,128]{2,1,0:T(8,128)S(1)} %get-tuple-element.52.refs_1_, ...), custom_call_target="tpu_custom_call" | custom-call | tf_op jit(solution)/shard_map/pass3/pallas_call | solution.py:169
  102.7 10.1 %all_to_all.23.refs_0_ = f32[8,8,128]{2,1,0:T(8,128)S(1)} all-to-all(f32[8,8,128]{2,1,0:T(8,128)S(1)} %get-tuple-element.58), channel_id=1, replica_groups={{0,8,16,24,32,40,48,56},{1,9,17,25,33,41,49,57},{2,10,18,26,34,42,50,58..., dimensions={0} | all-to-all | bytes 65536 | tf_op jit(solution)/shard_map/all_to_all | solution.py:871
  112.9 0.0 copy-done.7
  112.9 2.6 %last.1 = (f32[4,8,64,128]{3,2,1,0:T(8,128)}, f32[5,4,8,64]{3,2,1,0:T(8,128)}) custom-call(s32[2]{0:T(128)S(1)} %pad_add_fusion.idx, f32[8,8,128]{2,1,0:T(8,128)S(1)} %all_to_all.23.refs_0_, f32[80,8,128]{2,1,0:T(8,128)S(1)} %get-tuple-element.59.refs_1_, f32[80,8,128]{2,1,0:T(8,128)S(1)} %get-tuple-element.60.refs_2_, ...), custom_call_target="tpu_custom_call" | custom-call | tf_op jit(solution)/shard_map/last/pallas_call | solution.py:169
  (5 shorter events, 0.0 us)
Async XLA Ops:
  0.7 1.2 %copy-start = (f32[4,8,64,128]{3,2,1,0:T(8,128)S(1)}, f32[4,8,64,128]{3,2,1,0:T(8,128)}, u32[]{:S(2)}) copy-start(f32[4,8,64,128]{3,2,1,0:T(8,128)} %refs_0_.3) | copy-start | bytes 3145732
  1.9 12.0 %copy-start.1 = (f32[4,32,128]{2,1,0:T(8,128)S(1)}, f32[4,32,128]{2,1,0:T(8,128)}, u32[]{:S(2)}) copy-start(f32[4,32,128]{2,1,0:T(8,128)} %constant.44.clone.refs_3_.refs_5_) | copy-start | bytes 196612
  1.9 12.0 %copy-start.2 = (f32[64,512]{1,0:T(8,128)S(1)}, f32[64,512]{1,0:T(8,128)}, u32[]{:S(2)}) copy-start(f32[64,512]{1,0:T(8,128)} %constant.54.clone.refs_2_.refs_7_) | copy-start | bytes 393220
  1.9 12.0 %copy-start.8 = (f32[4,48,128]{2,1,0:T(8,128)S(1)}, f32[4,48,128]{2,1,0:T(8,128)}, u32[]{:S(2)}) copy-start(f32[4,48,128]{2,1,0:T(8,128)} %constant.47.clone.refs_4_) | copy-start | bytes 294916
  1.9 12.0 %copy-start.9 = (f32[4,48,128]{2,1,0:T(8,128)S(1)}, f32[4,48,128]{2,1,0:T(8,128)}, u32[]{:S(2)}) copy-start(f32[4,48,128]{2,1,0:T(8,128)} %constant.46.clone.refs_5_) | copy-start | bytes 294916
  2.0 12.0 %copy-start.10 = (f32[4,48,128]{2,1,0:T(8,128)S(1)}, f32[4,48,128]{2,1,0:T(8,128)}, u32[]{:S(2)}) copy-start(f32[4,48,128]{2,1,0:T(8,128)} %constant.45.clone.refs_6_) | copy-start | bytes 294916
  2.0 12.0 %copy-start.11 = (f32[3,4,8,64]{3,2,1,0:T(8,128)S(1)}, f32[3,4,8,64]{3,2,1,0:T(8,128)}, u32[]{:S(2)}) copy-start(f32[3,4,8,64]{3,2,1,0:T(8,128)} %refs_1_.2) | copy-start | bytes 73732
  3.9 16.6 %collective-permute-start = (f32[544,128]{1,0:T(8,128)S(1)}, f32[544,128]{1,0:T(8,128)S(1)}, u32[]{:S(2)}, u32[]{:S(2)}) collective-permute-start(f32[544,128]{1,0:T(8,128)S(1)} %get-tuple-element.33), channel_id=1, source_target_pairs={{0,1},{1,2},{2,3},{3,4},{4,5},{5,6},{6,7},{7,8},{8,9},{9,10},{10,1... | collective-permute-start | bytes 835592 | tf_op jit(solution)/shard_map/ppermute | solution.py:844
  5.8 14.6 %copy-start.3 = (f32[40,128]{1,0:T(8,128)S(1)}, f32[40,128]{1,0:T(8,128)}, u32[]{:S(2)}) copy-start(f32[40,128]{1,0:T(8,128)} %constant.50.clone.refs_4_.refs_1_.refs_6_.refs_7_) | copy-start | bytes 61444
  5.9 14.6 %copy-start.4 = (f32[4,144,128]{2,1,0:T(8,128)S(1)}, f32[4,144,128]{2,1,0:T(8,128)}, u32[]{:S(2)}) copy-start(f32[4,144,128]{2,1,0:T(8,128)} %constant.52.clone.refs_6_) | copy-start | bytes 884740
  5.9 14.6 %copy-start.5 = (f32[4,64,128]{2,1,0:T(8,128)S(1)}, f32[4,64,128]{2,1,0:T(8,128)}, u32[]{:S(2)}) copy-start(f32[4,64,128]{2,1,0:T(8,128)} %constant.53.clone.refs_7_) | copy-start | bytes 393220
  5.9 14.6 %copy-start.12 = (f32[40,64]{1,0:T(8,128)S(1)}, f32[40,64]{1,0:T(8,128)}, u32[]{:S(2)}) copy-start(f32[40,64]{1,0:T(8,128)} %constant.48.clone.refs_3_) | copy-start | bytes 30724
  5.9 14.6 %collective-permute-start.1 = (f32[544,128]{1,0:T(8,128)S(1)}, f32[544,128]{1,0:T(8,128)S(1)}, u32[]{:S(2)}, u32[]{:S(2)}) collective-permute-start(f32[544,128]{1,0:T(8,128)S(1)} %get-tuple-element.34), channel_id=1, source_target_pairs={{0,63},{1,0},{2,1},{3,2},{4,3},{5,4},{6,5},{7,6},{8,7},{9,8},{10,9... | collective-permute-start | bytes 835592 | tf_op jit(solution)/shard_map/ppermute | solution.py:844
  44.7 6.7 %copy-start.6 = (f32[4,56,128]{2,1,0:T(8,128)S(1)}, f32[4,56,128]{2,1,0:T(8,128)}, u32[]{:S(2)}) copy-start(f32[4,56,128]{2,1,0:T(8,128)} %constant.49.clone.refs_6_) | copy-start | bytes 344068
  45.3 8.3 %collective-permute-start.2 = (f32[125,128]{1,0:T(8,128)S(1)}, f32[125,128]{1,0:T(8,128)S(1)}, u32[]{:S(2)}, u32[]{:S(2)}) collective-permute-start(f32[125,128]{1,0:T(8,128)S(1)} %get-tuple-element.38.refs_4_), channel_id=1, source_target_pairs={{0,8},{1,9},{2,10},{3,11},{4,12},{5,13},{6,14},{7,15},{8,16},{9,17... | collective-permute-start | bytes 192008 | tf_op jit(solution)/shard_map/ppermute | solution.py:844
  45.4 8.2 %collective-permute-start.3 = (f32[125,128]{1,0:T(8,128)S(1)}, f32[125,128]{1,0:T(8,128)S(1)}, u32[]{:S(2)}, u32[]{:S(2)}) collective-permute-start(f32[125,128]{1,0:T(8,128)S(1)} %get-tuple-element.40.refs_3_), channel_id=1, source_target_pairs={{0,56},{1,57},{2,58},{3,59},{4,60},{5,61},{6,62},{7,63},{8,0},{9,1... | collective-permute-start | bytes 192008 | tf_op jit(solution)/shard_map/ppermute | solution.py:844
  98.2 14.6 %copy-start.7 = (f32[4,48,128]{2,1,0:T(8,128)S(1)}, f32[4,48,128]{2,1,0:T(8,128)}, u32[]{:S(2)}) copy-start(f32[4,48,128]{2,1,0:T(8,128)} %constant.51.clone.refs_8_) | copy-start | bytes 294916

commit v8 on v7

--- a/solution.py
+++ b/solution.py
@@ -153,7 +153,13 @@
     rows += [entry(lambda i, q: 0.5 * D4[i][q], 0), 3.0 * (yi == 0), 3.0 * (yi == 3)]
     while len(rows) < 40:
         rows.append(np.zeros(128))
-    lanes = np.stack(rows).astype(np.float32)
+    mats = np.zeros((3, 128, 128))
+    for n, sft in enumerate(shifts):
+        mats[0, (lane + 16 * sft) % 128, lane] += rows[n]
+    for a in range(2):
+        for sft in range(-3, 4):
+            mats[1 + a, (lane + 16 * sft) % 128, lane] += rows[6 + 7 * a + sft + 3]
+    lanes = np.concatenate([np.stack(rows), mats.reshape(384, 128)]).astype(np.float32)
     return dict(vec=vec, tab2=tab2, tab1=tab1, tab0=tab0, mix=mix.astype(np.float32),
                 final=final, lanes=lanes, split=split, tabd=tabd, tabs=tabs, select=select.astype(np.float32))
 
@@ -543,44 +549,40 @@
             dst[xi * 4 + zi] = dst[xi * 4 + zi] + du
             dst[48 + xi * 4 + zi] = dp
 
-    def along_y(c, _):
-        dst[c] = dst[c] + central_y(src[32 + c, rows], lt)
-        dst[32 + c] = central_y(pressure(c, rows), lt)
-        return 0
-    lax.fori_loop(0, 16, along_y, 0, unroll=8)
+    n = 8 if own else 24
+    u = src[32:48, rows]
+    p = 2.0 * src[0:16, rows] if four else src[0:16, rows] + src[64:80, rows]
+    x = jnp.concatenate([u, p], axis=0).reshape(32 * n, 128)
+    d = exact_dot(x, lt[40:168]).reshape(32, n, 128)
+    dst[0:16] = dst[0:16] + d[0:16]
+    dst[32:48] = d[16:32]
 
 
 def two_level(r, pe, co, lt):
-    def over_f(f, _):
-        tz = [[None, None] for _ in range(4)]
+    parts = []
+    for f in range(5):
+        tz = []
         for xi in range(4):
             q = [r[f * 16 + xi * 4 + zi] for zi in range(4)]
+            tz.append([combine(RT[za], q) for za in range(2)])
+        for xa in range(2):
             for za in range(2):
-                tz[xi][za] = combine(RT[za], q)
-        for za in range(2):
-            py = []
-            for xa in range(2):
-                t = combine(RT[xa], [tz[xi][za] for xi in range(4)])
-                e0, e1 = lt[9:10] * t, lt[16:17] * t
-                for s in SHIFTS:
-                    rolled = pltpu.roll(t, (-16 * s) % 128, 1)
-                    e0 = e0 + lt[9 + s:10 + s] * rolled
-                    e1 = e1 + lt[16 + s:17 + s] * rolled
-                co[f * 8 + xa * 4 + za * 2] = e0
-                co[f * 8 + xa * 4 + za * 2 + 1] = e1
-                py.append(lt[20:21] * e0 + lt[21:22] * e1)
-            for xi in range(4):
-                v = combine(PR[xi], py)
-                for zi in range(4):
-                    if PR[zi][za] == 0.0:
-                        continue
-                    at = f * 16 + xi * 4 + zi
-                    if za == 0 or PR[zi][0] == 0.0:
-                        pe[at] = PR[zi][za] * v
-                    else:
-                        pe[at] = pe[at] + PR[zi][za] * v
-        return 0
-    lax.fori_loop(0, 5, over_f, 0)
+                parts.append(combine(RT[xa], [tz[xi][za] for xi in range(4)]))
+    both = jnp.concatenate([lt[168:296], lt[296:424]], axis=1)
+    e = exact_dot(jnp.concatenate(parts, axis=0), both)
+    for f in range(5):
+        py = [[None, None], [None, None]]
+        for xa in range(2):
+            for za in range(2):
+                n = f * 4 + xa * 2 + za
+                e0, e1 = e[24 * n:24 * n + 24, 0:128], e[24 * n:24 * n + 24, 128:256]
+                co[2 * n] = e0
+                co[2 * n + 1] = e1
+                py[za][xa] = lt[20:21] * e0 + lt[21:22] * e1
+        for xi in range(4):
+            v = [combine(PR[xi], py[za]) for za in range(2)]
+            for zi in range(4):
+                pe[f * 16 + xi * 4 + zi] = combine(PR[zi], v)
 
 
 def coarse_products(co, lt):

time: 116 us -> 113 us (0.974)
  Pallas kernels: 31.7 us -> 28.7 us
    pallas_call x11, Pallas kernels: 31.7 us -> 28.7 us  [call(): pl.pallas_call(body, name=name, out_shape=[jax.ShapeDtypeStruct(s, jnp.fl...]
where the time goes in v8:
time: 113 us; the launch traced here: 112 us
  blocking collectives  64.5 us (57%)
  Pallas kernels  28.7 us (25%)
  starting transfers between devices  16.2 us (14%)
  local copies, waits for them, and re-layouts  1.29 us (1%)
    all_to_all x3, blocking collectives, summed(): lax.all_to_all(gram, 'space', 0, 0, axis_index_groups=far, tiled=True)  34.2 us
    pallas_call x11, Pallas kernels, call(): pl.pallas_call(body, name=name, out_shape=[jax.ShapeDtypeStruct(s, jnp.fl...  28.7 us
    ppermute x4, starting transfers between devices, shifted(): lax.ppermute(x, 'space', [(i, (i + by) % spaces) for i in range(spaces)])  16.2 us
    all_to_all x1, blocking collectives, on_device(): lax.all_to_all(res, 'space', 0, 0, axis_index_groups=near, tiled=True)  12.2 us
    all_gather x1, blocking collectives, on_device(): quarters = lax.all_gather(quarter, 'vel')  9.27 us
    all_gather x1, blocking collectives, on_device(): got = lax.all_gather(pay, 'vel')  8.81 us
  transfers between devices with their start and end apart: 4, of which 2 were waited for; matrix products, arithmetic and copies ran while one was open for 0% of the time, Pallas kernels for 7%

profile of v8, /device:TPU:2, one launch (start us, length us, event | category | flops | bytes accessed | tf_op | source)
XLA Modules:
  0.0 112.4 jit_solution(3737396369702580597)
XLA Ops:
  0.6 0.1 pad_add_fusion.idx
  0.7 0.0 copy-start.1
  0.7 1.2 %copy-done.1 = f32[4,8,64,128]{3,2,1,0:T(8,128)S(1)} copy-done((f32[4,8,64,128]{3,2,1,0:T(8,128)S(1)}, f32[4,8,64,128]{3,2,1,0:T(8,128)}, u32[]{:S(2)}) %copy-start.1) | copy-done | bytes 1048600
  1.9 0.0 copy-start.2
  1.9 0.0 copy-start.3
  1.9 0.0 copy-start.8
  1.9 0.0 copy-start.9
  2.0 0.0 copy-start.10
  2.0 0.0 copy-start.11
  2.0 1.9 %rims.1 = (f32[544,128]{1,0:T(8,128)S(1)}, f32[544,128]{1,0:T(8,128)S(1)}) custom-call(s32[2]{0:T(128)S(1)} %pad_add_fusion.idx, f32[4,8,64,128]{3,2,1,0:T(8,128)S(1)} %copy-done.1), custom_call_target="tpu_custom_call" | custom-call | tf_op jit(solution)/shard_map/rims/pallas_call | solution.py:175
  3.9 2.0 %collective-permute-start = (f32[544,128]{1,0:T(8,128)S(1)}, f32[544,128]{1,0:T(8,128)S(1)}, u32[]{:S(2)}, u32[]{:S(2)}) collective-permute-start(f32[544,128]{1,0:T(8,128)S(1)} %get-tuple-element.33), channel_id=1, source_target_pairs={{0,1},{1,2},{2,3},{3,4},{4,5},{5,6},{6,7},{7,8},{8,9},{9,10},{10,1... | collective-permute-start | bytes 835592 | tf_op jit(solution)/shard_map/ppermute | solution.py:846
  5.8 0.0 copy-start
  5.9 8.1 %collective-permute-start.1 = (f32[544,128]{1,0:T(8,128)S(1)}, f32[544,128]{1,0:T(8,128)S(1)}, u32[]{:S(2)}, u32[]{:S(2)}) collective-permute-start(f32[544,128]{1,0:T(8,128)S(1)} %get-tuple-element.34), channel_id=1, source_target_pairs={{0,63},{1,0},{2,1},{3,2},{4,3},{5,4},{6,5},{7,6},{8,7},{9,8},{10,9... | collective-permute-start | bytes 835592 | tf_op jit(solution)/shard_map/ppermute | solution.py:846
  13.9 0.0 copy-done.2
  13.9 0.0 copy-done.3
  13.9 0.0 copy-done.8
  13.9 0.0 copy-done.9
  14.0 0.0 copy-done.10
  14.0 0.0 copy-done.11
  14.0 5.9 %local.1 = (f32[16,8,16,128]{3,2,1,0:T(8,128)S(1)}, f32[16,48,128]{2,1,0:T(8,128)S(1)}, f32[4,20,128]{2,1,0:T(8,128)S(1)}) custom-call(s32[2]{0:T(128)S(1)} %pad_add_fusion.idx, f32[4,8,64,128]{3,2,1,0:T(8,128)S(1)} %copy-done.1, f32[3,4,8,64]{3,2,1,0:T(8,128)S(1)} %copy-done.11, f32[64,512]{1,0:T(8,128)S(1)} %copy-done.3, f32[4,32,128]{2,1,0:T(8,128)S(1)} %copy-done.2, ...), custom_call_target="tpu_custom_call" | custom-call | tf_op jit(solution)/shard_map/local/pallas_call | solution.py:175
  19.9 0.6 collective-permute-done.refs_0_
  20.5 0.0 collective-permute-done.1.refs_1_
  20.5 0.0 copy-done
  20.5 0.0 copy-done.4
  20.5 0.0 copy-done.5
  20.5 0.0 copy-done.12
  20.5 2.6 %moments.1 = (f32[408,128]{1,0:T(8,128)S(1)}, f32[4,8,16,128]{3,2,1,0:T(8,128)S(1)}, f32[4,8,16,128]{3,2,1,0:T(8,128)S(1)}) custom-call(s32[2]{0:T(128)S(1)} %pad_add_fusion.idx, f32[544,128]{1,0:T(8,128)S(1)} %collective-permute-done.refs_0_, f32[544,128]{1,0:T(8,128)S(1)} %collective-permute-done.1.refs_1_, f32[16,48,128]{2,1,0:T(8,128)S(1)} %get-tuple-element.35.refs_2_, ...), custom_call_target="tpu_custom_call" | custom-call | tf_op jit(solution)/shard_map/moments/pallas_call | solution.py:175
  23.1 8.8 %all-gather = f32[1632,128]{1,0:T(8,128)S(1)} all-gather(f32[408,128]{1,0:T(8,128)S(1)} %get-tuple-element.36), channel_id=2, replica_groups=mesh['vel'=4,'space'=64] {'vel'}, dimensions={0}, use_global_device_ids=true | all-gather | bytes 1044480 | tf_op jit(solution)/shard_map/all_gather | solution.py:857
  31.9 0.6 residual.1
  32.4 12.2 %all_to_all.20 = f32[8,30,128]{2,1,0:T(8,128)S(1)} all-to-all(f32[8,30,128]{2,1,0:T(8,128)S(1)} %residual.1), channel_id=1, replica_groups={{0,1,2,3,4,5,6,7},{8,9,10,11,12,13,14,15},{16,17,18,19,20,21,22,23},{24..., dimensions={0} | all-to-all | bytes 245760 | tf_op jit(solution)/shard_map/all_to_all | solution.py:861
  44.7 0.0 copy-start.6
  44.7 0.6 pack.1
  45.3 0.1 collective-permute-start.2
  45.4 6.0 %collective-permute-start.3 = (f32[125,128]{1,0:T(8,128)S(1)}, f32[125,128]{1,0:T(8,128)S(1)}, u32[]{:S(2)}, u32[]{:S(2)}) collective-permute-start(f32[125,128]{1,0:T(8,128)S(1)} %get-tuple-element.40.refs_3_), channel_id=1, source_target_pairs={{0,56},{1,57},{2,58},{3,59},{4,60},{5,61},{6,62},{7,63},{8,0},{9,1... | collective-permute-start | bytes 192008 | tf_op jit(solution)/shard_map/ppermute | solution.py:846
  51.4 0.0 copy-done.6
  51.4 1.8 %feq.1 = (f32[16,8,16,128]{3,2,1,0:T(8,128)S(1)}, f32[80,128]{1,0:T(8,128)S(1)}) custom-call(s32[2]{0:T(128)S(1)} %pad_add_fusion.idx, f32[4,408,128]{2,1,0:T(8,128)S(1)} %bitcast.5, f32[16,8,16,128]{3,2,1,0:T(8,128)S(1)} %get-tuple-element.41.refs_1_, f32[4,8,16,128]{3,2,1,0:T(8,128)S(1)} %get-tuple-element.42.refs_2_, ...), custom_call_target="tpu_custom_call" | custom-call | tf_op jit(solution)/shard_map/feq/pallas_call | solution.py:175
  53.2 0.3 collective-permute-done.2.refs_0_
  53.6 0.0 collective-permute-done.3.refs_2_
  53.6 0.6 window.1
  54.2 9.3 %all-gather.1 = f32[1600,128]{1,0:T(8,128)S(1)} all-gather(f32[400,128]{1,0:T(8,128)S(1)} %window.1), channel_id=3, replica_groups=mesh['vel'=4,'space'=64] {'vel'}, dimensions={0}, use_global_device_ids=true | all-gather | bytes 1024000 | tf_op jit(solution)/shard_map/all_gather | solution.py:870
  63.4 3.9 %pass1.1 = (f32[80,24,128]{2,1,0:T(8,128)S(1)}, f32[80,24,128]{2,1,0:T(8,128)S(1)}, f32[64,24,128]{2,1,0:T(8,128)S(1)}, f32[64,24,128]{2,1,0:T(8,128)S(1)}, f32[...) custom-call(s32[2]{0:T(128)S(1)} %pad_add_fusion.idx, f32[4,400,128]{2,1,0:T(8,128)S(1)} %bitcast.6, f32[424,128]{1,0:T(8,128)S(1)} %copy-done), custom_call_target="tpu_custom_call" | custom-call | tf_op jit(solution)/shard_map/pass1/pallas_call | solution.py:175
  67.4 14.0 %all_to_all.21.refs_0_ = f32[8,8,128]{2,1,0:T(8,128)S(1)} all-to-all(f32[8,8,128]{2,1,0:T(8,128)S(1)} %get-tuple-element.45), channel_id=1, replica_groups={{0,8,16,24,32,40,48,56},{1,9,17,25,33,41,49,57},{2,10,18,26,34,42,50,58..., dimensions={0} | all-to-all | bytes 65536 | tf_op jit(solution)/shard_map/all_to_all | solution.py:873
  81.3 4.5 %pass2.1 = (f32[80,24,128]{2,1,0:T(8,128)S(1)}, f32[80,24,128]{2,1,0:T(8,128)S(1)}, f32[64,24,128]{2,1,0:T(8,128)S(1)}, f32[64,24,128]{2,1,0:T(8,128)S(1)}, f32[...) custom-call(s32[2]{0:T(128)S(1)} %pad_add_fusion.idx, ...), custom_call_target="tpu_custom_call" | custom-call | tf_op jit(solution)/shard_map/pass2/pallas_call | solution.py:175
  85.8 10.1 %all_to_all.22.refs_0_ = f32[8,8,128]{2,1,0:T(8,128)S(1)} all-to-all(f32[8,8,128]{2,1,0:T(8,128)S(1)} %get-tuple-element.51), channel_id=1, replica_groups={{0,8,16,24,32,40,48,56},{1,9,17,25,33,41,49,57},{2,10,18,26,34,42,50,58..., dimensions={0} | all-to-all | bytes 65536 | tf_op jit(solution)/shard_map/all_to_all | solution.py:873
  95.9 3.7 %pass3.1 = (f32[80,8,128]{2,1,0:T(8,128)S(1)}, f32[80,8,128]{2,1,0:T(8,128)S(1)}, f32[64,8,128]{2,1,0:T(8,128)S(1)}, f32[80,8,128]{2,1,0:T(8,128)S(1)}, f32[8,8,128]{2,1,0:T(8,128)S(1)}) custom-call(s32[2]{0:T(128)S(1)} %pad_add_fusion.idx, f32[8,8,128]{2,1,0:T(8,128)S(1)} %all_to_all.22.refs_0_, f32[80,24,128]{2,1,0:T(8,128)S(1)} %get-tuple-element.52.refs_1_, ...), custom_call_target="tpu_custom_call" | custom-call | tf_op jit(solution)/shard_map/pass3/pallas_call | solution.py:175
  99.6 10.1 %all_to_all.23.refs_0_ = f32[8,8,128]{2,1,0:T(8,128)S(1)} all-to-all(f32[8,8,128]{2,1,0:T(8,128)S(1)} %get-tuple-element.58), channel_id=1, replica_groups={{0,8,16,24,32,40,48,56},{1,9,17,25,33,41,49,57},{2,10,18,26,34,42,50,58..., dimensions={0} | all-to-all | bytes 65536 | tf_op jit(solution)/shard_map/all_to_all | solution.py:873
  109.8 0.0 copy-done.7
  109.8 2.6 %last.1 = (f32[4,8,64,128]{3,2,1,0:T(8,128)}, f32[5,4,8,64]{3,2,1,0:T(8,128)}) custom-call(s32[2]{0:T(128)S(1)} %pad_add_fusion.idx, f32[8,8,128]{2,1,0:T(8,128)S(1)} %all_to_all.23.refs_0_, f32[80,8,128]{2,1,0:T(8,128)S(1)} %get-tuple-element.59.refs_1_, f32[80,8,128]{2,1,0:T(8,128)S(1)} %get-tuple-element.60.refs_2_, ...), custom_call_target="tpu_custom_call" | custom-call | tf_op jit(solution)/shard_map/last/pallas_call | solution.py:175
  (5 shorter events, 0.0 us)
Async XLA Ops:
  0.7 1.2 %copy-start.1 = (f32[4,8,64,128]{3,2,1,0:T(8,128)S(1)}, f32[4,8,64,128]{3,2,1,0:T(8,128)}, u32[]{:S(2)}) copy-start(f32[4,8,64,128]{3,2,1,0:T(8,128)} %refs_0_.3) | copy-start | bytes 3145732
  1.9 12.0 %copy-start.2 = (f32[4,32,128]{2,1,0:T(8,128)S(1)}, f32[4,32,128]{2,1,0:T(8,128)}, u32[]{:S(2)}) copy-start(f32[4,32,128]{2,1,0:T(8,128)} %constant.44.clone.refs_3_.refs_5_) | copy-start | bytes 196612
  1.9 12.0 %copy-start.3 = (f32[64,512]{1,0:T(8,128)S(1)}, f32[64,512]{1,0:T(8,128)}, u32[]{:S(2)}) copy-start(f32[64,512]{1,0:T(8,128)} %constant.54.clone.refs_2_.refs_7_) | copy-start | bytes 393220
  1.9 12.0 %copy-start.8 = (f32[4,48,128]{2,1,0:T(8,128)S(1)}, f32[4,48,128]{2,1,0:T(8,128)}, u32[]{:S(2)}) copy-start(f32[4,48,128]{2,1,0:T(8,128)} %constant.47.clone.refs_4_) | copy-start | bytes 294916
  1.9 12.0 %copy-start.9 = (f32[4,48,128]{2,1,0:T(8,128)S(1)}, f32[4,48,128]{2,1,0:T(8,128)}, u32[]{:S(2)}) copy-start(f32[4,48,128]{2,1,0:T(8,128)} %constant.46.clone.refs_5_) | copy-start | bytes 294916
  2.0 12.0 %copy-start.10 = (f32[4,48,128]{2,1,0:T(8,128)S(1)}, f32[4,48,128]{2,1,0:T(8,128)}, u32[]{:S(2)}) copy-start(f32[4,48,128]{2,1,0:T(8,128)} %constant.45.clone.refs_6_) | copy-start | bytes 294916
  2.0 12.0 %copy-start.11 = (f32[3,4,8,64]{3,2,1,0:T(8,128)S(1)}, f32[3,4,8,64]{3,2,1,0:T(8,128)}, u32[]{:S(2)}) copy-start(f32[3,4,8,64]{3,2,1,0:T(8,128)} %refs_1_.2) | copy-start | bytes 73732
  3.9 16.6 %collective-permute-start = (f32[544,128]{1,0:T(8,128)S(1)}, f32[544,128]{1,0:T(8,128)S(1)}, u32[]{:S(2)}, u32[]{:S(2)}) collective-permute-start(f32[544,128]{1,0:T(8,128)S(1)} %get-tuple-element.33), channel_id=1, source_target_pairs={{0,1},{1,2},{2,3},{3,4},{4,5},{5,6},{6,7},{7,8},{8,9},{9,10},{10,1... | collective-permute-start | bytes 835592 | tf_op jit(solution)/shard_map/ppermute | solution.py:846
  5.8 14.6 %copy-start = (f32[424,128]{1,0:T(8,128)S(1)}, f32[424,128]{1,0:T(8,128)}, u32[]{:S(2)}) copy-start(f32[424,128]{1,0:T(8,128)} %constant.50.clone.refs_4_.refs_1_.refs_6_.refs_7_) | copy-start | bytes 651268
  5.9 14.6 %copy-start.4 = (f32[4,144,128]{2,1,0:T(8,128)S(1)}, f32[4,144,128]{2,1,0:T(8,128)}, u32[]{:S(2)}) copy-start(f32[4,144,128]{2,1,0:T(8,128)} %constant.52.clone.refs_6_) | copy-start | bytes 884740
  5.9 14.6 %copy-start.5 = (f32[4,64,128]{2,1,0:T(8,128)S(1)}, f32[4,64,128]{2,1,0:T(8,128)}, u32[]{:S(2)}) copy-start(f32[4,64,128]{2,1,0:T(8,128)} %constant.53.clone.refs_7_) | copy-start | bytes 393220
  5.9 14.6 %copy-start.12 = (f32[40,64]{1,0:T(8,128)S(1)}, f32[40,64]{1,0:T(8,128)}, u32[]{:S(2)}) copy-start(f32[40,64]{1,0:T(8,128)} %constant.48.clone.refs_3_) | copy-start | bytes 30724
  5.9 14.6 %collective-permute-start.1 = (f32[544,128]{1,0:T(8,128)S(1)}, f32[544,128]{1,0:T(8,128)S(1)}, u32[]{:S(2)}, u32[]{:S(2)}) collective-permute-start(f32[544,128]{1,0:T(8,128)S(1)} %get-tuple-element.34), channel_id=1, source_target_pairs={{0,63},{1,0},{2,1},{3,2},{4,3},{5,4},{6,5},{7,6},{8,7},{9,8},{10,9... | collective-permute-start | bytes 835592 | tf_op jit(solution)/shard_map/ppermute | solution.py:846
  44.7 6.7 %copy-start.6 = (f32[4,56,128]{2,1,0:T(8,128)S(1)}, f32[4,56,128]{2,1,0:T(8,128)}, u32[]{:S(2)}) copy-start(f32[4,56,128]{2,1,0:T(8,128)} %constant.49.clone.refs_6_) | copy-start | bytes 344068
  45.3 8.3 %collective-permute-start.2 = (f32[125,128]{1,0:T(8,128)S(1)}, f32[125,128]{1,0:T(8,128)S(1)}, u32[]{:S(2)}, u32[]{:S(2)}) collective-permute-start(f32[125,128]{1,0:T(8,128)S(1)} %get-tuple-element.38.refs_4_), channel_id=1, source_target_pairs={{0,8},{1,9},{2,10},{3,11},{4,12},{5,13},{6,14},{7,15},{8,16},{9,17... | collective-permute-start | bytes 192008 | tf_op jit(solution)/shard_map/ppermute | solution.py:846
  45.4 8.2 %collective-permute-start.3 = (f32[125,128]{1,0:T(8,128)S(1)}, f32[125,128]{1,0:T(8,128)S(1)}, u32[]{:S(2)}, u32[]{:S(2)}) collective-permute-start(f32[125,128]{1,0:T(8,128)S(1)} %get-tuple-element.40.refs_3_), channel_id=1, source_target_pairs={{0,56},{1,57},{2,58},{3,59},{4,60},{5,61},{6,62},{7,63},{8,0},{9,1... | collective-permute-start | bytes 192008 | tf_op jit(solution)/shard_map/ppermute | solution.py:846
  95.9 13.9 %copy-start.7 = (f32[4,48,128]{2,1,0:T(8,128)S(1)}, f32[4,48,128]{2,1,0:T(8,128)}, u32[]{:S(2)}) copy-start(f32[4,48,128]{2,1,0:T(8,128)} %constant.51.clone.refs_8_) | copy-start | bytes 294916

commit v9 on v8

--- a/solution.py
+++ b/solution.py
@@ -377,24 +377,17 @@
     return total
 
 
-def one_sided(load, low, high, c, lt):
+def one_sided(load, low, high, c, cy, lt):
     xi, zi = c // 4, c % 4
     q = load(c)
     cx = combine([0.5 * v for v in D4[xi]], [load(j * 4 + zi) for j in range(4)])
     px = cx + 3.0 * (q - low(zi)) if xi == 0 else cx
     mx = cx + 3.0 * (high(zi) - q) if xi == 3 else cx
-    cy = lt[32:33] * q
-    for n, s in enumerate(SHIFTS):
-        r = pltpu.roll(q, (-16 * s) % 128, 1)
-        cy = cy + lt[26 + n:27 + n] * r
-        if s == -1:
-            py = lt[33:34] * (q - r)
-        if s == 1:
-            my = lt[34:35] * (r - q)
+    w = 0.5 * (lt[33:34] * (q - pltpu.roll(q, 16, 1)) - lt[34:35] * (pltpu.roll(q, 112, 1) - q))
     cz = combine([0.5 * v for v in D4[zi]], [load(xi * 4 + j) for j in range(4)])
     pz = cz + 3.0 * (q - z_before(load(xi * 4 + 3), lt)) if zi == 0 else cz
     mz = cz + 3.0 * (z_after(load(xi * 4), lt) - q) if zi == 3 else cz
-    return [px, mx, cy + py, cy + my, pz, mz]
+    return [px, mx, cy + w, cy - w, pz, mz]
 
 
 CENTRAL = [[0.0 if i == j else 0.5 * D4[i][j] for j in range(4)] for i in range(4)]
@@ -434,9 +427,10 @@
     def load0(c):
         return mom[c, 32:40]
 
+    cy = exact_dot(mom[:, 32:40].reshape(128, 128), lt[40:168])
     for c in range(16):
         six = one_sided(load0, lambda zi: up[512 + 8 * zi:520 + 8 * zi],
-                        lambda zi: down[512 + 8 * zi:520 + 8 * zi], c, lt)
+                        lambda zi: down[512 + 8 * zi:520 + 8 * zi], c, cy[8 * c:8 * c + 8], lt)
         at = slice(128 * c, 128 * c + 128)
         stack[0:16, at] = mom[c, 32:48]
         for n in range(6):
@@ -446,10 +440,11 @@
         at = slice(128 * c, 128 * c + 128)
         full[c, 0:32] = mom[c, 0:32] + add[0:32, at]
         full[c, 32:40] = add[32:40, at]
+    cy = exact_dot(full[:, 16:24].reshape(128, 128), lt[40:168])
     for c in range(16):
         xi, zi = c // 4, c % 4
         r = combine(CENTRAL[xi], [full[j * 4 + zi, 8:16] for j in range(4)])
-        r = r + central_y(full[c, 16:24], lt)
+        r = r + cy[8 * c:8 * c + 8]
         r = r + combine(CENTRAL[zi], [full[xi * 4 + j, 24:32] for j in range(4)])
         if zi == 0:
             r = r - 1.5 * z_before(full[xi * 4 + 3, 24:32], lt)
@@ -491,9 +486,11 @@
         hi[zi, 0:5] = total(388 + 5 * zi, 5)
     low[...] = total(128, 80)
     pad = jnp.zeros((3, 128), jnp.float32)
+    cy = exact_dot(s0[...].reshape(128, 128), lt[40:168])
     for c in range(16):
         z = jnp.concatenate([0.2 * total(288 + 5 * c, 5), pad], axis=0) + 0.16 * s0[c]
-        six = one_sided(lambda k: s0[k], lambda zi: lo[zi], lambda zi: hi[zi], c, lt)
+        six = one_sided(lambda k: s0[k], lambda zi: lo[zi], lambda zi: hi[zi], c,
+                        cy[8 * c:8 * c + 8], lt)
         for n, v in enumerate([z] + six):
             stack[8 * n:8 * n + 8, 128 * c:128 * c + 128] = v
     add = lax.dot_general(stack[...], final[0], (((0,), (0,)), ((), ())), precision=HI,
@@ -787,7 +784,7 @@
         tk = t[k]
         put(k, tk, ke[k] + b1 * tk - a1 * kt[k])
         return 0
-    lax.fori_loop(16, 64, rest_k, 0, unroll=4)
+    lax.fori_loop(16, 64, rest_k, 0, unroll=8)
     pass_words(r2, s2, t2, ke2, kt2, co, gram, lt, own=not first)
 
 
@@ -806,7 +803,7 @@
         r1 = e[k] + b1 * s[k] - a1 * t[k % 64]
         change[pl.ds(pl.multiple_of(k * 8, 8), 8)] = acc[k] + a1 * s[k] + a2 * r1
         return 0
-    lax.fori_loop(0, 80, over_k, 0, unroll=4)
+    lax.fori_loop(0, 80, over_k, 0, unroll=16)
     z = idx[1]
     stack[...] = jnp.zeros_like(stack)
     here = row_of_y()

time: 113 us -> 113 us (level)
  no operation moved by 1% of the time
where the time goes in v9:
time: 113 us; the launch traced here: 112 us
  blocking collectives  64.5 us (57%)
  Pallas kernels  28.9 us (26%)
  starting transfers between devices  16.2 us (14%)
  local copies, waits for them, and re-layouts  1.29 us (1%)
    all_to_all x3, blocking collectives, summed(): lax.all_to_all(gram, 'space', 0, 0, axis_index_groups=far, tiled=True)  34.2 us
    pallas_call x11, Pallas kernels, call(): pl.pallas_call(body, name=name, out_shape=[jax.ShapeDtypeStruct(s, jnp.fl...  28.9 us
    ppermute x4, starting transfers between devices, shifted(): lax.ppermute(x, 'space', [(i, (i + by) % spaces) for i in range(spaces)])  16.2 us
    all_to_all x1, blocking collectives, on_device(): lax.all_to_all(res, 'space', 0, 0, axis_index_groups=near, tiled=True)  12.2 us
    all_gather x1, blocking collectives, on_device(): quarters = lax.all_gather(quarter, 'vel')  9.27 us
    all_gather x1, blocking collectives, on_device(): got = lax.all_gather(pay, 'vel')  8.81 us
  transfers between devices with their start and end apart: 4, of which 2 were waited for; matrix products, arithmetic and copies ran while one was open for 0% of the time, Pallas kernels for 7%

profile of v9, /device:TPU:2, one launch (start us, length us, event | category | flops | bytes accessed | tf_op | source)
XLA Modules:
  0.0 112.5 jit_solution(1453579242880571498)
XLA Ops:
  0.6 0.1 pad_add_fusion.idx
  0.7 0.0 copy-start.1
  0.7 1.2 %copy-done.1 = f32[4,8,64,128]{3,2,1,0:T(8,128)S(1)} copy-done((f32[4,8,64,128]{3,2,1,0:T(8,128)S(1)}, f32[4,8,64,128]{3,2,1,0:T(8,128)}, u32[]{:S(2)}) %copy-start.1) | copy-done | bytes 1048600
  1.9 0.0 copy-start.2
  1.9 0.0 copy-start.3
  1.9 0.0 copy-start.8
  1.9 0.0 copy-start.9
  2.0 0.0 copy-start.10
  2.0 0.0 copy-start.11
  2.0 1.9 %rims.1 = (f32[544,128]{1,0:T(8,128)S(1)}, f32[544,128]{1,0:T(8,128)S(1)}) custom-call(s32[2]{0:T(128)S(1)} %pad_add_fusion.idx, f32[4,8,64,128]{3,2,1,0:T(8,128)S(1)} %copy-done.1), custom_call_target="tpu_custom_call" | custom-call | tf_op jit(solution)/shard_map/rims/pallas_call | solution.py:175
  3.9 2.0 %collective-permute-start = (f32[544,128]{1,0:T(8,128)S(1)}, f32[544,128]{1,0:T(8,128)S(1)}, u32[]{:S(2)}, u32[]{:S(2)}) collective-permute-start(f32[544,128]{1,0:T(8,128)S(1)} %get-tuple-element.33), channel_id=1, source_target_pairs={{0,1},{1,2},{2,3},{3,4},{4,5},{5,6},{6,7},{7,8},{8,9},{9,10},{10,1... | collective-permute-start | bytes 835592 | tf_op jit(solution)/shard_map/ppermute | solution.py:843
  5.8 0.0 copy-start
  5.9 8.1 %collective-permute-start.1 = (f32[544,128]{1,0:T(8,128)S(1)}, f32[544,128]{1,0:T(8,128)S(1)}, u32[]{:S(2)}, u32[]{:S(2)}) collective-permute-start(f32[544,128]{1,0:T(8,128)S(1)} %get-tuple-element.34), channel_id=1, source_target_pairs={{0,63},{1,0},{2,1},{3,2},{4,3},{5,4},{6,5},{7,6},{8,7},{9,8},{10,9... | collective-permute-start | bytes 835592 | tf_op jit(solution)/shard_map/ppermute | solution.py:843
  13.9 0.0 copy-done.2
  13.9 0.0 copy-done.3
  13.9 0.0 copy-done.8
  13.9 0.0 copy-done.9
  14.0 0.0 copy-done.10
  14.0 0.0 copy-done.11
  14.0 5.9 %local.1 = (f32[16,8,16,128]{3,2,1,0:T(8,128)S(1)}, f32[16,48,128]{2,1,0:T(8,128)S(1)}, f32[4,20,128]{2,1,0:T(8,128)S(1)}) custom-call(s32[2]{0:T(128)S(1)} %pad_add_fusion.idx, f32[4,8,64,128]{3,2,1,0:T(8,128)S(1)} %copy-done.1, f32[3,4,8,64]{3,2,1,0:T(8,128)S(1)} %copy-done.11, f32[64,512]{1,0:T(8,128)S(1)} %copy-done.3, f32[4,32,128]{2,1,0:T(8,128)S(1)} %copy-done.2, ...), custom_call_target="tpu_custom_call" | custom-call | tf_op jit(solution)/shard_map/local/pallas_call | solution.py:175
  19.9 0.6 collective-permute-done.refs_0_
  20.5 0.0 collective-permute-done.1.refs_1_
  20.5 0.0 copy-done
  20.5 0.0 copy-done.4
  20.5 0.0 copy-done.5
  20.5 0.0 copy-done.12
  20.5 2.8 %moments.1 = (f32[408,128]{1,0:T(8,128)S(1)}, f32[4,8,16,128]{3,2,1,0:T(8,128)S(1)}, f32[4,8,16,128]{3,2,1,0:T(8,128)S(1)}) custom-call(s32[2]{0:T(128)S(1)} %pad_add_fusion.idx, f32[544,128]{1,0:T(8,128)S(1)} %collective-permute-done.refs_0_, f32[544,128]{1,0:T(8,128)S(1)} %collective-permute-done.1.refs_1_, f32[16,48,128]{2,1,0:T(8,128)S(1)} %get-tuple-element.35.refs_2_, ...), custom_call_target="tpu_custom_call" | custom-call | tf_op jit(solution)/shard_map/moments/pallas_call | solution.py:175
  23.3 8.8 %all-gather = f32[1632,128]{1,0:T(8,128)S(1)} all-gather(f32[408,128]{1,0:T(8,128)S(1)} %get-tuple-element.36), channel_id=2, replica_groups=mesh['vel'=4,'space'=64] {'vel'}, dimensions={0}, use_global_device_ids=true | all-gather | bytes 1044480 | tf_op jit(solution)/shard_map/all_gather | solution.py:854
  32.1 0.6 residual.1
  32.7 12.2 %all_to_all.20 = f32[8,30,128]{2,1,0:T(8,128)S(1)} all-to-all(f32[8,30,128]{2,1,0:T(8,128)S(1)} %residual.1), channel_id=1, replica_groups={{0,1,2,3,4,5,6,7},{8,9,10,11,12,13,14,15},{16,17,18,19,20,21,22,23},{24..., dimensions={0} | all-to-all | bytes 245760 | tf_op jit(solution)/shard_map/all_to_all | solution.py:858
  44.9 0.0 copy-start.6
  44.9 0.6 pack.1
  45.5 0.1 collective-permute-start.2
  45.6 6.0 %collective-permute-start.3 = (f32[125,128]{1,0:T(8,128)S(1)}, f32[125,128]{1,0:T(8,128)S(1)}, u32[]{:S(2)}, u32[]{:S(2)}) collective-permute-start(f32[125,128]{1,0:T(8,128)S(1)} %get-tuple-element.40.refs_3_), channel_id=1, source_target_pairs={{0,56},{1,57},{2,58},{3,59},{4,60},{5,61},{6,62},{7,63},{8,0},{9,1... | collective-permute-start | bytes 192008 | tf_op jit(solution)/shard_map/ppermute | solution.py:843
  51.6 0.0 copy-done.6
  51.7 2.0 %feq.1 = (f32[16,8,16,128]{3,2,1,0:T(8,128)S(1)}, f32[80,128]{1,0:T(8,128)S(1)}) custom-call(s32[2]{0:T(128)S(1)} %pad_add_fusion.idx, f32[4,408,128]{2,1,0:T(8,128)S(1)} %bitcast.5, f32[16,8,16,128]{3,2,1,0:T(8,128)S(1)} %get-tuple-element.41.refs_1_, f32[4,8,16,128]{3,2,1,0:T(8,128)S(1)} %get-tuple-element.42.refs_2_, ...), custom_call_target="tpu_custom_call" | custom-call | tf_op jit(solution)/shard_map/feq/pallas_call | solution.py:175
  53.7 0.2 collective-permute-done.2.refs_0_
  53.8 0.0 collective-permute-done.3.refs_2_
  53.8 0.6 window.1
  54.4 9.3 %all-gather.1 = f32[1600,128]{1,0:T(8,128)S(1)} all-gather(f32[400,128]{1,0:T(8,128)S(1)} %window.1), channel_id=3, replica_groups=mesh['vel'=4,'space'=64] {'vel'}, dimensions={0}, use_global_device_ids=true | all-gather | bytes 1024000 | tf_op jit(solution)/shard_map/all_gather | solution.py:867
  63.7 3.9 %pass1.1 = (f32[80,24,128]{2,1,0:T(8,128)S(1)}, f32[80,24,128]{2,1,0:T(8,128)S(1)}, f32[64,24,128]{2,1,0:T(8,128)S(1)}, f32[64,24,128]{2,1,0:T(8,128)S(1)}, f32[...) custom-call(s32[2]{0:T(128)S(1)} %pad_add_fusion.idx, f32[4,400,128]{2,1,0:T(8,128)S(1)} %bitcast.6, f32[424,128]{1,0:T(8,128)S(1)} %copy-done), custom_call_target="tpu_custom_call" | custom-call | tf_op jit(solution)/shard_map/pass1/pallas_call | solution.py:175
  67.6 14.0 %all_to_all.21.refs_0_ = f32[8,8,128]{2,1,0:T(8,128)S(1)} all-to-all(f32[8,8,128]{2,1,0:T(8,128)S(1)} %get-tuple-element.45), channel_id=1, replica_groups={{0,8,16,24,32,40,48,56},{1,9,17,25,33,41,49,57},{2,10,18,26,34,42,50,58..., dimensions={0} | all-to-all | bytes 65536 | tf_op jit(solution)/shard_map/all_to_all | solution.py:870
  81.6 4.4 %pass2.1 = (f32[80,24,128]{2,1,0:T(8,128)S(1)}, f32[80,24,128]{2,1,0:T(8,128)S(1)}, f32[64,24,128]{2,1,0:T(8,128)S(1)}, f32[64,24,128]{2,1,0:T(8,128)S(1)}, f32[...) custom-call(s32[2]{0:T(128)S(1)} %pad_add_fusion.idx, ...), custom_call_target="tpu_custom_call" | custom-call | tf_op jit(solution)/shard_map/pass2/pallas_call | solution.py:175
  86.0 10.1 %all_to_all.22.refs_0_ = f32[8,8,128]{2,1,0:T(8,128)S(1)} all-to-all(f32[8,8,128]{2,1,0:T(8,128)S(1)} %get-tuple-element.51), channel_id=1, replica_groups={{0,8,16,24,32,40,48,56},{1,9,17,25,33,41,49,57},{2,10,18,26,34,42,50,58..., dimensions={0} | all-to-all | bytes 65536 | tf_op jit(solution)/shard_map/all_to_all | solution.py:870
  96.1 3.7 %pass3.1 = (f32[80,8,128]{2,1,0:T(8,128)S(1)}, f32[80,8,128]{2,1,0:T(8,128)S(1)}, f32[64,8,128]{2,1,0:T(8,128)S(1)}, f32[80,8,128]{2,1,0:T(8,128)S(1)}, f32[8,8,128]{2,1,0:T(8,128)S(1)}) custom-call(s32[2]{0:T(128)S(1)} %pad_add_fusion.idx, f32[8,8,128]{2,1,0:T(8,128)S(1)} %all_to_all.22.refs_0_, f32[80,24,128]{2,1,0:T(8,128)S(1)} %get-tuple-element.52.refs_1_, ...), custom_call_target="tpu_custom_call" | custom-call | tf_op jit(solution)/shard_map/pass3/pallas_call | solution.py:175
  99.8 10.1 %all_to_all.23.refs_0_ = f32[8,8,128]{2,1,0:T(8,128)S(1)} all-to-all(f32[8,8,128]{2,1,0:T(8,128)S(1)} %get-tuple-element.58), channel_id=1, replica_groups={{0,8,16,24,32,40,48,56},{1,9,17,25,33,41,49,57},{2,10,18,26,34,42,50,58..., dimensions={0} | all-to-all | bytes 65536 | tf_op jit(solution)/shard_map/all_to_all | solution.py:870
  110.0 0.0 copy-done.7
  110.0 2.5 %last.1 = (f32[4,8,64,128]{3,2,1,0:T(8,128)}, f32[5,4,8,64]{3,2,1,0:T(8,128)}) custom-call(s32[2]{0:T(128)S(1)} %pad_add_fusion.idx, f32[8,8,128]{2,1,0:T(8,128)S(1)} %all_to_all.23.refs_0_, f32[80,8,128]{2,1,0:T(8,128)S(1)} %get-tuple-element.59.refs_1_, f32[80,8,128]{2,1,0:T(8,128)S(1)} %get-tuple-element.60.refs_2_, ...), custom_call_target="tpu_custom_call" | custom-call | tf_op jit(solution)/shard_map/last/pallas_call | solution.py:175
  (5 shorter events, 0.0 us)
Async XLA Ops:
  0.7 1.2 %copy-start.1 = (f32[4,8,64,128]{3,2,1,0:T(8,128)S(1)}, f32[4,8,64,128]{3,2,1,0:T(8,128)}, u32[]{:S(2)}) copy-start(f32[4,8,64,128]{3,2,1,0:T(8,128)} %refs_0_.3) | copy-start | bytes 3145732
  1.9 12.0 %copy-start.2 = (f32[4,32,128]{2,1,0:T(8,128)S(1)}, f32[4,32,128]{2,1,0:T(8,128)}, u32[]{:S(2)}) copy-start(f32[4,32,128]{2,1,0:T(8,128)} %constant.44.clone.refs_3_.refs_5_) | copy-start | bytes 196612
  1.9 12.0 %copy-start.3 = (f32[64,512]{1,0:T(8,128)S(1)}, f32[64,512]{1,0:T(8,128)}, u32[]{:S(2)}) copy-start(f32[64,512]{1,0:T(8,128)} %constant.54.clone.refs_2_.refs_7_) | copy-start | bytes 393220
  1.9 12.0 %copy-start.8 = (f32[4,48,128]{2,1,0:T(8,128)S(1)}, f32[4,48,128]{2,1,0:T(8,128)}, u32[]{:S(2)}) copy-start(f32[4,48,128]{2,1,0:T(8,128)} %constant.47.clone.refs_4_) | copy-start | bytes 294916
  1.9 12.0 %copy-start.9 = (f32[4,48,128]{2,1,0:T(8,128)S(1)}, f32[4,48,128]{2,1,0:T(8,128)}, u32[]{:S(2)}) copy-start(f32[4,48,128]{2,1,0:T(8,128)} %constant.46.clone.refs_5_) | copy-start | bytes 294916
  2.0 12.0 %copy-start.10 = (f32[4,48,128]{2,1,0:T(8,128)S(1)}, f32[4,48,128]{2,1,0:T(8,128)}, u32[]{:S(2)}) copy-start(f32[4,48,128]{2,1,0:T(8,128)} %constant.45.clone.refs_6_) | copy-start | bytes 294916
  2.0 12.0 %copy-start.11 = (f32[3,4,8,64]{3,2,1,0:T(8,128)S(1)}, f32[3,4,8,64]{3,2,1,0:T(8,128)}, u32[]{:S(2)}) copy-start(f32[3,4,8,64]{3,2,1,0:T(8,128)} %refs_1_.2) | copy-start | bytes 73732
  3.9 16.6 %collective-permute-start = (f32[544,128]{1,0:T(8,128)S(1)}, f32[544,128]{1,0:T(8,128)S(1)}, u32[]{:S(2)}, u32[]{:S(2)}) collective-permute-start(f32[544,128]{1,0:T(8,128)S(1)} %get-tuple-element.33), channel_id=1, source_target_pairs={{0,1},{1,2},{2,3},{3,4},{4,5},{5,6},{6,7},{7,8},{8,9},{9,10},{10,1... | collective-permute-start | bytes 835592 | tf_op jit(solution)/shard_map/ppermute | solution.py:843
  5.8 14.6 %copy-start = (f32[424,128]{1,0:T(8,128)S(1)}, f32[424,128]{1,0:T(8,128)}, u32[]{:S(2)}) copy-start(f32[424,128]{1,0:T(8,128)} %constant.50.clone.refs_4_.refs_1_.refs_6_.refs_7_) | copy-start | bytes 651268
  5.9 14.6 %copy-start.4 = (f32[4,144,128]{2,1,0:T(8,128)S(1)}, f32[4,144,128]{2,1,0:T(8,128)}, u32[]{:S(2)}) copy-start(f32[4,144,128]{2,1,0:T(8,128)} %constant.52.clone.refs_6_) | copy-start | bytes 884740
  5.9 14.6 %copy-start.5 = (f32[4,64,128]{2,1,0:T(8,128)S(1)}, f32[4,64,128]{2,1,0:T(8,128)}, u32[]{:S(2)}) copy-start(f32[4,64,128]{2,1,0:T(8,128)} %constant.53.clone.refs_7_) | copy-start | bytes 393220
  5.9 14.6 %copy-start.12 = (f32[40,64]{1,0:T(8,128)S(1)}, f32[40,64]{1,0:T(8,128)}, u32[]{:S(2)}) copy-start(f32[40,64]{1,0:T(8,128)} %constant.48.clone.refs_3_) | copy-start | bytes 30724
  5.9 14.6 %collective-permute-start.1 = (f32[544,128]{1,0:T(8,128)S(1)}, f32[544,128]{1,0:T(8,128)S(1)}, u32[]{:S(2)}, u32[]{:S(2)}) collective-permute-start(f32[544,128]{1,0:T(8,128)S(1)} %get-tuple-element.34), channel_id=1, source_target_pairs={{0,63},{1,0},{2,1},{3,2},{4,3},{5,4},{6,5},{7,6},{8,7},{9,8},{10,9... | collective-permute-start | bytes 835592 | tf_op jit(solution)/shard_map/ppermute | solution.py:843
  44.9 6.7 %copy-start.6 = (f32[4,56,128]{2,1,0:T(8,128)S(1)}, f32[4,56,128]{2,1,0:T(8,128)}, u32[]{:S(2)}) copy-start(f32[4,56,128]{2,1,0:T(8,128)} %constant.49.clone.refs_6_) | copy-start | bytes 344068
  45.5 8.3 %collective-permute-start.2 = (f32[125,128]{1,0:T(8,128)S(1)}, f32[125,128]{1,0:T(8,128)S(1)}, u32[]{:S(2)}, u32[]{:S(2)}) collective-permute-start(f32[125,128]{1,0:T(8,128)S(1)} %get-tuple-element.38.refs_4_), channel_id=1, source_target_pairs={{0,8},{1,9},{2,10},{3,11},{4,12},{5,13},{6,14},{7,15},{8,16},{9,17... | collective-permute-start | bytes 192008 | tf_op jit(solution)/shard_map/ppermute | solution.py:843
  45.6 8.2 %collective-permute-start.3 = (f32[125,128]{1,0:T(8,128)S(1)}, f32[125,128]{1,0:T(8,128)S(1)}, u32[]{:S(2)}, u32[]{:S(2)}) collective-permute-start(f32[125,128]{1,0:T(8,128)S(1)} %get-tuple-element.40.refs_3_), channel_id=1, source_target_pairs={{0,56},{1,57},{2,58},{3,59},{4,60},{5,61},{6,62},{7,63},{8,0},{9,1... | collective-permute-start | bytes 192008 | tf_op jit(solution)/shard_map/ppermute | solution.py:843
  96.1 13.8 %copy-start.7 = (f32[4,48,128]{2,1,0:T(8,128)S(1)}, f32[4,48,128]{2,1,0:T(8,128)}, u32[]{:S(2)}) copy-start(f32[4,48,128]{2,1,0:T(8,128)} %constant.51.clone.refs_8_) | copy-start | bytes 294916

commit v10 on v9

--- a/solution.py
+++ b/solution.py
@@ -427,10 +427,10 @@
     def load0(c):
         return mom[c, 32:40]
 
-    cy = exact_dot(mom[:, 32:40].reshape(128, 128), lt[40:168])
     for c in range(16):
         six = one_sided(load0, lambda zi: up[512 + 8 * zi:520 + 8 * zi],
-                        lambda zi: down[512 + 8 * zi:520 + 8 * zi], c, cy[8 * c:8 * c + 8], lt)
+                        lambda zi: down[512 + 8 * zi:520 + 8 * zi], c,
+                        central_y(mom[c, 32:40], lt), lt)
         at = slice(128 * c, 128 * c + 128)
         stack[0:16, at] = mom[c, 32:48]
         for n in range(6):
@@ -440,11 +440,10 @@
         at = slice(128 * c, 128 * c + 128)
         full[c, 0:32] = mom[c, 0:32] + add[0:32, at]
         full[c, 32:40] = add[32:40, at]
-    cy = exact_dot(full[:, 16:24].reshape(128, 128), lt[40:168])
     for c in range(16):
         xi, zi = c // 4, c % 4
         r = combine(CENTRAL[xi], [full[j * 4 + zi, 8:16] for j in range(4)])
-        r = r + cy[8 * c:8 * c + 8]
+        r = r + central_y(full[c, 16:24], lt)
         r = r + combine(CENTRAL[zi], [full[xi * 4 + j, 24:32] for j in range(4)])
         if zi == 0:
             r = r - 1.5 * z_before(full[xi * 4 + 3, 24:32], lt)
@@ -678,7 +677,7 @@
     total = jnp.sum(jnp.concatenate(rows, axis=0), axis=1, keepdims=True)
     line = jnp.sum(jnp.where(diagonal(), total, 0.0), axis=0, keepdims=True)
     for n in range(gram.shape[0]):
-        gram[n] = jnp.broadcast_to(line, (8, 128))
+        gram[n] = line
 
 
 def pack_kernel(idx, mine, own, to_upper, to_lower):
@@ -869,7 +868,7 @@
     def summed(gram):
         return lax.all_to_all(gram, "space", 0, 0, axis_index_groups=far, tiled=True)
 
-    win, own, part = (80, 24, 128), (80, 8, 128), (blocks, 8, 128)
+    win, own, part = (80, 24, 128), (80, 8, 128), (blocks, 1, 128)
     four, own4 = (64, 24, 128), (64, 8, 128)
     co = (40, 24, 128)
     e, s, t, ke, kt, gram = call(first_pass_kernel, "pass1", idx, [quarters, lt], [],

time: 113 us -> 112 us (level)
  no operation moved by 1% of the time
where the time goes in v10:
time: 112 us
  blocking collectives  64.2 us (57%)
  Pallas kernels  28.6 us (26%)
  starting transfers between devices  16.2 us (14%)
  local copies, waits for them, and re-layouts  1.29 us (1%)
    all_to_all x3, blocking collectives, summed(): lax.all_to_all(gram, 'space', 0, 0, axis_index_groups=far, tiled=True)  33.9 us
    pallas_call x11, Pallas kernels, call(): pl.pallas_call(body, name=name, out_shape=[jax.ShapeDtypeStruct(s, jnp.fl...  28.6 us
    ppermute x4, starting transfers between devices, shifted(): lax.ppermute(x, 'space', [(i, (i + by) % spaces) for i in range(spaces)])  16.2 us
    all_to_all x1, blocking collectives, on_device(): lax.all_to_all(res, 'space', 0, 0, axis_index_groups=near, tiled=True)  12.2 us
    all_gather x1, blocking collectives, on_device(): quarters = lax.all_gather(quarter, 'vel')  9.27 us
    all_gather x1, blocking collectives, on_device(): got = lax.all_gather(pay, 'vel')  8.81 us
  transfers between devices with their start and end apart: 4, of which 2 were waited for; matrix products, arithmetic and copies ran while one was open for 0% of the time, Pallas kernels for 7%

profile of v10, /device:TPU:2, one launch (start us, length us, event | category | flops | bytes accessed | tf_op | source)
XLA Modules:
  0.0 111.9 jit_solution(9627424876380705815)
XLA Ops:
  0.6 0.1 pad_add_fusion.idx
  0.7 0.0 copy-start.1
  0.7 1.2 %copy-done.1 = f32[4,8,64,128]{3,2,1,0:T(8,128)S(1)} copy-done((f32[4,8,64,128]{3,2,1,0:T(8,128)S(1)}, f32[4,8,64,128]{3,2,1,0:T(8,128)}, u32[]{:S(2)}) %copy-start.1) | copy-done | bytes 1048600
  1.9 0.0 copy-start.2
  1.9 0.0 copy-start.3
  1.9 0.0 copy-start.8
  1.9 0.0 copy-start.9
  2.0 0.0 copy-start.10
  2.0 0.0 copy-start.11
  2.0 1.9 %rims.1 = (f32[544,128]{1,0:T(8,128)S(1)}, f32[544,128]{1,0:T(8,128)S(1)}) custom-call(s32[2]{0:T(128)S(1)} %pad_add_fusion.idx, f32[4,8,64,128]{3,2,1,0:T(8,128)S(1)} %copy-done.1), custom_call_target="tpu_custom_call" | custom-call | tf_op jit(solution)/shard_map/rims/pallas_call | solution.py:175
  3.9 2.0 %collective-permute-start = (f32[544,128]{1,0:T(8,128)S(1)}, f32[544,128]{1,0:T(8,128)S(1)}, u32[]{:S(2)}, u32[]{:S(2)}) collective-permute-start(f32[544,128]{1,0:T(8,128)S(1)} %get-tuple-element.33), channel_id=1, source_target_pairs={{0,1},{1,2},{2,3},{3,4},{4,5},{5,6},{6,7},{7,8},{8,9},{9,10},{10,1... | collective-permute-start | bytes 835592 | tf_op jit(solution)/shard_map/ppermute | solution.py:842
  5.9 0.0 copy-start.4
  5.9 8.1 %collective-permute-start.1 = (f32[544,128]{1,0:T(8,128)S(1)}, f32[544,128]{1,0:T(8,128)S(1)}, u32[]{:S(2)}, u32[]{:S(2)}) collective-permute-start(f32[544,128]{1,0:T(8,128)S(1)} %get-tuple-element.34), channel_id=1, source_target_pairs={{0,63},{1,0},{2,1},{3,2},{4,3},{5,4},{6,5},{7,6},{8,7},{9,8},{10,9... | collective-permute-start | bytes 835592 | tf_op jit(solution)/shard_map/ppermute | solution.py:842
  13.9 0.0 copy-done.2
  13.9 0.0 copy-done.3
  13.9 0.0 copy-done.8
  13.9 0.0 copy-done.9
  14.0 0.0 copy-done.10
  14.0 0.0 copy-done.11
  14.0 5.9 %local.1 = (f32[16,8,16,128]{3,2,1,0:T(8,128)S(1)}, f32[16,48,128]{2,1,0:T(8,128)S(1)}, f32[4,20,128]{2,1,0:T(8,128)S(1)}) custom-call(s32[2]{0:T(128)S(1)} %pad_add_fusion.idx, f32[4,8,64,128]{3,2,1,0:T(8,128)S(1)} %copy-done.1, f32[3,4,8,64]{3,2,1,0:T(8,128)S(1)} %copy-done.11, f32[64,512]{1,0:T(8,128)S(1)} %copy-done.3, f32[4,32,128]{2,1,0:T(8,128)S(1)} %copy-done.2, ...), custom_call_target="tpu_custom_call" | custom-call | tf_op jit(solution)/shard_map/local/pallas_call | solution.py:175
  19.9 0.6 collective-permute-done.refs_0_
  20.5 0.0 collective-permute-done.1.refs_1_
  20.5 0.0 copy-done
  20.5 0.0 copy-done.4
  20.5 0.0 copy-done.5
  20.5 0.0 copy-done.12
  20.5 2.6 %moments.1 = (f32[408,128]{1,0:T(8,128)S(1)}, f32[4,8,16,128]{3,2,1,0:T(8,128)S(1)}, f32[4,8,16,128]{3,2,1,0:T(8,128)S(1)}) custom-call(s32[2]{0:T(128)S(1)} %pad_add_fusion.idx, f32[544,128]{1,0:T(8,128)S(1)} %collective-permute-done.refs_0_, f32[544,128]{1,0:T(8,128)S(1)} %collective-permute-done.1.refs_1_, f32[16,48,128]{2,1,0:T(8,128)S(1)} %get-tuple-element.35.refs_2_, ...), custom_call_target="tpu_custom_call" | custom-call | tf_op jit(solution)/shard_map/moments/pallas_call | solution.py:175
  23.1 8.8 %all-gather = f32[1632,128]{1,0:T(8,128)S(1)} all-gather(f32[408,128]{1,0:T(8,128)S(1)} %get-tuple-element.36), channel_id=2, replica_groups=mesh['vel'=4,'space'=64] {'vel'}, dimensions={0}, use_global_device_ids=true | all-gather | bytes 1044480 | tf_op jit(solution)/shard_map/all_gather | solution.py:853
  31.9 0.6 residual.1
  32.4 12.2 %all_to_all.20 = f32[8,30,128]{2,1,0:T(8,128)S(1)} all-to-all(f32[8,30,128]{2,1,0:T(8,128)S(1)} %residual.1), channel_id=1, replica_groups={{0,1,2,3,4,5,6,7},{8,9,10,11,12,13,14,15},{16,17,18,19,20,21,22,23},{24..., dimensions={0} | all-to-all | bytes 245760 | tf_op jit(solution)/shard_map/all_to_all | solution.py:857
  44.7 0.0 copy-start.6
  44.7 0.6 pack.1
  45.3 0.1 collective-permute-start.2
  45.4 6.0 %collective-permute-start.3 = (f32[125,128]{1,0:T(8,128)S(1)}, f32[125,128]{1,0:T(8,128)S(1)}, u32[]{:S(2)}, u32[]{:S(2)}) collective-permute-start(f32[125,128]{1,0:T(8,128)S(1)} %get-tuple-element.40.refs_3_), channel_id=1, source_target_pairs={{0,56},{1,57},{2,58},{3,59},{4,60},{5,61},{6,62},{7,63},{8,0},{9,1... | collective-permute-start | bytes 192008 | tf_op jit(solution)/shard_map/ppermute | solution.py:842
  51.4 0.0 copy-done.6
  51.4 2.0 %feq.1 = (f32[16,8,16,128]{3,2,1,0:T(8,128)S(1)}, f32[80,128]{1,0:T(8,128)S(1)}) custom-call(s32[2]{0:T(128)S(1)} %pad_add_fusion.idx, f32[4,408,128]{2,1,0:T(8,128)S(1)} %bitcast.5, f32[16,8,16,128]{3,2,1,0:T(8,128)S(1)} %get-tuple-element.41.refs_1_, f32[4,8,16,128]{3,2,1,0:T(8,128)S(1)} %get-tuple-element.42.refs_2_, ...), custom_call_target="tpu_custom_call" | custom-call | tf_op jit(solution)/shard_map/feq/pallas_call | solution.py:175
  53.4 0.2 collective-permute-done.2.refs_0_
  53.6 0.0 collective-permute-done.3.refs_2_
  53.6 0.6 window.1
  54.2 9.3 %all-gather.1 = f32[1600,128]{1,0:T(8,128)S(1)} all-gather(f32[400,128]{1,0:T(8,128)S(1)} %window.1), channel_id=3, replica_groups=mesh['vel'=4,'space'=64] {'vel'}, dimensions={0}, use_global_device_ids=true | all-gather | bytes 1024000 | tf_op jit(solution)/shard_map/all_gather | solution.py:866
  63.4 3.9 %pass1.1 = (f32[80,24,128]{2,1,0:T(8,128)S(1)}, f32[80,24,128]{2,1,0:T(8,128)S(1)}, f32[64,24,128]{2,1,0:T(8,128)S(1)}, f32[64,24,128]{2,1,0:T(8,128)S(1)}, f32[...) custom-call(s32[2]{0:T(128)S(1)} %pad_add_fusion.idx, f32[4,400,128]{2,1,0:T(8,128)S(1)} %bitcast.6, f32[424,128]{1,0:T(8,128)S(1)} %copy-done), custom_call_target="tpu_custom_call" | custom-call | tf_op jit(solution)/shard_map/pass1/pallas_call | solution.py:175
  67.4 13.8 %all_to_all.21.refs_0_ = f32[8,1,128]{2,1,0:T(1,128)S(1)} all-to-all(f32[8,1,128]{2,1,0:T(1,128)S(1)} %get-tuple-element.45), channel_id=1, replica_groups={{0,8,16,24,32,40,48,56},{1,9,17,25,33,41,49,57},{2,10,18,26,34,42,50,58..., dimensions={0} | all-to-all | bytes 8192 | tf_op jit(solution)/shard_map/all_to_all | solution.py:869
  81.2 4.3 %pass2.1 = (f32[80,24,128]{2,1,0:T(8,128)S(1)}, f32[80,24,128]{2,1,0:T(8,128)S(1)}, f32[64,24,128]{2,1,0:T(8,128)S(1)}, f32[64,24,128]{2,1,0:T(8,128)S(1)}, f32[...) custom-call(s32[2]{0:T(128)S(1)} %pad_add_fusion.idx, ...), custom_call_target="tpu_custom_call" | custom-call | tf_op jit(solution)/shard_map/pass2/pallas_call | solution.py:175
  85.6 10.0 %all_to_all.22.refs_0_ = f32[8,1,128]{2,1,0:T(1,128)S(1)} all-to-all(f32[8,1,128]{2,1,0:T(1,128)S(1)} %get-tuple-element.51), channel_id=1, replica_groups={{0,8,16,24,32,40,48,56},{1,9,17,25,33,41,49,57},{2,10,18,26,34,42,50,58..., dimensions={0} | all-to-all | bytes 8192 | tf_op jit(solution)/shard_map/all_to_all | solution.py:869
  95.6 3.8 %pass3.1 = (f32[80,8,128]{2,1,0:T(8,128)S(1)}, f32[80,8,128]{2,1,0:T(8,128)S(1)}, f32[64,8,128]{2,1,0:T(8,128)S(1)}, f32[80,8,128]{2,1,0:T(8,128)S(1)}, f32[8,1,128]{2,1,0:T(1,128)S(1)}) custom-call(s32[2]{0:T(128)S(1)} %pad_add_fusion.idx, f32[8,1,128]{2,1,0:T(1,128)S(1)} %all_to_all.22.refs_0_, f32[80,24,128]{2,1,0:T(8,128)S(1)} %get-tuple-element.52.refs_1_, ...), custom_call_target="tpu_custom_call" | custom-call | tf_op jit(solution)/shard_map/pass3/pallas_call | solution.py:175
  99.4 10.0 %all_to_all.23.refs_0_ = f32[8,1,128]{2,1,0:T(1,128)S(1)} all-to-all(f32[8,1,128]{2,1,0:T(1,128)S(1)} %get-tuple-element.58), channel_id=1, replica_groups={{0,8,16,24,32,40,48,56},{1,9,17,25,33,41,49,57},{2,10,18,26,34,42,50,58..., dimensions={0} | all-to-all | bytes 8192 | tf_op jit(solution)/shard_map/all_to_all | solution.py:869
  109.4 0.0 copy-done.7
  109.4 2.5 %last.1 = (f32[4,8,64,128]{3,2,1,0:T(8,128)}, f32[5,4,8,64]{3,2,1,0:T(8,128)}) custom-call(s32[2]{0:T(128)S(1)} %pad_add_fusion.idx, f32[8,1,128]{2,1,0:T(1,128)S(1)} %all_to_all.23.refs_0_, f32[80,8,128]{2,1,0:T(8,128)S(1)} %get-tuple-element.59.refs_1_, f32[80,8,128]{2,1,0:T(8,128)S(1)} %get-tuple-element.60.refs_2_, ...), custom_call_target="tpu_custom_call" | custom-call | tf_op jit(solution)/shard_map/last/pallas_call | solution.py:175
  (5 shorter events, 0.0 us)
Async XLA Ops:
  0.7 1.2 %copy-start.1 = (f32[4,8,64,128]{3,2,1,0:T(8,128)S(1)}, f32[4,8,64,128]{3,2,1,0:T(8,128)}, u32[]{:S(2)}) copy-start(f32[4,8,64,128]{3,2,1,0:T(8,128)} %refs_0_.3) | copy-start | bytes 3145732
  1.9 12.0 %copy-start.2 = (f32[4,32,128]{2,1,0:T(8,128)S(1)}, f32[4,32,128]{2,1,0:T(8,128)}, u32[]{:S(2)}) copy-start(f32[4,32,128]{2,1,0:T(8,128)} %constant.44.clone.refs_3_.refs_5_) | copy-start | bytes 196612
  1.9 12.0 %copy-start.3 = (f32[64,512]{1,0:T(8,128)S(1)}, f32[64,512]{1,0:T(8,128)}, u32[]{:S(2)}) copy-start(f32[64,512]{1,0:T(8,128)} %constant.54.clone.refs_2_.refs_7_) | copy-start | bytes 393220
  1.9 12.0 %copy-start.8 = (f32[4,48,128]{2,1,0:T(8,128)S(1)}, f32[4,48,128]{2,1,0:T(8,128)}, u32[]{:S(2)}) copy-start(f32[4,48,128]{2,1,0:T(8,128)} %constant.47.clone.refs_4_) | copy-start | bytes 294916
  1.9 12.0 %copy-start.9 = (f32[4,48,128]{2,1,0:T(8,128)S(1)}, f32[4,48,128]{2,1,0:T(8,128)}, u32[]{:S(2)}) copy-start(f32[4,48,128]{2,1,0:T(8,128)} %constant.46.clone.refs_5_) | copy-start | bytes 294916
  2.0 12.0 %copy-start.10 = (f32[4,48,128]{2,1,0:T(8,128)S(1)}, f32[4,48,128]{2,1,0:T(8,128)}, u32[]{:S(2)}) copy-start(f32[4,48,128]{2,1,0:T(8,128)} %constant.45.clone.refs_6_) | copy-start | bytes 294916
  2.0 12.0 %copy-start.11 = (f32[3,4,8,64]{3,2,1,0:T(8,128)S(1)}, f32[3,4,8,64]{3,2,1,0:T(8,128)}, u32[]{:S(2)}) copy-start(f32[3,4,8,64]{3,2,1,0:T(8,128)} %refs_1_.2) | copy-start | bytes 73732
  3.9 16.6 %collective-permute-start = (f32[544,128]{1,0:T(8,128)S(1)}, f32[544,128]{1,0:T(8,128)S(1)}, u32[]{:S(2)}, u32[]{:S(2)}) collective-permute-start(f32[544,128]{1,0:T(8,128)S(1)} %get-tuple-element.33), channel_id=1, source_target_pairs={{0,1},{1,2},{2,3},{3,4},{4,5},{5,6},{6,7},{7,8},{8,9},{9,10},{10,1... | collective-permute-start | bytes 835592 | tf_op jit(solution)/shard_map/ppermute | solution.py:842
  5.8 14.6 %copy-start = (f32[424,128]{1,0:T(8,128)S(1)}, f32[424,128]{1,0:T(8,128)}, u32[]{:S(2)}) copy-start(f32[424,128]{1,0:T(8,128)} %constant.50.clone.refs_4_.refs_1_.refs_6_.refs_7_) | copy-start | bytes 651268
  5.9 14.6 %copy-start.4 = (f32[4,144,128]{2,1,0:T(8,128)S(1)}, f32[4,144,128]{2,1,0:T(8,128)}, u32[]{:S(2)}) copy-start(f32[4,144,128]{2,1,0:T(8,128)} %constant.52.clone.refs_6_) | copy-start | bytes 884740
  5.9 14.6 %copy-start.5 = (f32[4,64,128]{2,1,0:T(8,128)S(1)}, f32[4,64,128]{2,1,0:T(8,128)}, u32[]{:S(2)}) copy-start(f32[4,64,128]{2,1,0:T(8,128)} %constant.53.clone.refs_7_) | copy-start | bytes 393220
  5.9 14.6 %copy-start.12 = (f32[40,64]{1,0:T(8,128)S(1)}, f32[40,64]{1,0:T(8,128)}, u32[]{:S(2)}) copy-start(f32[40,64]{1,0:T(8,128)} %constant.48.clone.refs_3_) | copy-start | bytes 30724
  5.9 14.6 %collective-permute-start.1 = (f32[544,128]{1,0:T(8,128)S(1)}, f32[544,128]{1,0:T(8,128)S(1)}, u32[]{:S(2)}, u32[]{:S(2)}) collective-permute-start(f32[544,128]{1,0:T(8,128)S(1)} %get-tuple-element.34), channel_id=1, source_target_pairs={{0,63},{1,0},{2,1},{3,2},{4,3},{5,4},{6,5},{7,6},{8,7},{9,8},{10,9... | collective-permute-start | bytes 835592 | tf_op jit(solution)/shard_map/ppermute | solution.py:842
  44.7 6.7 %copy-start.6 = (f32[4,56,128]{2,1,0:T(8,128)S(1)}, f32[4,56,128]{2,1,0:T(8,128)}, u32[]{:S(2)}) copy-start(f32[4,56,128]{2,1,0:T(8,128)} %constant.49.clone.refs_6_) | copy-start | bytes 344068
  45.3 8.3 %collective-permute-start.2 = (f32[125,128]{1,0:T(8,128)S(1)}, f32[125,128]{1,0:T(8,128)S(1)}, u32[]{:S(2)}, u32[]{:S(2)}) collective-permute-start(f32[125,128]{1,0:T(8,128)S(1)} %get-tuple-element.38.refs_4_), channel_id=1, source_target_pairs={{0,8},{1,9},{2,10},{3,11},{4,12},{5,13},{6,14},{7,15},{8,16},{9,17... | collective-permute-start | bytes 192008 | tf_op jit(solution)/shard_map/ppermute | solution.py:842
  45.4 8.2 %collective-permute-start.3 = (f32[125,128]{1,0:T(8,128)S(1)}, f32[125,128]{1,0:T(8,128)S(1)}, u32[]{:S(2)}, u32[]{:S(2)}) collective-permute-start(f32[125,128]{1,0:T(8,128)S(1)} %get-tuple-element.40.refs_3_), channel_id=1, source_target_pairs={{0,56},{1,57},{2,58},{3,59},{4,60},{5,61},{6,62},{7,63},{8,0},{9,1... | collective-permute-start | bytes 192008 | tf_op jit(solution)/shard_map/ppermute | solution.py:842
  95.6 13.8 %copy-start.7 = (f32[4,48,128]{2,1,0:T(8,128)S(1)}, f32[4,48,128]{2,1,0:T(8,128)}, u32[]{:S(2)}) copy-start(f32[4,48,128]{2,1,0:T(8,128)} %constant.51.clone.refs_8_) | copy-start | bytes 294916
